TPU v7x, 32 devices: a whole 2x2x4 slice. The times are simulated.
32 devices in a mesh: grp: 2 (over x), seq: 8 (over z, y), tile: 2 (over core).
Axes of the slice: x: 2, y: 2, z: 4, core: 2. Of those that a mesh axis runs over, the one named last changes fastest.
Arguments:
- query_input: bfloat16 [4096, 4096], P(None, ('grp', 'seq', 'tile')), parts along dimension 1, may hold values from -6 to 6
- key_input: bfloat16 [4096, 4096], P(None, ('grp', 'seq', 'tile')), parts along dimension 1, may hold values from -6 to 6
- value_input: bfloat16 [4096, 4096], P(None, ('grp', 'seq', 'tile')), parts along dimension 1, may hold values from -6 to 6
- short_taps: float32 [3, 7, 4096], replicated, may hold values from -2 to 2
- long_filter: float32 [4096, 2048], P(('seq', 'tile')), may hold values from -4 to 4
- skip_gain: float32 [4096], P(('seq', 'tile')), may hold values from -4 to 4
- unembed: bfloat16 [4096, 512], replicated, may hold values from -0.25 to 0.25
- targets: int32 [4096], P(('grp', 'seq', 'tile')), parts along dimension 0, may hold values from 0 to 511
- rankings: int32 [64, 64], P(('grp', 'seq', 'tile')), parts along dimension 0, may hold values from 0 to 63, each once within a row
Outputs:
- hyena_out: bfloat16 [4096, 4096], P(None, ('grp', 'seq', 'tile')), parts along dimension 1
- list_loss: float32 [64], P(('grp', 'seq', 'tile')), parts along dimension 0
There are 2 independent parts, one for each index of `grp`. A program takes and returns all parts, laid end to end along the dimension named above; an argument that names none is the same for every part. Nothing has to cross between parts.
Inputs may be any that keep to these rules, and one draw needn't show every extreme that they name: Each row of rankings holds every number from 0 to 63 once.
All inputs are finite; a program needn't handle non-finite values.
Results may differ from a plain program's by a relative error of at most 0.0058.
Values may be sent and summed in bfloat16 or wider, within the bound.
No kernel may reach another device: no remote copies, remote signals or barrier semaphores. Data moves between devices by JAX's collectives and lax.ppermute only.
A program may use at most 128 MiB of HBM per device.

v0:
```python
import functools
import math

import jax
import jax.numpy as jnp
import numpy as np
from jax import lax
from jax.experimental import pallas as pl
from jax.experimental.pallas import tpu as pltpu
from jax.sharding import PartitionSpec as P

soft_cap = 5.0
token_axes = ("seq", "tile")
bf16 = jnp.bfloat16
f32 = jnp.float32
rim = 8
mebibyte = 1 << 20


def params(limit=48):
    return pltpu.CompilerParams(vmem_limit_bytes=limit * mebibyte)


def cost(flops, size):
    return pl.CostEstimate(flops=flops, bytes_accessed=size, transcendentals=0)


def dot(a, b, over):
    return lax.dot_general(a, b, ((over[0], over[1]), ((), ())), preferred_element_type=f32)


def passed_along(block, axis, distance):
    devices = range(lax.axis_size(axis))
    route = [(i - distance, i) for i in devices if i - distance in devices]
    return lax.ppermute(block, axis, route)


def c_mul(z, angle):
    re, im = z
    turns = angle / (math.pi / 4)
    nearest = round(turns)
    if abs(turns - nearest) < 1e-9:
        eighth = nearest % 8
        if eighth == 0:
            return (re, im)
        if eighth == 2:
            return (-im, re)
        if eighth == 4:
            return (-re, -im)
        if eighth == 6:
            return (im, -re)
        half = math.sqrt(0.5)
        if eighth == 1:
            return ((re - im) * half, (re + im) * half)
        if eighth == 3:
            return ((re + im) * -half, (re - im) * half)
        if eighth == 5:
            return ((im - re) * half, (re + im) * -half)
        return ((re + im) * half, (im - re) * half)
    c, s = math.cos(angle), math.sin(angle)
    return (re * c - im * s, re * s + im * c)


def c_add(a, b):
    return (a[0] + b[0], a[1] + b[1])


def c_sub(a, b):
    return (a[0] - b[0], a[1] - b[1])


def c_dft(z, sign):
    n = len(z)
    if n == 1:
        return list(z)
    even = c_dft(z[0::2], sign)
    odd = c_dft(z[1::2], sign)
    turned = [c_mul(o, sign * 2 * math.pi * p / n) for p, o in enumerate(odd)]
    return [c_add(e, o) for e, o in zip(even, turned)] + [c_sub(e, o) for e, o in zip(even, turned)]


def odd_dft(x):
    n = len(x)
    if n == 1:
        return [(x[0], None)]
    half = n // 2
    z = [c_mul((x[j], -x[j + half]), -math.pi * j / n) for j in range(half)]
    wide = c_dft(z, -1)
    out = []
    for m in range(half):
        if m % 2 == 0:
            out.append(wide[m // 2])
        else:
            re, im = wide[(n - 1 - m) // 2]
            out.append((re, -im))
    return out


def real_dft(x):
    n = len(x)
    if n == 1:
        return [(x[0], None)]
    half = n // 2
    even = real_dft([x[j] + x[j + half] for j in range(half)])
    odd = odd_dft([x[j] - x[j + half] for j in range(half)])
    out = [None] * (half + 1)
    out[0::2] = even if half > 1 else [even[0]]
    out[1::2] = odd
    return out


def padded_real_dft(x):
    n = len(x)
    out = [None] * (n + 1)
    out[0::2] = real_dft(x)
    out[1::2] = odd_dft(x)
    return out


def odd_dft_adjoint(y):
    half = len(y)
    if y[0][1] is None:
        return [y[0][0]]
    n = 2 * half
    wide = []
    for p in range(half):
        if 2 * p < half:
            wide.append(y[2 * p])
        else:
            re, im = y[n - 1 - 2 * p]
            wide.append((re, -im))
    z = c_dft(wide, 1)
    turned = [c_mul(value, math.pi * j / n) for j, value in enumerate(z)]
    return [u[0] for u in turned] + [-u[1] for u in turned]


def real_dft_adjoint(x):
    if len(x) == 1:
        return [x[0][0]]
    even = real_dft_adjoint(x[0::2])
    odd = odd_dft_adjoint(x[1::2])
    return [e + o for e, o in zip(even, odd)] + [e - o for e, o in zip(even, odd)]


def padded_real_dft_adjoint(x):
    even = real_dft_adjoint(x[0::2])
    odd = odd_dft_adjoint(x[1::2])
    return [e + o for e, o in zip(even, odd)]


def rim_picker(lanes):
    row = lax.broadcasted_iota(jnp.int32, (rim, lanes), 0)
    lane = lax.broadcasted_iota(jnp.int32, (rim, lanes), 1)
    return (lane == row + (lanes - rim)).astype(bf16)


def rim_kernel(k_ref, v_ref, q_ref, kv_ref, qo_ref):
    picker = rim_picker(k_ref.shape[1])

    def last(ref):
        return dot(picker, ref[...], ((1,), (1,)))

    kv_ref[...] = jnp.concatenate([last(k_ref), last(v_ref)], axis=0).astype(bf16)
    qo_ref[...] = last(q_ref).astype(bf16)


def rims(key_input, value_input, query_input):
    channels, tokens = key_input.shape
    rows = min(channels, 1024)
    block = pl.BlockSpec((rows, tokens), lambda i: (i, 0))
    return pl.pallas_call(
        rim_kernel,
        grid=(channels // rows,),
        in_specs=[block] * 3,
        out_specs=[
            pl.BlockSpec((2 * rim, rows), lambda i: (0, i)),
            pl.BlockSpec((rim, rows), lambda i: (0, i)),
        ],
        out_shape=[
            jax.ShapeDtypeStruct((2 * rim, channels), bf16),
            jax.ShapeDtypeStruct((rim, channels), bf16),
        ],
        compiler_params=params(),
        cost_estimate=cost(6 * channels * tokens * rim, 6 * channels * tokens),
        name="rims",
    )(key_input, value_input, query_input)


step_rows = 16


def short_conv(x, before, taps):
    rows, lanes = x.shape
    width = taps.shape[0]
    tail = dot(before, rim_picker(lanes), ((0,), (0,)))
    padded = jnp.concatenate([taps, jnp.zeros((8 - width, rows), f32)], axis=0)
    columns = padded.T
    lane = lax.broadcasted_iota(jnp.int32, (step_rows, lanes), 1)
    out = []
    for begin in range(0, rows, step_rows):
        part = slice(begin, begin + step_rows)
        here = x[part].astype(f32)
        there = tail[part]
        total = columns[part, 0:1] * here
        for offset in range(1, width):
            moved = pltpu.roll(jnp.where(lane < lanes - offset, here, there), offset, 1)
            total = total + columns[part, offset : offset + 1] * moved
        out.append(total)
    return out


def gated_kernel(k_ref, v_ref, before_ref, taps_k_ref, taps_v_ref, out_ref):
    before = before_ref[...].astype(f32)
    key_short = short_conv(k_ref[0], before[:rim].astype(bf16), taps_k_ref[0])
    value_short = short_conv(v_ref[0], before[rim:].astype(bf16), taps_v_ref[0])
    for at, (k, v) in enumerate(zip(key_short, value_short)):
        out_ref[0, at * step_rows : (at + 1) * step_rows] = (k * v).astype(bf16)


def gated_features(key_input, value_input, before, short_taps):
    channels, tokens = key_input.shape
    width = short_taps.shape[1]
    rows = min(channels, 256)
    count = channels // rows
    block = pl.BlockSpec((1, rows, tokens), lambda i: (i, 0, 0))
    return pl.pallas_call(
        gated_kernel,
        grid=(count,),
        in_specs=[
            block,
            block,
            pl.BlockSpec((2 * rim, rows), lambda i: (0, i)),
            pl.BlockSpec((1, width, rows), lambda i: (1, 0, i)),
            pl.BlockSpec((1, width, rows), lambda i: (2, 0, i)),
        ],
        out_specs=block,
        out_shape=jax.ShapeDtypeStruct((count, rows, tokens), bf16),
        compiler_params=params(),
        cost_estimate=cost(28 * channels * tokens, 6 * channels * tokens),
        name="gated",
    )(
        key_input.reshape(count, rows, tokens),
        value_input.reshape(count, rows, tokens),
        before,
        short_taps,
        short_taps,
    )


def halves(x):
    high = x.astype(bf16)
    return high, (x - high.astype(f32)).astype(bf16)


def put_spectrum(spectrum, high_ref, low_ref, rows, lanes):
    for at, (re, im) in enumerate(spectrum):
        high, low = halves(re)
        high_ref[at, rows, :lanes] = high
        low_ref[at, rows, :lanes] = low
        if im is None:
            high, low = jnp.zeros_like(high), jnp.zeros_like(low)
        else:
            high, low = halves(im)
        high_ref[at, rows, lanes:] = high
        low_ref[at, rows, lanes:] = low


def three_pass(ah, al, wh, wl, over):
    return dot(ah, wh, over) + (dot(al, wh, over) + dot(ah, wl, over))


def filter_kernel(taps_ref, skip_ref, base_ref, turn_ref, spec_ref, wh_ref, wl_ref, ah, al):
    channels = taps_ref.shape[0]
    lanes = base_ref.shape[1]
    blocks = taps_ref.shape[1] // lanes
    skip = jnp.broadcast_to(skip_ref[...], (8, channels)).T
    lane = lax.broadcasted_iota(jnp.int32, (step_rows, lanes), 1)
    for step in range(channels // step_rows):
        rows = slice(step * step_rows, (step + 1) * step_rows)
        x = [taps_ref[rows, j * lanes : (j + 1) * lanes] for j in range(blocks)]
        x[0] = x[0] + jnp.where(lane == 0, skip[rows, 0:1], 0.0)
        put_spectrum(padded_real_dft(x), ah, al, rows, lanes)

    base_c, base_s = base_ref[0], base_ref[1]

    @pl.loop(0, blocks + 1)
    def _(k):
        turn_c, turn_s = turn_ref[0, k].T[:, 0:1], turn_ref[1, k].T[:, 0:1]
        c = turn_c * base_c - turn_s * base_s
        s = turn_s * base_c + turn_c * base_s
        ch, cl = halves(c)
        sh, sl = halves(s)
        for ref, cc, ss in ((wh_ref, ch, sh), (wl_ref, cl, sl)):
            ref[k, :lanes, :lanes] = cc
            ref[k, :lanes, lanes:] = -ss
            ref[k, lanes:, :lanes] = ss
            ref[k, lanes:, lanes:] = cc
        scale = jnp.where((k == 0) | (k == blocks), 1.0, 2.0) / (2 * blocks * lanes)
        spec_ref[k] = three_pass(ah[k], al[k], wh_ref[k], wl_ref[k], ((1,), (0,))) * scale


def filter_spectrum(long_filter, skip_gain, lanes):
    channels, length = long_filter.shape
    blocks = length // lanes
    count = blocks + 1
    period = 2 * length
    s = np.arange(lanes)
    base = 2 * np.pi * (s[:, None] * s[None, :] % lanes) / lanes
    turn = 2 * np.pi * (np.arange(count)[:, None] * s[None, :] % period) / period
    base = np.stack([np.cos(base), np.sin(base)]).astype(np.float32)
    turn = np.stack([np.cos(turn), np.sin(turn)]).astype(np.float32)
    turn = np.broadcast_to(turn[:, :, None, :], (2, count, 8, lanes))
    whole = pl.BlockSpec(memory_space=pltpu.VMEM)
    return pl.pallas_call(
        filter_kernel,
        in_specs=[whole] * 4,
        out_specs=[whole] * 3,
        out_shape=[
            jax.ShapeDtypeStruct((count, channels, 2 * lanes), f32),
            jax.ShapeDtypeStruct((count, 2 * lanes, 2 * lanes), bf16),
            jax.ShapeDtypeStruct((count, 2 * lanes, 2 * lanes), bf16),
        ],
        scratch_shapes=[
            pltpu.VMEM((count, channels, 2 * lanes), bf16),
            pltpu.VMEM((count, channels, 2 * lanes), bf16),
        ],
        compiler_params=params(),
        cost_estimate=cost(6 * count * channels * 4 * lanes * lanes, 12 * count * channels * lanes),
        name="filter_spectrum",
    )(long_filter, skip_gain.reshape(1, channels), jnp.asarray(base), jnp.asarray(turn))


def long_kernel(x_ref, spec_ref, wh_ref, wl_ref, out_ref, ah, al, back):
    blocks, channels, lanes = x_ref.shape

    @pl.loop(0, channels // step_rows)
    def _(step):
        rows = pl.ds(pl.multiple_of(step * step_rows, step_rows), step_rows)
        x = [x_ref[j, rows].astype(f32) for j in range(blocks)]
        put_spectrum(padded_real_dft(x), ah, al, rows, lanes)

    @pl.loop(0, blocks + 1)
    def _(k):
        x = three_pass(ah[k], al[k], wh_ref[k], wl_ref[k], ((1,), (0,)))
        spec = spec_ref[k]
        xr, xi = x[:, :lanes], x[:, lanes:]
        fr, fi = spec[:, :lanes], spec[:, lanes:]
        product = jnp.concatenate([xr * fr - xi * fi, xr * fi + xi * fr], axis=1)
        high, low = halves(product)
        back[k] = three_pass(high, low, wh_ref[k], wl_ref[k], ((1,), (1,)))

    @pl.loop(0, channels // step_rows)
    def _(step):
        rows = pl.ds(pl.multiple_of(step * step_rows, step_rows), step_rows)
        spectrum = []
        for k in range(blocks + 1):
            im = None if k in (0, blocks) else back[k, rows, lanes:]
            spectrum.append((back[k, rows, :lanes], im))
        for j, y in enumerate(padded_real_dft_adjoint(spectrum)):
            out_ref[j, rows] = y.astype(bf16)


def long_convolution(arrived, spec, wh, wl):
    blocks, channels, lanes = arrived.shape
    count = blocks + 1
    whole = pl.BlockSpec(memory_space=pltpu.VMEM)
    return pl.pallas_call(
        long_kernel,
        in_specs=[whole] * 4,
        out_specs=whole,
        out_shape=jax.ShapeDtypeStruct(arrived.shape, bf16),
        scratch_shapes=[
            pltpu.VMEM((count, channels, 2 * lanes), bf16),
            pltpu.VMEM((count, channels, 2 * lanes), bf16),
            pltpu.VMEM((count, channels, 2 * lanes), f32),
        ],
        compiler_params=params(),
        cost_estimate=cost(12 * count * channels * 4 * lanes * lanes, 12 * count * channels * lanes),
        name="long_convolution",
    )(arrived, spec, wh, wl)


def query_kernel(q_ref, before_ref, taps_ref, unembed_ref, targets_ref, ranks_ref, qs_ref, picked_ref, after_ref):
    parts = short_conv(q_ref[...], before_ref[...], taps_ref[0])
    for at, part in enumerate(parts):
        qs_ref[at * step_rows : (at + 1) * step_rows] = part
    tokens = q_ref.shape[1]
    vocabulary = unembed_ref.shape[1]
    word = lax.broadcasted_iota(jnp.int32, (vocabulary, tokens), 0)
    chosen = (word == targets_ref[...]).astype(bf16)
    picked_ref[...] = dot(unembed_ref[...], chosen, ((1,), (0,))).astype(bf16)

    @pl.when(pl.program_id(0) == 0)
    def _():
        lists, size = ranks_ref.shape
        token = lax.broadcasted_iota(jnp.int32, (size, size), 0)
        rank = lax.broadcasted_iota(jnp.int32, (size, size), 1).astype(f32)
        at = [
            jnp.sum(jnp.where(token == ranks_ref[b : b + 1, :], rank, 0.0), axis=1, keepdims=True)
            for b in range(lists)
        ]
        column = jnp.concatenate(at, axis=0)
        row_of = lax.broadcasted_iota(jnp.int32, (tokens, tokens), 0)
        col_of = lax.broadcasted_iota(jnp.int32, (tokens, tokens), 1)
        row = jnp.sum(jnp.where(row_of == col_of, column, 0.0), axis=0, keepdims=True)
        same = row_of // size == col_of // size
        after_ref[...] = jnp.where(same & (row >= column), 1.0, 0.0)


def query_side(query_input, before, short_taps, unembed, targets, rankings):
    channels, tokens = query_input.shape
    width = short_taps.shape[1]
    vocabulary = unembed.shape[1]
    rows = min(channels, 256)
    block = pl.BlockSpec((rows, tokens), lambda i: (i, 0))
    return pl.pallas_call(
        query_kernel,
        grid=(channels // rows,),
        in_specs=[
            block,
            pl.BlockSpec((rim, rows), lambda i: (0, i)),
            pl.BlockSpec((1, width, rows), lambda i: (0, 0, i)),
            pl.BlockSpec((rows, vocabulary), lambda i: (i, 0)),
            pl.BlockSpec((1, tokens), lambda i: (0, 0)),
            pl.BlockSpec(rankings.shape, lambda i: (0, 0)),
        ],
        out_specs=[block, block, pl.BlockSpec((tokens, tokens), lambda i: (0, 0))],
        out_shape=[
            jax.ShapeDtypeStruct((channels, tokens), f32),
            jax.ShapeDtypeStruct((channels, tokens), bf16),
            jax.ShapeDtypeStruct((tokens, tokens), f32),
        ],
        compiler_params=params(),
        cost_estimate=cost(2 * channels * tokens * (vocabulary + 7), channels * (8 * tokens + 2 * vocabulary)),
        name="query_side",
    )(query_input, before, short_taps, unembed, targets.reshape(1, tokens), rankings)


def result_kernel(size, carried_ref, qs_ref, picked_ref, after_ref, out_ref, loss_ref, total):
    rows, tokens = carried_ref.shape
    out = (qs_ref[...] * carried_ref[...].astype(f32)).astype(bf16)
    out_ref[...] = out
    terms = out.astype(f32) * picked_ref[...].astype(f32)
    terms = jnp.sum(terms.reshape(rows // 8, 8, tokens), axis=0)

    @pl.when(pl.program_id(0) == 0)
    def _():
        total[...] = terms

    @pl.when(pl.program_id(0) > 0)
    def _():
        total[...] += terms

    @pl.when(pl.program_id(0) == pl.num_programs(0) - 1)
    def _():
        logit = jnp.sum(total[...], axis=0, keepdims=True)
        score = soft_cap * jnp.tanh(logit / soft_cap)
        mass = jnp.sum(after_ref[...] * jnp.exp(score), axis=1, keepdims=True)
        level = jnp.log(mass)
        lists = tokens // size
        lane = lax.broadcasted_iota(jnp.int32, (1, lists), 1)
        losses = jnp.zeros((1, lists), f32)
        for b in range(lists):
            part = slice(b * size, (b + 1) * size)
            own = jnp.sum(level[part]) - jnp.sum(score[:, part])
            losses = jnp.where(lane == b, own / size, losses)
        loss_ref[...] = losses


def result(carried, query_short, picked, after, lists):
    channels, tokens = carried.shape
    rows = min(channels, 1024)
    block = pl.BlockSpec((rows, tokens), lambda i: (i, 0))
    return pl.pallas_call(
        functools.partial(result_kernel, tokens // lists),
        grid=(channels // rows,),
        in_specs=[block, block, block, pl.BlockSpec((tokens, tokens), lambda i: (0, 0))],
        out_specs=[block, pl.BlockSpec((1, lists), lambda i: (0, 0))],
        out_shape=[
            jax.ShapeDtypeStruct((channels, tokens), bf16),
            jax.ShapeDtypeStruct((1, lists), f32),
        ],
        scratch_shapes=[pltpu.VMEM((8, tokens), f32)],
        compiler_params=params(),
        cost_estimate=cost(4 * channels * tokens, 10 * channels * tokens),
        name="result",
    )(carried, query_short, picked, after)


def per_device(
    query_input,
    key_input,
    value_input,
    short_taps,
    long_filter,
    skip_gain,
    unembed,
    targets,
    rankings,
):
    channels, tokens = query_input.shape
    owners = lax.axis_size(token_axes)
    local = channels // owners
    rim_kv, rim_q = rims(key_input, value_input, query_input)
    before_kv = passed_along(rim_kv, token_axes, 1)
    before_q = passed_along(rim_q, token_axes, 1)
    gated = gated_features(key_input, value_input, before_kv, short_taps)
    arrived = lax.all_to_all(gated.reshape(owners, local, tokens), token_axes, 0, 0, tiled=True)
    spec, wh, wl = filter_spectrum(long_filter, skip_gain, tokens)
    query_short, picked, after = query_side(
        query_input, before_q, short_taps, unembed, targets, rankings
    )
    carried = long_convolution(arrived, spec, wh, wl)
    returned = lax.all_to_all(carried, token_axes, 0, 0, tiled=True)
    out, losses = result(
        returned.reshape(channels, tokens), query_short, picked, after, rankings.shape[0]
    )
    return out, losses.reshape(rankings.shape[0])


def solution(mesh):
    placed = (
        P(None, ("grp", "seq", "tile")),
        P(None, ("grp", "seq", "tile")),
        P(None, ("grp", "seq", "tile")),
        P(),
        P(("seq", "tile"), None),
        P(("seq", "tile")),
        P(),
        P(("grp", "seq", "tile")),
        P(("grp", "seq", "tile"), None),
    )
    return jax.shard_map(
        per_device,
        mesh=mesh,
        in_specs=placed,
        out_specs=(P(None, ("grp", "seq", "tile")), P(("grp", "seq", "tile"))),
        check_vma=False,
    )
```

profile of v0, /device:TPU:16, one launch (start us, length us, event | category | flops | bytes accessed | tf_op | source)
XLA Modules:
  0.0 142.1 jit_solution(7778128816023209122)
XLA Ops:
  0.6 0.0 copy-start
  0.6 1.2 copy-done
  1.9 1.2 copy-done.2
  3.1 1.2 copy-done.3
  4.3 1.3 rims.1
  5.6 1.9 %collective-permute-start = (bf16[16,4096]{1,0:T(8,128)(2,1)S(1)}, bf16[16,4096]{1,0:T(8,128)(2,1)S(1)}, u32[]{:S(2)}, u32[]{:S(2)}) collective-permute-start(bf16[16,4096]{1,0:T(8,128)(2,1)S(1)} %get-tuple-element.12), channel_id=1, source_target_pairs={{0,1},{1,2},{2,3},{3,4},{4,5},{5,6},{6,7},{7,8},{8,9},{9,10},{10,1... | collective-permute-start | bytes 393224 | tf_op jit(solution)/shard_map/ppermute | solution.py:35
  7.5 5.3 %collective-permute-done.before_ref = bf16[16,4096]{1,0:T(8,128)(2,1)S(1)} collective-permute-done((bf16[16,4096]{1,0:T(8,128)(2,1)S(1)}, bf16[16,4096]{1,0:T(8,128)(2,1)S(1)}, u32[]{:S(2)}, u32[]{:S(2)}) %collective-permute-start) | collective-permute-done | bytes 131104 | tf_op jit(solution)/shard_map/ppermute | solution.py:35
  12.8 0.0 copy-done.4
  12.8 27.1 %gated.1 = bf16[16,256,128]{2,1,0:T(8,128)(2,1)} custom-call(bf16[16,256,128]{2,1,0:T(8,128)(2,1)S(1)} %bitcast.6, bf16[16,256,128]{2,1,0:T(8,128)(2,1)S(1)} %bitcast.7, bf16[16,4096]{1,0:T(8,128)(2,1)S(1)} %collective-permute-done.before_ref, f32[3,7,4096]{2,1,0:T(8,128)S(1)} %copy-done.4, f32[3,7,4096]{2,1,0:T(8,128)S(1)} %copy-done.4), custom_call_target="tpu_custom_call" | custom-call | flops 14680064 | bytes 3145728 | tf_op jit(solution)/shard_map/gated/pallas_call | solution.py:226
  39.9 5.3 %all-to-all-start = ((bf16[16,256,128]{2,1,0:T(8,128)(2,1)}), bf16[16,256,128]{2,1,0:T(8,128)(2,1)S(1)}, u32[]{:S(2)}, u32[]{:S(2)}) async-start(bf16[16,256,128]{2,1,0:T(8,128)(2,1)} %gated.1), calls=%async_computation | async-start | bytes 2097152 | tf_op jit(solution)/shard_map/all_to_all | solution.py:508
  45.2 0.0 copy-done.16
  45.2 0.0 copy-done.12
  45.3 0.0 copy-done.13
  45.3 0.0 copy-start.11
  45.3 1.6 %copy-done.11 = f32[256,2048]{1,0:T(8,128)S(1)} copy-done((f32[256,2048]{1,0:T(8,128)S(1)}, f32[256,2048]{1,0:T(8,128)}, u32[]{:S(2)}) %copy-start.11) | copy-done | bytes 2097176
  46.9 13.3 %filter_spectrum.1 = (f32[17,256,256]{2,1,0:T(8,128)}, bf16[17,256,256]{2,1,0:T(8,128)(2,1)S(1)}, bf16[17,256,256]{2,1,0:T(8,128)(2,1)}) custom-call(f32[256,2048]{1,0:T(8,128)S(1)} %copy-done.11, f32[1,256]{1,0:T(1,128)S(1)} %bitcast.10, f32[2,128,128]{2,1,0:T(8,128)S(1)} %copy-done.13, f32[2,17,8,128]{3,2,1,0:T(8,128)S(1)} %jit_solution_.3.turn_ref), custom_call_target="tpu_custom_call" | custom-call | flops 1711276032 | bytes 6684672 | tf_op jit(solution)/shard_map/filter_spectrum/pallas_call | solution.py:314
  60.2 1.4 copy-done.14
  61.6 8.8 %all-to-all-done.x_ref = bf16[16,256,128]{2,1,0:T(8,128)(2,1)S(1)} async-done(((bf16[16,256,128]{2,1,0:T(8,128)(2,1)}), bf16[16,256,128]{2,1,0:T(8,128)(2,1)S(1)}, u32[]{:S(2)}, u32[]{:S(2)}) %all-to-all-start) | async-done | bytes 1048608 | tf_op jit(solution)/shard_map/all_to_all | solution.py:508
  70.4 1.6 %copy-done.15 = bf16[17,256,256]{2,1,0:T(8,128)(2,1)S(1)} copy-done((bf16[17,256,256]{2,1,0:T(8,128)(2,1)S(1)}, bf16[17,256,256]{2,1,0:T(8,128)(2,1)}, u32[]{:S(2)}) %copy-start.15) | copy-done | bytes 2228248
  72.0 17.0 %long_convolution.1 = bf16[16,256,128]{2,1,0:T(8,128)(2,1)} custom-call(bf16[16,256,128]{2,1,0:T(8,128)(2,1)S(1)} %all-to-all-done.x_ref, f32[17,256,256]{2,1,0:T(8,128)} %get-tuple-element.13.spec_ref, bf16[17,256,256]{2,1,0:T(8,128)(2,1)S(1)} %copy-done.15, bf16[17,256,256]{2,1,0:T(8,128)(2,1)} %get-tuple-element.15.wl_ref), custom_call_target="tpu_custom_call" | custom-call | flops 3422552064 | bytes 6684672 | tf_op jit(solution)/shard_map/long_convolution/pallas_call | solution.py:367
  89.1 4.8 %all-to-all-start.1 = ((bf16[16,256,128]{2,1,0:T(8,128)(2,1)}), bf16[16,256,128]{2,1,0:T(8,128)(2,1)S(1)}, u32[]{:S(2)}, u32[]{:S(2)}) async-start(bf16[16,256,128]{2,1,0:T(8,128)(2,1)} %long_convolution.1), calls=%async_computation.1 | async-start | bytes 2097152 | tf_op jit(solution)/shard_map/all_to_all | solution.py:514
  93.8 2.0 %collective-permute-start.1 = (bf16[8,4096]{1,0:T(8,128)(2,1)S(1)}, bf16[8,4096]{1,0:T(8,128)(2,1)S(1)}, u32[]{:S(2)}, u32[]{:S(2)}) collective-permute-start(bf16[8,4096]{1,0:T(8,128)(2,1)S(1)} %get-tuple-element.16), channel_id=1, source_target_pairs={{0,1},{1,2},{2,3},{3,4},{4,5},{5,6},{6,7},{7,8},{8,9},{9,10},{10,1... | collective-permute-start | bytes 196616 | tf_op jit(solution)/shard_map/ppermute | solution.py:35
  95.9 23.8 %collective-permute-done.1.before_ref = bf16[8,4096]{1,0:T(8,128)(2,1)S(1)} collective-permute-done((bf16[8,4096]{1,0:T(8,128)(2,1)S(1)}, bf16[8,4096]{1,0:T(8,128)(2,1)S(1)}, u32[]{:S(2)}, u32[]{:S(2)}) %collective-permute-start.1) | collective-permute-done | bytes 65568 | tf_op jit(solution)/shard_map/ppermute | solution.py:35
  119.7 0.0 copy-done.9
  119.7 0.0 copy-done.10
  119.7 15.9 %query_side.1 = (f32[4096,128]{1,0:T(8,128)S(1)}, bf16[4096,128]{1,0:T(8,128)(2,1)S(1)}, f32[128,128]{1,0:T(8,128)S(1)}) custom-call(bf16[4096,128]{1,0:T(8,128)(2,1)S(1)} %copy-done.1, bf16[8,4096]{1,0:T(8,128)(2,1)S(1)} %collective-permute-done.1.before_ref, f32[3,7,4096]{2,1,0:T(8,128)S(1)} %copy-done.4, bf16[4096,512]{1,0:T(8,128)(2,1)} %unembed_ref.1, ...), custom_call_target="tpu_custom_call" | custom-call | flops 544210944 | bytes 8388608 | tf_op jit(solution)/shard_map/query_side/pallas_call | solution.py:416
  135.6 1.3 copy-done.5
  136.9 0.6 copy-done.7
  137.6 0.0 all-to-all-done.1
  137.6 1.6 %copy-done.6 = f32[4096,128]{1,0:T(8,128)S(1)} copy-done((f32[4096,128]{1,0:T(8,128)S(1)}, f32[4096,128]{1,0:T(8,128)}, u32[]{:S(2)}) %copy-start.6) | copy-done | bytes 2097176
  139.2 0.8 copy-done.8
  140.0 2.1 %result.1 = (bf16[4096,128]{1,0:T(8,128)(2,1)}, f32[1,2]{1,0:T(1,128)}) custom-call(bf16[4096,128]{1,0:T(8,128)(2,1)S(1)} %bitcast.8, f32[4096,128]{1,0:T(8,128)S(1)} %copy-done.6, bf16[4096,128]{1,0:T(8,128)(2,1)S(1)} %get-tuple-element.18.picked_ref, f32[128,128]{1,0:T(8,128)S(1)} %copy-done.8), custom_call_target="tpu_custom_call" | custom-call | flops 2097152 | bytes 5242880 | tf_op jit(solution)/shard_map/result/pallas_call | solution.py:474
  (17 shorter events, 0.0 us)
Async XLA Ops:
  0.6 1.2 copy-start
  1.9 1.2 copy-start.2
  3.1 1.2 copy-start.3
  4.3 8.5 %copy-start.4 = (f32[3,7,4096]{2,1,0:T(8,128)S(1)}, f32[3,7,4096]{2,1,0:T(8,128)}, u32[]{:S(2)}) copy-start(f32[3,7,4096]{2,1,0:T(8,128)} %taps_ref.3) | copy-start | bytes 1032196
  5.6 7.2 %collective-permute-start = (bf16[16,4096]{1,0:T(8,128)(2,1)S(1)}, bf16[16,4096]{1,0:T(8,128)(2,1)S(1)}, u32[]{:S(2)}, u32[]{:S(2)}) collective-permute-start(bf16[16,4096]{1,0:T(8,128)(2,1)S(1)} %get-tuple-element.12), channel_id=1, source_target_pairs={{0,1},{1,2},{2,3},{3,4},{4,5},{5,6},{6,7},{7,8},{8,9},{9,10},{10,1... | collective-permute-start | bytes 393224 | tf_op jit(solution)/shard_map/ppermute | solution.py:35
  12.8 32.4 %copy-start.16 = (f32[2,17,128]{2,1,0:T(8,128)S(1)}, f32[2,17,128]{2,1,0:T(8,128)}, u32[]{:S(2)}) copy-start(f32[2,17,128]{2,1,0:T(8,128)} %constant.5.clone) | copy-start | bytes 52228
  12.8 32.5 %copy-start.12 = (f32[256]{0:T(256)S(1)}, f32[256]{0:T(256)}, u32[]{:S(2)}) copy-start(f32[256]{0:T(256)} %param.16) | copy-start | bytes 3076
  12.8 32.5 %copy-start.13 = (f32[2,128,128]{2,1,0:T(8,128)S(1)}, f32[2,128,128]{2,1,0:T(8,128)}, u32[]{:S(2)}) copy-start(f32[2,128,128]{2,1,0:T(8,128)} %constant.4.clone.base_ref) | copy-start | bytes 393220
  39.9 30.5 %all-to-all-start = ((bf16[16,256,128]{2,1,0:T(8,128)(2,1)}), bf16[16,256,128]{2,1,0:T(8,128)(2,1)S(1)}, u32[]{:S(2)}, u32[]{:S(2)}) async-start(bf16[16,256,128]{2,1,0:T(8,128)(2,1)} %gated.1), calls=%async_computation | async-start | bytes 2097152 | tf_op jit(solution)/shard_map/all_to_all | solution.py:508
  45.3 1.6 %copy-start.11 = (f32[256,2048]{1,0:T(8,128)S(1)}, f32[256,2048]{1,0:T(8,128)}, u32[]{:S(2)}) copy-start(f32[256,2048]{1,0:T(8,128)} %taps_ref.2) | copy-start | bytes 6291460
  60.2 1.4 copy-start.14
  70.4 1.6 %copy-start.15 = (bf16[17,256,256]{2,1,0:T(8,128)(2,1)S(1)}, bf16[17,256,256]{2,1,0:T(8,128)(2,1)}, u32[]{:S(2)}) copy-start(bf16[17,256,256]{2,1,0:T(8,128)(2,1)} %copy-done.14) | copy-start | bytes 6684676
  72.0 47.7 %copy-start.9 = (s32[2,64]{1,0:T(2,128)S(1)}, s32[2,64]{1,0:T(2,128)}, u32[]{:S(2)}) copy-start(s32[2,64]{1,0:T(2,128)} %ranks_ref.1) | copy-start | bytes 1540
  72.0 47.7 %copy-start.10 = (s32[128]{0:T(128)S(1)}, s32[128]{0:T(128)}, u32[]{:S(2)}) copy-start(s32[128]{0:T(128)} %param.18) | copy-start | bytes 1540
  89.1 30.7 %copy-start.1 = (bf16[4096,128]{1,0:T(8,128)(2,1)S(1)}, bf16[4096,128]{1,0:T(8,128)(2,1)}, u32[]{:S(2)}) copy-start(bf16[4096,128]{1,0:T(8,128)(2,1)} %q_ref.3) | copy-start | bytes 3145732
  89.1 48.5 %all-to-all-start.1 = ((bf16[16,256,128]{2,1,0:T(8,128)(2,1)}), bf16[16,256,128]{2,1,0:T(8,128)(2,1)S(1)}, u32[]{:S(2)}, u32[]{:S(2)}) async-start(bf16[16,256,128]{2,1,0:T(8,128)(2,1)} %long_convolution.1), calls=%async_computation.1 | async-start | bytes 2097152 | tf_op jit(solution)/shard_map/all_to_all | solution.py:514
  93.8 25.9 %collective-permute-start.1 = (bf16[8,4096]{1,0:T(8,128)(2,1)S(1)}, bf16[8,4096]{1,0:T(8,128)(2,1)S(1)}, u32[]{:S(2)}, u32[]{:S(2)}) collective-permute-start(bf16[8,4096]{1,0:T(8,128)(2,1)S(1)} %get-tuple-element.16), channel_id=1, source_target_pairs={{0,1},{1,2},{2,3},{3,4},{4,5},{5,6},{6,7},{7,8},{8,9},{9,10},{10,1... | collective-permute-start | bytes 196616 | tf_op jit(solution)/shard_map/ppermute | solution.py:35
  135.6 1.3 copy-start.5
  136.9 0.6 copy-start.7
  137.6 1.6 %copy-start.6 = (f32[4096,128]{1,0:T(8,128)S(1)}, f32[4096,128]{1,0:T(8,128)}, u32[]{:S(2)}) copy-start(f32[4096,128]{1,0:T(8,128)} %copy-done.5) | copy-start | bytes 6291460
  139.2 0.8 copy-start.8
where the time goes:
time: 143 us; the launch traced here: 142 us
  Pallas kernels  76.7 us (54%)
  waiting for transfers between devices  37.9 us (27%)
  starting transfers between devices  14 us (10%)
  local copies, waits for them, and re-layouts  12.7 us (9%)
    ppermute x2, waiting for transfers between devices, passed_along(): return lax.ppermute(block, axis, route)  29.1 us
    pallas_call x1, Pallas kernels, gated_features(): pl.pallas_call(gated_kernel, grid=(count,), in_specs=[block, block, pl.Bl...  27.1 us
    pallas_call x1, Pallas kernels, long_convolution(): pl.pallas_call(long_kernel, in_specs=[whole] * 4, out_specs=whole, out_sh...  17 us
    pallas_call x1, Pallas kernels, query_side(): pl.pallas_call(query_kernel, grid=(channels // rows,), in_specs=[block, p...  15.9 us
    pallas_call x1, Pallas kernels, filter_spectrum(): pl.pallas_call(filter_kernel, in_specs=[whole] * 4, out_specs=[whole] * 3...  13.3 us
    unnamed x34, local copies, waits for them, and re-layouts  12.7 us
    all_to_all x1, waiting for transfers between devices, per_device(): lax.all_to_all(gated.reshape(owners, local, tokens), token_axes, 0, 0, ti...  8.83 us
    all_to_all x1, starting transfers between devices, per_device(): lax.all_to_all(gated.reshape(owners, local, tokens), token_axes, 0, 0, ti...  5.29 us
  transfers between devices with their start and end apart: 4, of which 3 were waited for; matrix products, arithmetic and copies ran while one was open for 0% of the time, Pallas kernels for 21%

commit v1 on v0

v1 whole, which is shorter than its diff:
```python
import functools
import math

import jax
import jax.numpy as jnp
import ml_dtypes
import numpy as np
from jax import lax
from jax.experimental import pallas as pl
from jax.experimental.pallas import tpu as pltpu
from jax.sharding import PartitionSpec as P

soft_cap = 5.0
token_axes = ("seq", "tile")
bf16 = jnp.bfloat16
f32 = jnp.float32
rim = 8
most_chunks = 1
mebibyte = 1 << 20


whole = pl.BlockSpec(memory_space=pltpu.VMEM)
outside = pl.BlockSpec(memory_space=pltpu.HBM)


def in_hbm(x):
    return pltpu.with_memory_space_constraint(x, pltpu.HBM)


def params(limit=48):
    return pltpu.CompilerParams(vmem_limit_bytes=limit * mebibyte)


def cost(flops, size):
    return pl.CostEstimate(flops=flops, bytes_accessed=size, transcendentals=0)


def dot(a, b, over):
    return lax.dot_general(a, b, ((over[0], over[1]), ((), ())), preferred_element_type=f32)


def passed_along(block, axis, distance):
    devices = range(lax.axis_size(axis))
    route = [(i - distance, i) for i in devices if i - distance in devices]
    return lax.ppermute(block, axis, route)


def c_mul(z, angle):
    re, im = z
    turns = angle / (math.pi / 4)
    nearest = round(turns)
    if abs(turns - nearest) < 1e-9:
        eighth = nearest % 8
        if eighth == 0:
            return (re, im)
        if eighth == 2:
            return (-im, re)
        if eighth == 4:
            return (-re, -im)
        if eighth == 6:
            return (im, -re)
        half = math.sqrt(0.5)
        if eighth == 1:
            return ((re - im) * half, (re + im) * half)
        if eighth == 3:
            return ((re + im) * -half, (re - im) * half)
        if eighth == 5:
            return ((im - re) * half, (re + im) * -half)
        return ((re + im) * half, (im - re) * half)
    c, s = math.cos(angle), math.sin(angle)
    return (re * c - im * s, re * s + im * c)


def c_add(a, b):
    return (a[0] + b[0], a[1] + b[1])


def c_sub(a, b):
    return (a[0] - b[0], a[1] - b[1])


def c_dft(z, sign):
    n = len(z)
    if n == 1:
        return list(z)
    even = c_dft(z[0::2], sign)
    odd = c_dft(z[1::2], sign)
    turned = [c_mul(o, sign * 2 * math.pi * p / n) for p, o in enumerate(odd)]
    return [c_add(e, o) for e, o in zip(even, turned)] + [c_sub(e, o) for e, o in zip(even, turned)]


def odd_dft(x):
    n = len(x)
    if n == 1:
        return [(x[0], None)]
    half = n // 2
    z = [c_mul((x[j], -x[j + half]), -math.pi * j / n) for j in range(half)]
    wide = c_dft(z, -1)
    out = []
    for m in range(half):
        if m % 2 == 0:
            out.append(wide[m // 2])
        else:
            re, im = wide[(n - 1 - m) // 2]
            out.append((re, -im))
    return out


def real_dft(x):
    n = len(x)
    if n == 1:
        return [(x[0], None)]
    half = n // 2
    even = real_dft([x[j] + x[j + half] for j in range(half)])
    odd = odd_dft([x[j] - x[j + half] for j in range(half)])
    out = [None] * (half + 1)
    out[0::2] = even if half > 1 else [even[0]]
    out[1::2] = odd
    return out


def padded_real_dft(x):
    n = len(x)
    out = [None] * (n + 1)
    out[0::2] = real_dft(x)
    out[1::2] = odd_dft(x)
    return out


def odd_dft_adjoint(y):
    half = len(y)
    if y[0][1] is None:
        return [y[0][0]]
    n = 2 * half
    wide = []
    for p in range(half):
        if 2 * p < half:
            wide.append(y[2 * p])
        else:
            re, im = y[n - 1 - 2 * p]
            wide.append((re, -im))
    z = c_dft(wide, 1)
    turned = [c_mul(value, math.pi * j / n) for j, value in enumerate(z)]
    return [u[0] for u in turned] + [-u[1] for u in turned]


def real_dft_adjoint(x):
    if len(x) == 1:
        return [x[0][0]]
    even = real_dft_adjoint(x[0::2])
    odd = odd_dft_adjoint(x[1::2])
    return [e + o for e, o in zip(even, odd)] + [e - o for e, o in zip(even, odd)]


def padded_real_dft_adjoint(x):
    even = real_dft_adjoint(x[0::2])
    odd = odd_dft_adjoint(x[1::2])
    return [e + o for e, o in zip(even, odd)]


tile = 128


def rim_kernel(q_ref, k_ref, v_ref, out_ref, held, sems):
    pieces = sems.shape[1]
    channels, lanes = q_ref.shape
    rows = channels // pieces
    copies = [
        [
            pltpu.make_async_copy(
                ref.at[p * rows : (p + 1) * rows], held.at[a, p * rows : (p + 1) * rows], sems.at[a, p]
            )
            for a, ref in enumerate((q_ref, k_ref, v_ref))
        ]
        for p in range(pieces)
    ]
    for group in copies:
        for copy in group:
            copy.start()
    row = lax.broadcasted_iota(jnp.int32, (rim, lanes), 0)
    lane = lax.broadcasted_iota(jnp.int32, (rim, lanes), 1)
    picker = (lane == row + (lanes - rim)).astype(bf16)
    for p, group in enumerate(copies):
        for copy in group:
            copy.wait()
        part = slice(p * rows, (p + 1) * rows)
        last = [dot(picker, held[a, part], ((1,), (1,))) for a in range(3)]
        out_ref[:, part] = jnp.concatenate(last, axis=0).astype(bf16)


def rims(query_input, key_input, value_input):
    channels, tokens = key_input.shape
    pieces = 2
    return pl.pallas_call(
        rim_kernel,
        in_specs=[outside] * 3,
        out_specs=whole,
        out_shape=jax.ShapeDtypeStruct((3 * rim, channels), bf16),
        scratch_shapes=[
            pltpu.VMEM((3, channels, tokens), bf16),
            pltpu.SemaphoreType.DMA((3, pieces)),
        ],
        compiler_params=params(6),
        cost_estimate=cost(6 * channels * tokens * rim, 6 * channels * tokens),
        name="rims",
    )(in_hbm(query_input), in_hbm(key_input), in_hbm(value_input))


def short_conv(x, before, taps_ref, which, lanes, space):
    tokens = x.shape[1]
    space[:rim] = before
    space[rim:] = x.astype(f32).T
    width = taps_ref.shape[1]
    taps = [
        jnp.broadcast_to(taps_ref[which, offset : offset + 1, lanes], (8, tile)) for offset in range(width)
    ]
    out = []
    for begin in range(0, tokens, 8):
        total = taps[0] * space[rim + begin : rim + begin + 8]
        for offset in range(1, width):
            first = rim + begin - offset
            total = total + taps[offset] * space[first : first + 8]
        out.append(total)
    return out


def aligned(start, size):
    return pl.ds(pl.multiple_of(start, size), size)


def gated_kernel(
    chunk, k_ref, v_ref, before_ref, taps_out, out_ref, held, made, key_space, value_space, taps_ref, sems, taps_sem
):
    owners, per, tokens = made.shape
    local = k_ref.shape[1]
    groups = sems.shape[1]
    size = owners // groups
    first = chunk * per
    loads, stores = [], []
    for g in range(groups):
        part = slice(g * size, (g + 1) * size)
        loads.append(
            [
                pltpu.make_async_copy(ref.at[part, first : first + per], held.at[a, part], sems.at[a, g])
                for a, ref in enumerate((k_ref, v_ref))
            ]
        )
        stores.append(pltpu.make_async_copy(made.at[part], out_ref.at[part], sems.at[2, g]))
    taps_load = pltpu.make_async_copy(taps_out, taps_ref, taps_sem)
    taps_load.start()
    for pair in loads:
        for copy in pair:
            copy.start()
    taps_load.wait()
    tiles = per // tile
    for g in range(groups):
        for copy in loads[g]:
            copy.wait()

        @pl.loop(0, size * tiles, unroll=4)
        def _(at):
            owner = g * size + at // tiles
            row = at % tiles * tile
            rows = aligned(row, tile)
            lanes = aligned(owner * local + first + row, tile)
            before = before_ref[:, lanes].astype(f32)
            key_short = short_conv(
                held[0, owner, rows], before[rim : 2 * rim], taps_ref, 1, lanes, key_space.at[at % 2]
            )
            value_short = short_conv(
                held[1, owner, rows], before[2 * rim :], taps_ref, 2, lanes, value_space.at[at % 2]
            )
            made[owner, rows] = jnp.concatenate([k * v for k, v in zip(key_short, value_short)], 0).T.astype(bf16)

        stores[g].start()
    for copy in stores:
        copy.wait()


def gated_features(chunk, chunks, key_input, value_input, before, short_taps, owners):
    channels, tokens = key_input.shape
    if chunks == 1:
        owners = channels // tile
    local = channels // owners
    per = local // chunks
    groups = math.gcd(owners, 4)
    return pl.pallas_call(
        functools.partial(gated_kernel, chunk),
        in_specs=[outside, outside, whole, outside],
        out_specs=outside,
        out_shape=jax.ShapeDtypeStruct((owners, per, tokens), bf16),
        scratch_shapes=[
            pltpu.VMEM((2, owners, per, tokens), bf16),
            pltpu.VMEM((owners, per, tokens), bf16),
            pltpu.VMEM((2, rim + tokens, tile), f32),
            pltpu.VMEM((2, rim + tokens, tile), f32),
            pltpu.VMEM(short_taps.shape, f32),
            pltpu.SemaphoreType.DMA((3, groups)),
            pltpu.SemaphoreType.DMA,
        ],
        compiler_params=params(8),
        cost_estimate=cost(28 * channels * tokens // chunks, 6 * channels * tokens // chunks),
        name="gated",
    )(
        in_hbm(key_input.reshape(owners, local, tokens)),
        in_hbm(value_input.reshape(owners, local, tokens)),
        before,
        in_hbm(short_taps),
    )


step_rows = 16


def halves(x):
    high = x.astype(bf16)
    return high, (x - high.astype(f32)).astype(bf16)


def put_spectrum(spectrum, turn_ref, high_ref, low_ref, rows, lanes):
    for at, (re, im) in enumerate(spectrum):
        if at == 0:
            im = jnp.zeros_like(re)
        else:
            c, s = turn_ref[0, at : at + 1], turn_ref[1, at : at + 1]
            if im is None:
                re, im = re * c, -(re * s)
            else:
                re, im = re * c + im * s, im * c - re * s
        for value, part in ((re, slice(0, lanes)), (im, slice(lanes, 2 * lanes))):
            high, low = halves(value)
            high_ref[at, rows, part] = high
            low_ref[at, rows, part] = low


def three_pass(ah, al, wh, wl, over):
    return dot(ah, wh, over) + (dot(al, wh, over) + dot(ah, wl, over))


def over_frequencies(count, body):
    if count <= 33:
        for k in range(count):
            body(k)
    else:
        pl.loop(0, count)(body)


def filter_kernel(taps_ref, skip_ref, table_ref, *rest):
    *spec_refs, ah, al, turn_ref = rest
    put_turns(turn_ref)
    channels = taps_ref.shape[0]
    lanes = turn_ref.shape[2]
    blocks = taps_ref.shape[1] // lanes
    skip = jnp.broadcast_to(skip_ref[...], (8, channels)).T
    lane = lax.broadcasted_iota(jnp.int32, (step_rows, lanes), 1)
    for step in range(channels // step_rows):
        rows = slice(step * step_rows, (step + 1) * step_rows)
        x = [taps_ref[rows, j * lanes : (j + 1) * lanes] for j in range(blocks)]
        x[0] = x[0] + jnp.where(lane == 0, skip[rows, 0:1], 0.0)
        put_spectrum(padded_real_dft(x), turn_ref, ah, al, rows, lanes)
    per = channels // len(spec_refs)

    def one(k):
        ends = (k == 0) | (k == blocks)
        scale = jnp.where(ends, 1.0, 2.0) / (2 * blocks * lanes)
        spec = three_pass(ah[k], al[k], table_ref[0], table_ref[1], ((1,), (0,))) * scale
        for at, ref in enumerate(spec_refs):
            ref[k] = spec[at * per : (at + 1) * per]

    over_frequencies(blocks + 1, one)


def put_turns(turn_ref):
    _, count, lanes = turn_ref.shape
    period = 2 * (count - 1) * lanes
    k = lax.broadcasted_iota(jnp.int32, (count, lanes), 0)
    s = lax.broadcasted_iota(jnp.int32, (count, lanes), 1)
    turn = (k * s).astype(f32) * (2 * math.pi / period)
    turn_ref[0] = jnp.cos(turn)
    turn_ref[1] = jnp.sin(turn)


def table(lanes):
    s = np.arange(lanes)
    base = 2 * np.pi * (s[:, None] * s[None, :] % lanes) / lanes
    c, n = np.cos(base), np.sin(base)
    full = np.block([[c, -n], [n, c]]).astype(np.float32)
    high = full.astype(ml_dtypes.bfloat16)
    low = (full - high.astype(np.float32)).astype(ml_dtypes.bfloat16)
    return jnp.asarray(np.stack([high, low]))


def filter_spectrum(long_filter, skip_gain, table, chunks):
    channels, length = long_filter.shape
    lanes = table.shape[2] // 2
    count = length // lanes + 1
    return pl.pallas_call(
        filter_kernel,
        in_specs=[whole] * 3,
        out_specs=[whole] * chunks,
        out_shape=[pltpu.HBM((count, channels // chunks, 2 * lanes), f32)] * chunks,
        scratch_shapes=[pltpu.VMEM((count, channels, 2 * lanes), bf16)] * 2
        + [pltpu.VMEM((2, count, lanes), f32)],
        compiler_params=params(24),
        cost_estimate=cost(6 * count * channels * 4 * lanes * lanes, 12 * count * channels * lanes),
        name="filter_spectrum",
    )(long_filter, skip_gain.reshape(1, channels), table)


def long_kernel(x_ref, spec_out, table_out, out_ref, ah, al, back, spec_ref, table_ref, turn_ref, sems):
    blocks, channels, lanes = x_ref.shape
    pieces = sems.shape[0] - 1
    edges = [(blocks + 1) * p // pieces for p in range(pieces + 1)]
    loads = [
        pltpu.make_async_copy(spec_out.at[low:high], spec_ref.at[low:high], sems.at[p])
        for p, (low, high) in enumerate(zip(edges, edges[1:]))
    ]
    loads.append(pltpu.make_async_copy(table_out, table_ref, sems.at[pieces]))
    for copy in reversed(loads):
        copy.start()
    put_turns(turn_ref)

    @pl.loop(0, channels // step_rows, unroll=2)
    def _(step):
        rows = pl.ds(pl.multiple_of(step * step_rows, step_rows), step_rows)
        x = [x_ref[j, rows].astype(f32) for j in range(blocks)]
        put_spectrum(padded_real_dft(x), turn_ref, ah, al, rows, lanes)

    for copy in loads:
        copy.wait()

    def one(k):
        x = three_pass(ah[k], al[k], table_ref[0], table_ref[1], ((1,), (0,)))
        spec = spec_ref[k]
        xr, xi = x[:, :lanes], x[:, lanes:]
        fr, fi = spec[:, :lanes], spec[:, lanes:]
        product = jnp.concatenate([xr * fr - xi * fi, xr * fi + xi * fr], axis=1)
        high, low = halves(product)
        back[k] = three_pass(high, low, table_ref[0], table_ref[1], ((1,), (1,)))

    over_frequencies(blocks + 1, one)

    @pl.loop(0, channels // step_rows, unroll=2)
    def _(step):
        rows = pl.ds(pl.multiple_of(step * step_rows, step_rows), step_rows)
        spectrum = [(back[0, rows, :lanes], None)]
        for k in range(1, blocks + 1):
            re, im = back[k, rows, :lanes], back[k, rows, lanes:]
            c, s = turn_ref[0, k : k + 1], turn_ref[1, k : k + 1]
            spectrum.append((re * c - im * s, None if k == blocks else re * s + im * c))
        for j, y in enumerate(padded_real_dft_adjoint(spectrum)):
            out_ref[j, rows] = y.astype(bf16)


def long_convolution(arrived, spec, table):
    blocks, channels, lanes = arrived.shape
    count = blocks + 1
    return pl.pallas_call(
        long_kernel,
        in_specs=[whole, outside, outside],
        out_specs=whole,
        out_shape=jax.ShapeDtypeStruct(arrived.shape, bf16),
        scratch_shapes=[
            pltpu.VMEM((count, channels, 2 * lanes), bf16),
            pltpu.VMEM((count, channels, 2 * lanes), bf16),
            pltpu.VMEM((count, channels, 2 * lanes), f32),
            pltpu.VMEM((count, channels, 2 * lanes), f32),
            pltpu.VMEM(table.shape, bf16),
            pltpu.VMEM((2, count, lanes), f32),
            pltpu.SemaphoreType.DMA((5,)),
        ],
        compiler_params=params(24),
        cost_estimate=cost(12 * count * channels * 4 * lanes * lanes, 12 * count * channels * lanes),
        name="long_convolution",
    )(arrived, in_hbm(spec), in_hbm(table))


def query_kernel(q_ref, before_ref, taps_ref, unembed_ref, targets_ref, ranks_ref, qs_ref, picked_ref, after_ref, space):
    rows, tokens = q_ref.shape

    @pl.loop(0, rows // tile, unroll=min(4, rows // tile))
    def _(at):
        part = aligned(at * tile, tile)
        before = before_ref[:, part].astype(f32)
        query_short = short_conv(q_ref[part], before[:rim], taps_ref, 0, part, space.at[at % 2])
        qs_ref[part] = jnp.concatenate(query_short, 0).T

    vocabulary = unembed_ref.shape[1]
    word = lax.broadcasted_iota(jnp.int32, (vocabulary, tokens), 0)
    chosen = (word == targets_ref[...]).astype(bf16)
    picked_ref[...] = dot(unembed_ref[...], chosen, ((1,), (0,))).astype(bf16)

    @pl.when(pl.program_id(0) == 0)
    def _():
        lists, size = ranks_ref.shape
        token = lax.broadcasted_iota(jnp.int32, (size, size), 0)
        rank = lax.broadcasted_iota(jnp.int32, (size, size), 1).astype(f32)
        at = [
            jnp.sum(jnp.where(token == ranks_ref[b : b + 1, :], rank, 0.0), axis=1, keepdims=True)
            for b in range(lists)
        ]
        column = jnp.concatenate(at, axis=0)
        row_of = lax.broadcasted_iota(jnp.int32, (tokens, tokens), 0)
        col_of = lax.broadcasted_iota(jnp.int32, (tokens, tokens), 1)
        row = jnp.sum(jnp.where(row_of == col_of, column, 0.0), axis=0, keepdims=True)
        same = row_of // size == col_of // size
        after_ref[...] = jnp.where(same & (row >= column), 1.0, 0.0)


def query_side(query_input, before, short_taps, unembed, targets, rankings):
    channels, tokens = query_input.shape
    width = short_taps.shape[1]
    vocabulary = unembed.shape[1]
    rows = channels // 4
    block = pl.BlockSpec((rows, tokens), lambda i: (i, 0))
    return pl.pallas_call(
        query_kernel,
        grid=(channels // rows,),
        in_specs=[
            block,
            pl.BlockSpec((3 * rim, rows), lambda i: (0, i)),
            pl.BlockSpec((1, width, rows), lambda i: (0, 0, i)),
            pl.BlockSpec((rows, vocabulary), lambda i: (i, 0)),
            pl.BlockSpec((1, tokens), lambda i: (0, 0)),
            pl.BlockSpec(rankings.shape, lambda i: (0, 0)),
        ],
        out_specs=[block, block, pl.BlockSpec((tokens, tokens), lambda i: (0, 0))],
        out_shape=[
            pltpu.HBM((channels, tokens), f32),
            pltpu.HBM((channels, tokens), bf16),
            pltpu.HBM((tokens, tokens), f32),
        ],
        scratch_shapes=[pltpu.VMEM((2, rim + tokens, tile), f32)],
        compiler_params=params(12),
        cost_estimate=cost(2 * channels * tokens * (vocabulary + 7), channels * (8 * tokens + 2 * vocabulary)),
        name="query_side",
    )(in_hbm(query_input), before, short_taps, in_hbm(unembed), targets.reshape(1, tokens), rankings)


def result_kernel(
    size, last, first, carried_ref, qs_out, picked_out, after_out, total_ref, _, out_hbm, next_ref, loss_ref,
    qs_ref, picked_ref, out_ref, after_ref, sems, after_sem,
):
    owners, per, tokens = carried_ref.shape
    groups = sems.shape[1]
    share = owners // groups
    loads, stores = [], []
    for g in range(groups):
        part = slice(g * share, (g + 1) * share)
        rows = slice(first, first + per)
        loads.append(
            [
                pltpu.make_async_copy(qs_out.at[part, rows], qs_ref.at[part], sems.at[0, g]),
                pltpu.make_async_copy(picked_out.at[part, rows], picked_ref.at[part], sems.at[1, g]),
            ]
        )
        stores.append(pltpu.make_async_copy(out_ref.at[part], out_hbm.at[part, rows], sems.at[2, g]))
    for pair in loads:
        for copy in pair:
            copy.start()
    after_load = pltpu.make_async_copy(after_out, after_ref, after_sem)
    after_load.start()
    total = total_ref[...]
    for g in range(groups):
        for copy in loads[g]:
            copy.wait()
        part = slice(g * share, (g + 1) * share)
        out = (qs_ref[part] * carried_ref[part].astype(f32)).astype(bf16)
        out_ref[part] = out
        stores[g].start()
        terms = out.astype(f32) * picked_ref[part].astype(f32)
        total = total + jnp.sum(terms.reshape(share * per // 8, 8, tokens), axis=0)
    next_ref[...] = total
    after_load.wait()
    if last:
        logit = jnp.sum(total, axis=0, keepdims=True)
        score = soft_cap * jnp.tanh(logit / soft_cap)
        mass = jnp.sum(after_ref[...] * jnp.exp(score), axis=1, keepdims=True)
        level = jnp.log(mass)
        lists = tokens // size
        lane = lax.broadcasted_iota(jnp.int32, (1, lists), 1)
        losses = jnp.zeros((1, lists), f32)
        for b in range(lists):
            part = slice(b * size, (b + 1) * size)
            own = jnp.sum(level[part]) - jnp.sum(score[:, part])
            losses = jnp.where(lane == b, own / size, losses)
        loss_ref[...] = losses
    for copy in stores:
        copy.wait()


def result(chunk, chunks, carried, query_short, picked, after, lists, total, out):
    owners, per, tokens = carried.shape
    local = per * chunks
    groups = math.gcd(owners, 8)
    start = out is None
    if start:
        total, out = jnp.zeros((8, tokens), f32), jnp.zeros((8, tokens), bf16)
    return pl.pallas_call(
        functools.partial(result_kernel, tokens // lists, chunk == chunks - 1, chunk * per),
        in_specs=[whole, outside, outside, outside, whole, outside],
        out_specs=[outside, whole, whole],
        out_shape=[
            jax.ShapeDtypeStruct((owners, local, tokens), bf16),
            jax.ShapeDtypeStruct((8, tokens), f32),
            jax.ShapeDtypeStruct((1, lists), f32),
        ],
        scratch_shapes=[
            pltpu.VMEM((owners, per, tokens), f32),
            pltpu.VMEM((owners, per, tokens), bf16),
            pltpu.VMEM((owners, per, tokens), bf16),
            pltpu.VMEM((tokens, tokens), f32),
            pltpu.SemaphoreType.DMA((3, groups)),
            pltpu.SemaphoreType.DMA,
        ],
        input_output_aliases={} if start else {5: 0},
        compiler_params=params(8),
        cost_estimate=cost(4 * owners * per * tokens, 10 * owners * per * tokens),
        name="result",
    )(
        carried,
        in_hbm(query_short.reshape(owners, local, tokens)),
        in_hbm(picked.reshape(owners, local, tokens)),
        in_hbm(after),
        total,
        out,
    )


def per_device(
    query_input,
    key_input,
    value_input,
    short_taps,
    long_filter,
    skip_gain,
    unembed,
    targets,
    rankings,
):
    channels, tokens = query_input.shape
    owners = lax.axis_size(token_axes)
    local = channels // owners
    lists = rankings.shape[0]
    chunks = most_chunks if local % (most_chunks * tile) == 0 else 1
    before = passed_along(rims(query_input, key_input, value_input), token_axes, 1)
    arrived = []
    for chunk in range(chunks):
        gated = gated_features(chunk, chunks, key_input, value_input, before, short_taps, owners)
        arrived.append(
            lax.all_to_all(gated.reshape(owners, local // chunks, tokens), token_axes, 0, 0, tiled=True)
        )
    transform = table(tokens)
    specs = filter_spectrum(long_filter, skip_gain, transform, chunks)
    query_short, picked, after = query_side(query_input, before, short_taps, unembed, targets, rankings)
    returned = []
    for chunk in range(chunks):
        carried = long_convolution(arrived[chunk], specs[chunk], transform)
        returned.append(lax.all_to_all(carried, token_axes, 0, 0, tiled=True))
    total = out = None
    for chunk in range(chunks):
        out, total, losses = result(
            chunk, chunks, returned[chunk], query_short, picked, after, lists, total, out
        )
    return out.reshape(channels, tokens), losses.reshape(lists)


def solution(mesh):
    placed = (
        P(None, ("grp", "seq", "tile")),
        P(None, ("grp", "seq", "tile")),
        P(None, ("grp", "seq", "tile")),
        P(),
        P(("seq", "tile"), None),
        P(("seq", "tile")),
        P(),
        P(("grp", "seq", "tile")),
        P(("grp", "seq", "tile"), None),
    )
    return jax.shard_map(
        per_device,
        mesh=mesh,
        in_specs=placed,
        out_specs=(P(None, ("grp", "seq", "tile")), P(("grp", "seq", "tile"))),
        check_vma=False,
    )
```

time: 143 us -> 91.2 us (0.64)
  Pallas kernels: 76.7 us -> 35.6 us
  local copies, waits for them, and re-layouts: 12.7 us -> 0.97 us
  waiting for transfers between devices: 37.9 us -> 41.5 us
  starting transfers between devices: 14 us -> 11.9 us
    pallas_call x5, Pallas kernels: 60.8 us -> 27.6 us  [the longest x1 8.77 us: long_convolution(): pl.pallas_call(long_kernel, in_specs=[whole, outside, outside], out_specs...]
    all_to_all x2, waiting for transfers between devices: 8.83 us -> 35.6 us  [the longest x1 18.3 us: per_device(): lax.all_to_all(gated.reshape(owners, local // chunks, tokens), token_axes...]
    ppermute x2 -> x1, waiting for transfers between devices: 29.1 us -> 5.96 us  [passed_along(): return lax.ppermute(block, axis, route)]
    unnamed x34 -> x12, local copies, waits for them, and re-layouts: 12.7 us -> 0.97 us
    pallas_call x1, Pallas kernels: 15.9 us -> 7.92 us  [query_side(): pl.pallas_call(query_kernel, grid=(channels // rows,), in_specs=[block, p...]
    ppermute x2 -> x1, starting transfers between devices: 3.98 us -> 1.92 us  [passed_along(): return lax.ppermute(block, axis, route)]
  transfers between devices with their start and end apart: 4 -> 3, of which waited for: 3 -> 3; matrix products, arithmetic and copies ran while one was open for 0% -> 0% of each run, Pallas kernels for 21% -> 15%
where the time goes in v1:
time: 91.2 us; the launch traced here: 90.7 us
  waiting for transfers between devices  41.5 us (46%)
  Pallas kernels  35.6 us (39%)
  starting transfers between devices  11.9 us (13%)
  local copies, waits for them, and re-layouts  0.97 us (1%)
    all_to_all x1, waiting for transfers between devices, per_device(): lax.all_to_all(gated.reshape(owners, local // chunks, tokens), token_axes...  18.3 us
    all_to_all x1, waiting for transfers between devices, per_device(): returned.append(lax.all_to_all(carried, token_axes, 0, 0, tiled=True))  17.2 us
    pallas_call x1, Pallas kernels, long_convolution(): pl.pallas_call(long_kernel, in_specs=[whole, outside, outside], out_specs...  8.77 us
    pallas_call x1, Pallas kernels, query_side(): pl.pallas_call(query_kernel, grid=(channels // rows,), in_specs=[block, p...  7.92 us
    pallas_call x1, Pallas kernels, gated_features(): pl.pallas_call(functools.partial(gated_kernel, chunk), in_specs=[outside,...  7.06 us
    ppermute x1, waiting for transfers between devices, passed_along(): return lax.ppermute(block, axis, route)  5.96 us
    pallas_call x1, Pallas kernels, filter_spectrum(): pl.pallas_call(filter_kernel, in_specs=[whole] * 3, out_specs=[whole] * c...  5.86 us
    all_to_all x1, starting transfers between devices, per_device(): lax.all_to_all(gated.reshape(owners, local // chunks, tokens), token_axes...  5.3 us
  transfers between devices with their start and end apart: 3, of which 3 were waited for; matrix products, arithmetic and copies ran while one was open for 0% of the time, Pallas kernels for 15%

profile of v1, /device:TPU:16, one launch (start us, length us, event | category | flops | bytes accessed | tf_op | source)
XLA Modules:
  0.0 90.7 jit_solution(3860385646925806129)
XLA Ops:
  0.6 0.0 copy-start
  0.6 0.0 copy-start.3
  0.6 2.6 %rims.1 = bf16[24,4096]{1,0:T(8,128)(2,1)S(1)} custom-call(bf16[4096,128]{1,0:T(8,128)(2,1)} %q_ref.3, bf16[4096,128]{1,0:T(8,128)(2,1)} %k_ref.1, bf16[4096,128]{1,0:T(8,128)(2,1)} %v_ref.1), custom_call_target="tpu_custom_call" | custom-call | flops 25165824 | bytes 3145728 | tf_op jit(solution)/shard_map/rims/pallas_call | solution.py:194
  3.3 1.9 %collective-permute-start = (bf16[24,4096]{1,0:T(8,128)(2,1)S(1)}, bf16[24,4096]{1,0:T(8,128)(2,1)S(1)}, u32[]{:S(2)}, u32[]{:S(2)}) collective-permute-start(bf16[24,4096]{1,0:T(8,128)(2,1)S(1)} %rims.1), channel_id=1, source_target_pairs={{0,1},{1,2},{2,3},{3,4},{4,5},{5,6},{6,7},{7,8},{8,9},{9,10},{10,1... | collective-permute-start | bytes 589832 | tf_op jit(solution)/shard_map/ppermute | solution.py:45
  5.2 6.0 %collective-permute-done.before_ref = bf16[24,4096]{1,0:T(8,128)(2,1)S(1)} collective-permute-done((bf16[24,4096]{1,0:T(8,128)(2,1)S(1)}, bf16[24,4096]{1,0:T(8,128)(2,1)S(1)}, u32[]{:S(2)}, u32[]{:S(2)}) %collective-permute-start) | collective-permute-done | bytes 196640 | tf_op jit(solution)/shard_map/ppermute | solution.py:45
  11.2 7.1 %gated.1 = bf16[32,128,128]{2,1,0:T(8,128)(2,1)} custom-call(bf16[32,128,128]{2,1,0:T(8,128)(2,1)} %bitcast.11, bf16[32,128,128]{2,1,0:T(8,128)(2,1)} %bitcast.12, bf16[24,4096]{1,0:T(8,128)(2,1)S(1)} %collective-permute-done.before_ref, f32[3,7,4096]{2,1,0:T(8,128)} %taps_ref.3), custom_call_target="tpu_custom_call" | custom-call | flops 14680064 | bytes 3145728 | tf_op jit(solution)/shard_map/gated/pallas_call | solution.py:287
  18.2 5.3 %all-to-all-start = ((bf16[16,256,128]{2,1,0:T(8,128)(2,1)}), bf16[16,256,128]{2,1,0:T(8,128)(2,1)S(1)}, u32[]{:S(2)}, u32[]{:S(2)}) async-start(bf16[16,256,128]{2,1,0:T(8,128)(2,1)} %bitcast.2), calls=%async_computation | async-start | bytes 2097152 | tf_op jit(solution)/shard_map/all_to_all | solution.py:651
  23.5 0.0 copy-done
  23.5 0.0 copy-done.3
  23.5 0.0 copy-start.2
  23.6 0.9 %copy-done.2 = bf16[2,256,256]{2,1,0:T(8,128)(2,1)S(1)} copy-done((bf16[2,256,256]{2,1,0:T(8,128)(2,1)S(1)}, bf16[2,256,256]{2,1,0:T(8,128)(2,1)}, u32[]{:S(2)}) %copy-start.2) | copy-done | bytes 262168
  24.5 5.9 %filter_spectrum.1.spec_out = f32[17,256,256]{2,1,0:T(8,128)} custom-call(f32[256,2048]{1,0:T(8,128)S(1)} %copy-done, f32[1,256]{1,0:T(1,128)S(1)} %bitcast.9, bf16[2,256,256]{2,1,0:T(8,128)(2,1)S(1)} %copy-done.2), custom_call_target="tpu_custom_call" | custom-call | flops 1711276032 | bytes 6684672 | tf_op jit(solution)/shard_map/filter_spectrum/pallas_call | solution.py:397
  30.4 0.0 copy-start.1
  30.4 0.0 copy-start.4
  30.4 0.0 copy-start.5
  30.4 18.3 %all-to-all-done.x_ref = bf16[16,256,128]{2,1,0:T(8,128)(2,1)S(1)} async-done(((bf16[16,256,128]{2,1,0:T(8,128)(2,1)}), bf16[16,256,128]{2,1,0:T(8,128)(2,1)S(1)}, u32[]{:S(2)}, u32[]{:S(2)}) %all-to-all-start) | async-done | bytes 1048608 | tf_op jit(solution)/shard_map/all_to_all | solution.py:651
  48.7 8.8 %long_convolution.1 = bf16[16,256,128]{2,1,0:T(8,128)(2,1)} custom-call(bf16[16,256,128]{2,1,0:T(8,128)(2,1)S(1)} %all-to-all-done.x_ref, f32[17,256,256]{2,1,0:T(8,128)} %filter_spectrum.1.spec_out, bf16[2,256,256]{2,1,0:T(8,128)(2,1)} %constant.6.clone.table_ref.table_out), custom_call_target="tpu_custom_call" | custom-call | flops 3422552064 | bytes 6684672 | tf_op jit(solution)/shard_map/long_convolution/pallas_call | solution.py:458
  57.5 4.6 %all-to-all-start.1 = ((bf16[16,256,128]{2,1,0:T(8,128)(2,1)}), bf16[16,256,128]{2,1,0:T(8,128)(2,1)S(1)}, u32[]{:S(2)}, u32[]{:S(2)}) async-start(bf16[16,256,128]{2,1,0:T(8,128)(2,1)} %long_convolution.1), calls=%async_computation.1 | async-start | bytes 2097152 | tf_op jit(solution)/shard_map/all_to_all | solution.py:659
  62.1 0.0 copy-done.1
  62.1 0.0 copy-done.4
  62.1 0.0 copy-done.5
  62.1 7.9 %query_side.1 = (f32[4096,128]{1,0:T(8,128)}, bf16[4096,128]{1,0:T(8,128)(2,1)}, f32[128,128]{1,0:T(8,128)}) custom-call(bf16[4096,128]{1,0:T(8,128)(2,1)} %q_ref.3, bf16[24,4096]{1,0:T(8,128)(2,1)S(1)} %collective-permute-done.before_ref, f32[3,7,4096]{2,1,0:T(8,128)S(1)} %copy-done.1, bf16[4096,512]{1,0:T(8,128)(2,1)} %unembed_ref.1, ...), custom_call_target="tpu_custom_call" | custom-call | flops 544210944 | bytes 8388608 | tf_op jit(solution)/shard_map/query_side/pallas_call | solution.py:516
  70.1 17.2 %all-to-all-done.1.carried_ref = bf16[16,256,128]{2,1,0:T(8,128)(2,1)S(1)} async-done(((bf16[16,256,128]{2,1,0:T(8,128)(2,1)}), bf16[16,256,128]{2,1,0:T(8,128)(2,1)S(1)}, u32[]{:S(2)}, u32[]{:S(2)}) %all-to-all-start.1) | async-done | bytes 1048608 | tf_op jit(solution)/shard_map/all_to_all | solution.py:659
  87.3 3.3 %result.1 = (bf16[16,256,128]{2,1,0:T(8,128)(2,1)}, f32[8,128]{1,0:T(8,128)}, f32[1,2]{1,0:T(1,128)}) custom-call(bf16[16,256,128]{2,1,0:T(8,128)(2,1)S(1)} %all-to-all-done.1.carried_ref, f32[16,256,128]{2,1,0:T(8,128)} %bitcast.13, bf16[16,256,128]{2,1,0:T(8,128)(2,1)} %bitcast.14, f32[128,128]{1,0:T(8,128)} %get-tuple-element.9.after_out, ...), custom_call_target="tpu_custom_call" | custom-call | flops 2097152 | bytes 5242880 | tf_op jit(solution)/shard_map/result/pallas_call | solution.py:599
  (2 shorter events, 0.0 us)
Async XLA Ops:
  0.6 22.9 %copy-start = (f32[256,2048]{1,0:T(8,128)S(1)}, f32[256,2048]{1,0:T(8,128)}, u32[]{:S(2)}) copy-start(f32[256,2048]{1,0:T(8,128)} %taps_ref.2) | copy-start | bytes 6291460
  0.6 22.9 %copy-start.3 = (f32[256]{0:T(256)S(1)}, f32[256]{0:T(256)}, u32[]{:S(2)}) copy-start(f32[256]{0:T(256)} %param.15) | copy-start | bytes 3076
  3.3 7.9 %collective-permute-start = (bf16[24,4096]{1,0:T(8,128)(2,1)S(1)}, bf16[24,4096]{1,0:T(8,128)(2,1)S(1)}, u32[]{:S(2)}, u32[]{:S(2)}) collective-permute-start(bf16[24,4096]{1,0:T(8,128)(2,1)S(1)} %rims.1), channel_id=1, source_target_pairs={{0,1},{1,2},{2,3},{3,4},{4,5},{5,6},{6,7},{7,8},{8,9},{9,10},{10,1... | collective-permute-start | bytes 589832 | tf_op jit(solution)/shard_map/ppermute | solution.py:45
  18.2 30.5 %all-to-all-start = ((bf16[16,256,128]{2,1,0:T(8,128)(2,1)}), bf16[16,256,128]{2,1,0:T(8,128)(2,1)S(1)}, u32[]{:S(2)}, u32[]{:S(2)}) async-start(bf16[16,256,128]{2,1,0:T(8,128)(2,1)} %bitcast.2), calls=%async_computation | async-start | bytes 2097152 | tf_op jit(solution)/shard_map/all_to_all | solution.py:651
  23.5 1.0 %copy-start.2 = (bf16[2,256,256]{2,1,0:T(8,128)(2,1)S(1)}, bf16[2,256,256]{2,1,0:T(8,128)(2,1)}, u32[]{:S(2)}) copy-start(bf16[2,256,256]{2,1,0:T(8,128)(2,1)} %constant.6.clone.table_ref.table_out) | copy-start | bytes 786436
  30.4 31.8 %copy-start.1 = (f32[3,7,4096]{2,1,0:T(8,128)S(1)}, f32[3,7,4096]{2,1,0:T(8,128)}, u32[]{:S(2)}) copy-start(f32[3,7,4096]{2,1,0:T(8,128)} %taps_ref.3) | copy-start | bytes 1032196
  30.4 31.8 %copy-start.4 = (s32[2,64]{1,0:T(2,128)S(1)}, s32[2,64]{1,0:T(2,128)}, u32[]{:S(2)}) copy-start(s32[2,64]{1,0:T(2,128)} %ranks_ref.1) | copy-start | bytes 1540
  30.4 31.8 %copy-start.5 = (s32[128]{0:T(128)S(1)}, s32[128]{0:T(128)}, u32[]{:S(2)}) copy-start(s32[128]{0:T(128)} %param.17) | copy-start | bytes 1540
  57.5 29.8 %all-to-all-start.1 = ((bf16[16,256,128]{2,1,0:T(8,128)(2,1)}), bf16[16,256,128]{2,1,0:T(8,128)(2,1)S(1)}, u32[]{:S(2)}, u32[]{:S(2)}) async-start(bf16[16,256,128]{2,1,0:T(8,128)(2,1)} %long_convolution.1), calls=%async_computation.1 | async-start | bytes 2097152 | tf_op jit(solution)/shard_map/all_to_all | solution.py:659

commit v2 on v1

--- a/solution.py
+++ b/solution.py
@@ -161,18 +161,15 @@
 tile = 128
 
 
-def rim_kernel(q_ref, k_ref, v_ref, out_ref, held, sems):
+def rim_kernel(q_ref, k_ref, v_ref, out_ref, held_k, held_v, held_q, sems):
     pieces = sems.shape[1]
     channels, lanes = q_ref.shape
     rows = channels // pieces
+    pairs = ((q_ref, held_q), (k_ref, held_k), (v_ref, held_v))
+    parts = [slice(p * rows, (p + 1) * rows) for p in range(pieces)]
     copies = [
-        [
-            pltpu.make_async_copy(
-                ref.at[p * rows : (p + 1) * rows], held.at[a, p * rows : (p + 1) * rows], sems.at[a, p]
-            )
-            for a, ref in enumerate((q_ref, k_ref, v_ref))
-        ]
-        for p in range(pieces)
+        [pltpu.make_async_copy(ref.at[part], held.at[part], sems.at[a, p]) for a, (ref, held) in enumerate(pairs)]
+        for p, part in enumerate(parts)
     ]
     for group in copies:
         for copy in group:
@@ -180,11 +177,10 @@
     row = lax.broadcasted_iota(jnp.int32, (rim, lanes), 0)
     lane = lax.broadcasted_iota(jnp.int32, (rim, lanes), 1)
     picker = (lane == row + (lanes - rim)).astype(bf16)
-    for p, group in enumerate(copies):
+    for part, group in zip(parts, copies):
         for copy in group:
             copy.wait()
-        part = slice(p * rows, (p + 1) * rows)
-        last = [dot(picker, held[a, part], ((1,), (1,))) for a in range(3)]
+        last = [dot(picker, held[part], ((1,), (1,))) for _, held in pairs]
         out_ref[:, part] = jnp.concatenate(last, axis=0).astype(bf16)
 
 
@@ -194,10 +190,11 @@
     return pl.pallas_call(
         rim_kernel,
         in_specs=[outside] * 3,
-        out_specs=whole,
-        out_shape=jax.ShapeDtypeStruct((3 * rim, channels), bf16),
+        out_specs=[whole] * 3,
+        out_shape=[jax.ShapeDtypeStruct((3 * rim, channels), bf16)]
+        + [pltpu.VMEM((channels, tokens), bf16)] * 2,
         scratch_shapes=[
-            pltpu.VMEM((3, channels, tokens), bf16),
+            pltpu.VMEM((channels, tokens), bf16),
             pltpu.SemaphoreType.DMA((3, pieces)),
         ],
         compiler_params=params(6),
@@ -228,53 +225,39 @@
     return pl.ds(pl.multiple_of(start, size), size)
 
 
-def gated_kernel(
-    chunk, k_ref, v_ref, before_ref, taps_out, out_ref, held, made, key_space, value_space, taps_ref, sems, taps_sem
-):
+def gated_kernel(chunk, k_ref, v_ref, before_ref, taps_out, out_ref, made, key_space, value_space, taps_ref, sems, taps_sem):
     owners, per, tokens = made.shape
     local = k_ref.shape[1]
-    groups = sems.shape[1]
+    (groups,) = sems.shape
     size = owners // groups
     first = chunk * per
-    loads, stores = [], []
-    for g in range(groups):
-        part = slice(g * size, (g + 1) * size)
-        loads.append(
-            [
-                pltpu.make_async_copy(ref.at[part, first : first + per], held.at[a, part], sems.at[a, g])
-                for a, ref in enumerate((k_ref, v_ref))
-            ]
-        )
-        stores.append(pltpu.make_async_copy(made.at[part], out_ref.at[part], sems.at[2, g]))
     taps_load = pltpu.make_async_copy(taps_out, taps_ref, taps_sem)
     taps_load.start()
-    for pair in loads:
-        for copy in pair:
-            copy.start()
+    parts = [slice(g * size, (g + 1) * size) for g in range(groups)]
+    stores = [pltpu.make_async_copy(made.at[part], out_ref.at[part], sems.at[g]) for g, part in enumerate(parts)]
     taps_load.wait()
     tiles = per // tile
     for g in range(groups):
-        for copy in loads[g]:
-            copy.wait()
-
-        @pl.loop(0, size * tiles, unroll=4)
+
+        @pl.loop(0, size * tiles, unroll=gated_unroll)
         def _(at):
             owner = g * size + at // tiles
             row = at % tiles * tile
-            rows = aligned(row, tile)
+            rows = aligned(first + row, tile)
             lanes = aligned(owner * local + first + row, tile)
             before = before_ref[:, lanes].astype(f32)
-            key_short = short_conv(
-                held[0, owner, rows], before[rim : 2 * rim], taps_ref, 1, lanes, key_space.at[at % 2]
+            key_short = short_conv(k_ref[owner, rows], before[rim : 2 * rim], taps_ref, 1, lanes, key_space)
+            value_short = short_conv(v_ref[owner, rows], before[2 * rim :], taps_ref, 2, lanes, value_space)
+            made[owner, aligned(row, tile)] = (
+                jnp.concatenate([k * v for k, v in zip(key_short, value_short)], 0).T.astype(bf16)
             )
-            value_short = short_conv(
-                held[1, owner, rows], before[2 * rim :], taps_ref, 2, lanes, value_space.at[at % 2]
-            )
-            made[owner, rows] = jnp.concatenate([k * v for k, v in zip(key_short, value_short)], 0).T.astype(bf16)
 
         stores[g].start()
     for copy in stores:
         copy.wait()
+
+
+gated_unroll = 4
 
 
 def gated_features(chunk, chunks, key_input, value_input, before, short_taps, owners):
@@ -283,33 +266,33 @@
         owners = channels // tile
     local = channels // owners
     per = local // chunks
-    groups = math.gcd(owners, 4)
+    groups = math.gcd(owners, 8)
     return pl.pallas_call(
         functools.partial(gated_kernel, chunk),
-        in_specs=[outside, outside, whole, outside],
+        in_specs=[whole, whole, whole, outside],
         out_specs=outside,
         out_shape=jax.ShapeDtypeStruct((owners, per, tokens), bf16),
         scratch_shapes=[
-            pltpu.VMEM((2, owners, per, tokens), bf16),
             pltpu.VMEM((owners, per, tokens), bf16),
-            pltpu.VMEM((2, rim + tokens, tile), f32),
-            pltpu.VMEM((2, rim + tokens, tile), f32),
+            pltpu.VMEM((rim + tokens, tile), f32),
+            pltpu.VMEM((rim + tokens, tile), f32),
             pltpu.VMEM(short_taps.shape, f32),
-            pltpu.SemaphoreType.DMA((3, groups)),
+            pltpu.SemaphoreType.DMA((groups,)),
             pltpu.SemaphoreType.DMA,
         ],
         compiler_params=params(8),
         cost_estimate=cost(28 * channels * tokens // chunks, 6 * channels * tokens // chunks),
         name="gated",
     )(
-        in_hbm(key_input.reshape(owners, local, tokens)),
-        in_hbm(value_input.reshape(owners, local, tokens)),
+        key_input.reshape(owners, local, tokens),
+        value_input.reshape(owners, local, tokens),
         before,
         in_hbm(short_taps),
     )
 
 
 step_rows = 16
+long_parts = 2
 
 
 def halves(x):
@@ -407,49 +390,102 @@
     )(long_filter, skip_gain.reshape(1, channels), table)
 
 
-def long_kernel(x_ref, spec_out, table_out, out_ref, ah, al, back, spec_ref, table_ref, turn_ref, sems):
+def long_kernel(x_ref, spec_out, table_out, out_hbm, ah, al, back, spec_ref, table_ref, turn_ref, out_ref, sems):
     blocks, channels, lanes = x_ref.shape
-    pieces = sems.shape[0] - 1
-    edges = [(blocks + 1) * p // pieces for p in range(pieces + 1)]
+    count = blocks + 1
+    table_load = pltpu.make_async_copy(table_out, table_ref, sems.at[0])
+    split = channels % (long_parts * step_rows) == 0 and count <= 33
+    share = channels // long_parts if split else channels
+    parts = [slice(first, first + share) for first in range(0, channels, share)]
     loads = [
-        pltpu.make_async_copy(spec_out.at[low:high], spec_ref.at[low:high], sems.at[p])
-        for p, (low, high) in enumerate(zip(edges, edges[1:]))
+        pltpu.make_async_copy(spec_out.at[:, part], spec_ref.at[:, part], sems.at[1 + at])
+        for at, part in enumerate(parts)
     ]
-    loads.append(pltpu.make_async_copy(table_out, table_ref, sems.at[pieces]))
-    for copy in reversed(loads):
+    table_load.start()
+    for copy in loads[:2]:
         copy.start()
     put_turns(turn_ref)
 
-    @pl.loop(0, channels // step_rows, unroll=2)
-    def _(step):
-        rows = pl.ds(pl.multiple_of(step * step_rows, step_rows), step_rows)
+    def forward(rows):
         x = [x_ref[j, rows].astype(f32) for j in range(blocks)]
         put_spectrum(padded_real_dft(x), turn_ref, ah, al, rows, lanes)
 
-    for copy in loads:
-        copy.wait()
-
-    def one(k):
-        x = three_pass(ah[k], al[k], table_ref[0], table_ref[1], ((1,), (0,)))
-        spec = spec_ref[k]
+    def multiply(first, size, rows):
+        def take(ref):
+            part = ref[pl.ds(first, size), rows]
+            return part.reshape(size * part.shape[1], 2 * lanes)
+
+        x = three_pass(take(ah), take(al), table_ref[0], table_ref[1], ((1,), (0,)))
+        spec = take(spec_ref)
         xr, xi = x[:, :lanes], x[:, lanes:]
         fr, fi = spec[:, :lanes], spec[:, lanes:]
         product = jnp.concatenate([xr * fr - xi * fi, xr * fi + xi * fr], axis=1)
         high, low = halves(product)
-        back[k] = three_pass(high, low, table_ref[0], table_ref[1], ((1,), (1,)))
-
-    over_frequencies(blocks + 1, one)
-
-    @pl.loop(0, channels // step_rows, unroll=2)
-    def _(step):
-        rows = pl.ds(pl.multiple_of(step * step_rows, step_rows), step_rows)
+        y = three_pass(high, low, table_ref[0], table_ref[1], ((1,), (1,)))
+        back[pl.ds(first, size), rows] = y.reshape(size, -1, 2 * lanes)
+
+    def backward(rows):
         spectrum = [(back[0, rows, :lanes], None)]
-        for k in range(1, blocks + 1):
+        for k in range(1, count):
             re, im = back[k, rows, :lanes], back[k, rows, lanes:]
             c, s = turn_ref[0, k : k + 1], turn_ref[1, k : k + 1]
             spectrum.append((re * c - im * s, None if k == blocks else re * s + im * c))
         for j, y in enumerate(padded_real_dft_adjoint(spectrum)):
             out_ref[j, rows] = y.astype(bf16)
+
+    def store(part, at):
+        return pltpu.make_async_copy(out_ref.at[:, part], out_hbm.at[:, part], sems.at[1 + long_parts + at])
+
+    if split:
+        size = max(1, 256 // share)
+        steps = [[slice(r, r + step_rows) for r in range(p.start, p.stop, step_rows)] for p in parts]
+        groups = [(k, min(size, count - k)) for k in range(0, count, size)]
+
+        def together(part, others):
+            done = 0
+            for at, (k, many) in enumerate(groups):
+                multiply(k, many, part)
+                upto = len(others) * (at + 1) // len(groups)
+                for body, rows in others[done:upto]:
+                    body(rows)
+                done = upto
+
+        ahead = 2
+        for step in steps[:ahead]:
+            for rows in step:
+                forward(rows)
+        table_load.wait()
+        for at, part in enumerate(parts):
+            loads[at].wait()
+            if at + 2 < len(parts):
+                loads[at + 2].start()
+            others = [(forward, rows) for rows in (steps[at + ahead] if at + ahead < len(parts) else [])]
+            others += [(backward, rows) for rows in (steps[at - 1] if at else [])]
+            together(part, others)
+            if at:
+                store(parts[at - 1], at - 1).start()
+        for rows in steps[-1]:
+            backward(rows)
+        store(parts[-1], len(parts) - 1).start()
+        for at, part in enumerate(parts):
+            store(part, at).wait()
+    else:
+        everything = slice(0, channels)
+
+        @pl.loop(0, channels // step_rows)
+        def _(step):
+            forward(aligned(step * step_rows, step_rows))
+
+        table_load.wait()
+        loads[0].wait()
+        over_frequencies(count, lambda k: multiply(k, 1, everything))
+
+        @pl.loop(0, channels // step_rows)
+        def _(step):
+            backward(aligned(step * step_rows, step_rows))
+
+        store(everything, 0).start()
+        store(everything, 0).wait()
 
 
 def long_convolution(arrived, spec, table):
@@ -458,7 +494,7 @@
     return pl.pallas_call(
         long_kernel,
         in_specs=[whole, outside, outside],
-        out_specs=whole,
+        out_specs=outside,
         out_shape=jax.ShapeDtypeStruct(arrived.shape, bf16),
         scratch_shapes=[
             pltpu.VMEM((count, channels, 2 * lanes), bf16),
@@ -467,7 +503,8 @@
             pltpu.VMEM((count, channels, 2 * lanes), f32),
             pltpu.VMEM(table.shape, bf16),
             pltpu.VMEM((2, count, lanes), f32),
-            pltpu.SemaphoreType.DMA((5,)),
+            pltpu.VMEM(arrived.shape, bf16),
+            pltpu.SemaphoreType.DMA((1 + 2 * long_parts,)),
         ],
         compiler_params=params(24),
         cost_estimate=cost(12 * count * channels * 4 * lanes * lanes, 12 * count * channels * lanes),
@@ -643,10 +680,11 @@
     local = channels // owners
     lists = rankings.shape[0]
     chunks = most_chunks if local % (most_chunks * tile) == 0 else 1
-    before = passed_along(rims(query_input, key_input, value_input), token_axes, 1)
+    last, held_key, held_value = rims(query_input, key_input, value_input)
+    before = passed_along(last, token_axes, 1)
     arrived = []
     for chunk in range(chunks):
-        gated = gated_features(chunk, chunks, key_input, value_input, before, short_taps, owners)
+        gated = gated_features(chunk, chunks, held_key, held_value, before, short_taps, owners)
         arrived.append(
             lax.all_to_all(gated.reshape(owners, local // chunks, tokens), token_axes, 0, 0, tiled=True)
         )

time: 91.2 us -> 88.1 us (0.966)
  Pallas kernels: 35.6 us -> 32.3 us
    pallas_call x2, Pallas kernels: 9.67 us -> 6.91 us  [the longest x1 4.3 us: gated_features(): pl.pallas_call(functools.partial(gated_kernel, chunk), in_specs=[whole, w...]
  transfers between devices with their start and end apart: 3 -> 3, of which waited for: 3 -> 3; matrix products, arithmetic and copies ran while one was open for 0% -> 0% of each run, Pallas kernels for 15% -> 16%
where the time goes in v2:
time: 88.1 us; the launch traced here: 87.6 us
  waiting for transfers between devices  41.5 us (47%)
  Pallas kernels  32.3 us (37%)
  starting transfers between devices  11.9 us (14%)
  local copies, waits for them, and re-layouts  0.97 us (1%)
  between operations  0.89 us (1%)
    all_to_all x1, waiting for transfers between devices, per_device(): lax.all_to_all(gated.reshape(owners, local // chunks, tokens), token_axes...  18.3 us
    all_to_all x1, waiting for transfers between devices, per_device(): returned.append(lax.all_to_all(carried, token_axes, 0, 0, tiled=True))  17.2 us
    pallas_call x1, Pallas kernels, long_convolution(): pl.pallas_call(long_kernel, in_specs=[whole, outside, outside], out_specs...  8.25 us
    pallas_call x1, Pallas kernels, query_side(): pl.pallas_call(query_kernel, grid=(channels // rows,), in_specs=[block, p...  7.92 us
    ppermute x1, waiting for transfers between devices, passed_along(): return lax.ppermute(block, axis, route)  5.96 us
    pallas_call x1, Pallas kernels, filter_spectrum(): pl.pallas_call(filter_kernel, in_specs=[whole] * 3, out_specs=[whole] * c...  5.88 us
    all_to_all x1, starting transfers between devices, per_device(): lax.all_to_all(gated.reshape(owners, local // chunks, tokens), token_axes...  5.3 us
    all_to_all x1, starting transfers between devices, per_device(): returned.append(lax.all_to_all(carried, token_axes, 0, 0, tiled=True))  4.66 us
  transfers between devices with their start and end apart: 3, of which 3 were waited for; matrix products, arithmetic and copies ran while one was open for 0% of the time, Pallas kernels for 16%

profile of v2, /device:TPU:16, one launch (start us, length us, event | category | flops | bytes accessed | tf_op | source)
XLA Modules:
  0.0 87.6 jit_solution(3714354830671300216)
XLA Ops:
  0.6 0.0 copy-start.3
  0.6 0.0 copy-start
  0.7 2.6 %rims.1 = (bf16[24,4096]{1,0:T(8,128)(2,1)S(1)}, bf16[4096,128]{1,0:T(8,128)(2,1)S(1)}, bf16[4096,128]{1,0:T(8,128)(2,1)S(1)}) custom-call(bf16[4096,128]{1,0:T(8,128)(2,1)} %q_ref.3, bf16[4096,128]{1,0:T(8,128)(2,1)} %k_ref.1, bf16[4096,128]{1,0:T(8,128)(2,1)} %v_ref.1), custom_call_target="tpu_custom_call" | custom-call | flops 25165824 | bytes 3145728 | tf_op jit(solution)/shard_map/rims/pallas_call | solution.py:190
  3.3 1.9 %collective-permute-start = (bf16[24,4096]{1,0:T(8,128)(2,1)S(1)}, bf16[24,4096]{1,0:T(8,128)(2,1)S(1)}, u32[]{:S(2)}, u32[]{:S(2)}) collective-permute-start(bf16[24,4096]{1,0:T(8,128)(2,1)S(1)} %get-tuple-element.12), channel_id=1, source_target_pairs={{0,1},{1,2},{2,3},{3,4},{4,5},{5,6},{6,7},{7,8},{8,9},{9,10},{10,1... | collective-permute-start | bytes 589832 | tf_op jit(solution)/shard_map/ppermute | solution.py:45
  5.2 6.0 %collective-permute-done.before_ref = bf16[24,4096]{1,0:T(8,128)(2,1)S(1)} collective-permute-done((bf16[24,4096]{1,0:T(8,128)(2,1)S(1)}, bf16[24,4096]{1,0:T(8,128)(2,1)S(1)}, u32[]{:S(2)}, u32[]{:S(2)}) %collective-permute-start) | collective-permute-done | bytes 196640 | tf_op jit(solution)/shard_map/ppermute | solution.py:45
  11.2 4.3 %gated.1 = bf16[32,128,128]{2,1,0:T(8,128)(2,1)} custom-call(bf16[32,128,128]{2,1,0:T(8,128)(2,1)S(1)} %bitcast.9, bf16[32,128,128]{2,1,0:T(8,128)(2,1)S(1)} %bitcast.10, bf16[24,4096]{1,0:T(8,128)(2,1)S(1)} %collective-permute-done.before_ref, f32[3,7,4096]{2,1,0:T(8,128)} %taps_ref.3), custom_call_target="tpu_custom_call" | custom-call | flops 14680064 | bytes 3145728 | tf_op jit(solution)/shard_map/gated/pallas_call | solution.py:270
  15.5 5.3 %all-to-all-start = ((bf16[16,256,128]{2,1,0:T(8,128)(2,1)}), bf16[16,256,128]{2,1,0:T(8,128)(2,1)S(1)}, u32[]{:S(2)}, u32[]{:S(2)}) async-start(bf16[16,256,128]{2,1,0:T(8,128)(2,1)} %bitcast.2), calls=%async_computation | async-start | bytes 2097152 | tf_op jit(solution)/shard_map/all_to_all | solution.py:689
  20.8 0.0 copy-done.3
  20.8 0.0 copy-done
  20.8 0.0 copy-start.2
  20.8 0.9 %copy-done.2 = bf16[2,256,256]{2,1,0:T(8,128)(2,1)S(1)} copy-done((bf16[2,256,256]{2,1,0:T(8,128)(2,1)S(1)}, bf16[2,256,256]{2,1,0:T(8,128)(2,1)}, u32[]{:S(2)}) %copy-start.2) | copy-done | bytes 262168
  21.7 5.9 %filter_spectrum.1.spec_out = f32[17,256,256]{2,1,0:T(8,128)} custom-call(f32[256,2048]{1,0:T(8,128)S(1)} %copy-done, f32[1,256]{1,0:T(1,128)S(1)} %bitcast.11, bf16[2,256,256]{2,1,0:T(8,128)(2,1)S(1)} %copy-done.2), custom_call_target="tpu_custom_call" | custom-call | flops 1711276032 | bytes 6684672 | tf_op jit(solution)/shard_map/filter_spectrum/pallas_call | solution.py:380
  27.6 0.0 copy-start.1
  27.6 0.0 copy-start.4
  27.6 0.0 copy-start.5
  27.6 18.3 %all-to-all-done.x_ref = bf16[16,256,128]{2,1,0:T(8,128)(2,1)S(1)} async-done(((bf16[16,256,128]{2,1,0:T(8,128)(2,1)}), bf16[16,256,128]{2,1,0:T(8,128)(2,1)S(1)}, u32[]{:S(2)}, u32[]{:S(2)}) %all-to-all-start) | async-done | bytes 1048608 | tf_op jit(solution)/shard_map/all_to_all | solution.py:689
  45.9 8.3 %long_convolution.1 = bf16[16,256,128]{2,1,0:T(8,128)(2,1)} custom-call(bf16[16,256,128]{2,1,0:T(8,128)(2,1)S(1)} %all-to-all-done.x_ref, f32[17,256,256]{2,1,0:T(8,128)} %filter_spectrum.1.spec_out, bf16[2,256,256]{2,1,0:T(8,128)(2,1)} %constant.6.clone.table_ref.table_out), custom_call_target="tpu_custom_call" | custom-call | flops 3422552064 | bytes 6684672 | tf_op jit(solution)/shard_map/long_convolution/pallas_call | solution.py:494
  54.2 4.7 %all-to-all-start.1 = ((bf16[16,256,128]{2,1,0:T(8,128)(2,1)}), bf16[16,256,128]{2,1,0:T(8,128)(2,1)S(1)}, u32[]{:S(2)}, u32[]{:S(2)}) async-start(bf16[16,256,128]{2,1,0:T(8,128)(2,1)} %long_convolution.1), calls=%async_computation.1 | async-start | bytes 2097152 | tf_op jit(solution)/shard_map/all_to_all | solution.py:697
  58.9 0.0 copy-done.1
  58.9 0.0 copy-done.4
  58.9 0.0 copy-done.5
  58.9 7.9 %query_side.1 = (f32[4096,128]{1,0:T(8,128)}, bf16[4096,128]{1,0:T(8,128)(2,1)}, f32[128,128]{1,0:T(8,128)}) custom-call(bf16[4096,128]{1,0:T(8,128)(2,1)} %q_ref.3, bf16[24,4096]{1,0:T(8,128)(2,1)S(1)} %collective-permute-done.before_ref, f32[3,7,4096]{2,1,0:T(8,128)S(1)} %copy-done.1, bf16[4096,512]{1,0:T(8,128)(2,1)} %unembed_ref.1, ...), custom_call_target="tpu_custom_call" | custom-call | flops 544210944 | bytes 8388608 | tf_op jit(solution)/shard_map/query_side/pallas_call | solution.py:553
  66.8 17.2 %all-to-all-done.1.carried_ref = bf16[16,256,128]{2,1,0:T(8,128)(2,1)S(1)} async-done(((bf16[16,256,128]{2,1,0:T(8,128)(2,1)}), bf16[16,256,128]{2,1,0:T(8,128)(2,1)S(1)}, u32[]{:S(2)}, u32[]{:S(2)}) %all-to-all-start.1) | async-done | bytes 1048608 | tf_op jit(solution)/shard_map/all_to_all | solution.py:697
  84.0 3.3 %result.1 = (bf16[16,256,128]{2,1,0:T(8,128)(2,1)}, f32[8,128]{1,0:T(8,128)}, f32[1,2]{1,0:T(1,128)}) custom-call(bf16[16,256,128]{2,1,0:T(8,128)(2,1)S(1)} %all-to-all-done.1.carried_ref, f32[16,256,128]{2,1,0:T(8,128)} %bitcast.13, bf16[16,256,128]{2,1,0:T(8,128)(2,1)} %bitcast.14, f32[128,128]{1,0:T(8,128)} %get-tuple-element.15.after_out, ...), custom_call_target="tpu_custom_call" | custom-call | flops 2097152 | bytes 5242880 | tf_op jit(solution)/shard_map/result/pallas_call | solution.py:636
  (2 shorter events, 0.0 us)
Async XLA Ops:
  0.6 20.1 %copy-start.3 = (f32[256]{0:T(256)S(1)}, f32[256]{0:T(256)}, u32[]{:S(2)}) copy-start(f32[256]{0:T(256)} %param.15) | copy-start | bytes 3076
  0.6 20.1 %copy-start = (f32[256,2048]{1,0:T(8,128)S(1)}, f32[256,2048]{1,0:T(8,128)}, u32[]{:S(2)}) copy-start(f32[256,2048]{1,0:T(8,128)} %taps_ref.2) | copy-start | bytes 6291460
  3.3 7.9 %collective-permute-start = (bf16[24,4096]{1,0:T(8,128)(2,1)S(1)}, bf16[24,4096]{1,0:T(8,128)(2,1)S(1)}, u32[]{:S(2)}, u32[]{:S(2)}) collective-permute-start(bf16[24,4096]{1,0:T(8,128)(2,1)S(1)} %get-tuple-element.12), channel_id=1, source_target_pairs={{0,1},{1,2},{2,3},{3,4},{4,5},{5,6},{6,7},{7,8},{8,9},{9,10},{10,1... | collective-permute-start | bytes 589832 | tf_op jit(solution)/shard_map/ppermute | solution.py:45
  15.5 30.5 %all-to-all-start = ((bf16[16,256,128]{2,1,0:T(8,128)(2,1)}), bf16[16,256,128]{2,1,0:T(8,128)(2,1)S(1)}, u32[]{:S(2)}, u32[]{:S(2)}) async-start(bf16[16,256,128]{2,1,0:T(8,128)(2,1)} %bitcast.2), calls=%async_computation | async-start | bytes 2097152 | tf_op jit(solution)/shard_map/all_to_all | solution.py:689
  20.8 1.0 %copy-start.2 = (bf16[2,256,256]{2,1,0:T(8,128)(2,1)S(1)}, bf16[2,256,256]{2,1,0:T(8,128)(2,1)}, u32[]{:S(2)}) copy-start(bf16[2,256,256]{2,1,0:T(8,128)(2,1)} %constant.6.clone.table_ref.table_out) | copy-start | bytes 786436
  27.6 31.2 %copy-start.1 = (f32[3,7,4096]{2,1,0:T(8,128)S(1)}, f32[3,7,4096]{2,1,0:T(8,128)}, u32[]{:S(2)}) copy-start(f32[3,7,4096]{2,1,0:T(8,128)} %taps_ref.3) | copy-start | bytes 1032196
  27.6 31.2 %copy-start.4 = (s32[2,64]{1,0:T(2,128)S(1)}, s32[2,64]{1,0:T(2,128)}, u32[]{:S(2)}) copy-start(s32[2,64]{1,0:T(2,128)} %ranks_ref.1) | copy-start | bytes 1540
  27.6 31.3 %copy-start.5 = (s32[128]{0:T(128)S(1)}, s32[128]{0:T(128)}, u32[]{:S(2)}) copy-start(s32[128]{0:T(128)} %param.17) | copy-start | bytes 1540
  54.2 29.8 %all-to-all-start.1 = ((bf16[16,256,128]{2,1,0:T(8,128)(2,1)}), bf16[16,256,128]{2,1,0:T(8,128)(2,1)S(1)}, u32[]{:S(2)}, u32[]{:S(2)}) async-start(bf16[16,256,128]{2,1,0:T(8,128)(2,1)} %long_convolution.1), calls=%async_computation.1 | async-start | bytes 2097152 | tf_op jit(solution)/shard_map/all_to_all | solution.py:697

commit v3 on v2

--- a/solution.py
+++ b/solution.py
@@ -161,11 +161,17 @@
 tile = 128
 
 
-def rim_kernel(q_ref, k_ref, v_ref, out_ref, held_k, held_v, held_q, sems):
+def rim_picker(lanes):
+    row = lax.broadcasted_iota(jnp.int32, (rim, lanes), 0)
+    lane = lax.broadcasted_iota(jnp.int32, (rim, lanes), 1)
+    return (lane == row + (lanes - rim)).astype(bf16)
+
+
+def rim_kernel(k_ref, v_ref, out_ref, held_k, held_v, sems):
     pieces = sems.shape[1]
-    channels, lanes = q_ref.shape
+    channels, lanes = k_ref.shape
     rows = channels // pieces
-    pairs = ((q_ref, held_q), (k_ref, held_k), (v_ref, held_v))
+    pairs = ((k_ref, held_k), (v_ref, held_v))
     parts = [slice(p * rows, (p + 1) * rows) for p in range(pieces)]
     copies = [
         [pltpu.make_async_copy(ref.at[part], held.at[part], sems.at[a, p]) for a, (ref, held) in enumerate(pairs)]
@@ -174,9 +180,7 @@
     for group in copies:
         for copy in group:
             copy.start()
-    row = lax.broadcasted_iota(jnp.int32, (rim, lanes), 0)
-    lane = lax.broadcasted_iota(jnp.int32, (rim, lanes), 1)
-    picker = (lane == row + (lanes - rim)).astype(bf16)
+    picker = rim_picker(lanes)
     for part, group in zip(parts, copies):
         for copy in group:
             copy.wait()
@@ -184,23 +188,20 @@
         out_ref[:, part] = jnp.concatenate(last, axis=0).astype(bf16)
 
 
-def rims(query_input, key_input, value_input):
+def rims(key_input, value_input):
     channels, tokens = key_input.shape
     pieces = 2
     return pl.pallas_call(
         rim_kernel,
-        in_specs=[outside] * 3,
+        in_specs=[outside] * 2,
         out_specs=[whole] * 3,
-        out_shape=[jax.ShapeDtypeStruct((3 * rim, channels), bf16)]
+        out_shape=[jax.ShapeDtypeStruct((2 * rim, channels), bf16)]
         + [pltpu.VMEM((channels, tokens), bf16)] * 2,
-        scratch_shapes=[
-            pltpu.VMEM((channels, tokens), bf16),
-            pltpu.SemaphoreType.DMA((3, pieces)),
-        ],
+        scratch_shapes=[pltpu.SemaphoreType.DMA((2, pieces))],
         compiler_params=params(6),
-        cost_estimate=cost(6 * channels * tokens * rim, 6 * channels * tokens),
+        cost_estimate=cost(4 * channels * tokens * rim, 4 * channels * tokens),
         name="rims",
-    )(in_hbm(query_input), in_hbm(key_input), in_hbm(value_input))
+    )(in_hbm(key_input), in_hbm(value_input))
 
 
 def short_conv(x, before, taps_ref, which, lanes, space):
@@ -246,8 +247,8 @@
             rows = aligned(first + row, tile)
             lanes = aligned(owner * local + first + row, tile)
             before = before_ref[:, lanes].astype(f32)
-            key_short = short_conv(k_ref[owner, rows], before[rim : 2 * rim], taps_ref, 1, lanes, key_space)
-            value_short = short_conv(v_ref[owner, rows], before[2 * rim :], taps_ref, 2, lanes, value_space)
+            key_short = short_conv(k_ref[owner, rows], before[:rim], taps_ref, 1, lanes, key_space)
+            value_short = short_conv(v_ref[owner, rows], before[rim:], taps_ref, 2, lanes, value_space)
             made[owner, aligned(row, tile)] = (
                 jnp.concatenate([k * v for k, v in zip(key_short, value_short)], 0).T.astype(bf16)
             )
@@ -328,8 +329,10 @@
         pl.loop(0, count)(body)
 
 
-def filter_kernel(taps_ref, skip_ref, table_ref, *rest):
-    *spec_refs, ah, al, turn_ref = rest
+def filter_kernel(taps_ref, skip_ref, table_ref, q_ref, *rest):
+    *spec_refs, last_ref, ah, al, turn_ref, held, sem = rest
+    load = pltpu.make_async_copy(q_ref, held, sem)
+    load.start()
     put_turns(turn_ref)
     channels = taps_ref.shape[0]
     lanes = turn_ref.shape[2]
@@ -351,6 +354,8 @@
             ref[k] = spec[at * per : (at + 1) * per]
 
     over_frequencies(blocks + 1, one)
+    load.wait()
+    last_ref[...] = dot(rim_picker(held.shape[1]), held[...], ((1,), (1,))).astype(bf16)
 
 
 def put_turns(turn_ref):
@@ -373,21 +378,26 @@
     return jnp.asarray(np.stack([high, low]))
 
 
-def filter_spectrum(long_filter, skip_gain, table, chunks):
+def filter_spectrum(long_filter, skip_gain, table, query_input, chunks):
     channels, length = long_filter.shape
     lanes = table.shape[2] // 2
     count = length // lanes + 1
     return pl.pallas_call(
         filter_kernel,
-        in_specs=[whole] * 3,
-        out_specs=[whole] * chunks,
-        out_shape=[pltpu.HBM((count, channels // chunks, 2 * lanes), f32)] * chunks,
+        in_specs=[whole, whole, whole, outside],
+        out_specs=[whole] * (chunks + 1),
+        out_shape=[pltpu.HBM((count, channels // chunks, 2 * lanes), f32)] * chunks
+        + [pltpu.HBM((rim, query_input.shape[0]), bf16)],
         scratch_shapes=[pltpu.VMEM((count, channels, 2 * lanes), bf16)] * 2
-        + [pltpu.VMEM((2, count, lanes), f32)],
+        + [
+            pltpu.VMEM((2, count, lanes), f32),
+            pltpu.VMEM(query_input.shape, bf16),
+            pltpu.SemaphoreType.DMA,
+        ],
         compiler_params=params(24),
         cost_estimate=cost(6 * count * channels * 4 * lanes * lanes, 12 * count * channels * lanes),
         name="filter_spectrum",
-    )(long_filter, skip_gain.reshape(1, channels), table)
+    )(long_filter, skip_gain.reshape(1, channels), table, in_hbm(query_input))
 
 
 def long_kernel(x_ref, spec_out, table_out, out_hbm, ah, al, back, spec_ref, table_ref, turn_ref, out_ref, sems):
@@ -555,7 +565,7 @@
         grid=(channels // rows,),
         in_specs=[
             block,
-            pl.BlockSpec((3 * rim, rows), lambda i: (0, i)),
+            pl.BlockSpec((rim, rows), lambda i: (0, i)),
             pl.BlockSpec((1, width, rows), lambda i: (0, 0, i)),
             pl.BlockSpec((rows, vocabulary), lambda i: (i, 0)),
             pl.BlockSpec((1, tokens), lambda i: (0, 0)),
@@ -680,7 +690,7 @@
     local = channels // owners
     lists = rankings.shape[0]
     chunks = most_chunks if local % (most_chunks * tile) == 0 else 1
-    last, held_key, held_value = rims(query_input, key_input, value_input)
+    last, held_key, held_value = rims(key_input, value_input)
     before = passed_along(last, token_axes, 1)
     arrived = []
     for chunk in range(chunks):
@@ -689,8 +699,10 @@
             lax.all_to_all(gated.reshape(owners, local // chunks, tokens), token_axes, 0, 0, tiled=True)
         )
     transform = table(tokens)
-    specs = filter_spectrum(long_filter, skip_gain, transform, chunks)
-    query_short, picked, after = query_side(query_input, before, short_taps, unembed, targets, rankings)
+    *specs, last_query = filter_spectrum(long_filter, skip_gain, transform, query_input, chunks)
+    before_query = passed_along(last_query, token_axes, 1)
+    arrived, before_query = lax.optimization_barrier((arrived, before_query))
+    query_short, picked, after = query_side(query_input, before_query, short_taps, unembed, targets, rankings)
     returned = []
     for chunk in range(chunks):
         carried = long_convolution(arrived[chunk], specs[chunk], transform)

time: 88.1 us -> 87.3 us (level)
  waiting for transfers between devices: 41.5 us -> 39.2 us
  starting transfers between devices: 11.9 us -> 13.7 us
  local copies, waits for them, and re-layouts: 0.97 us -> 0.03 us
    all_to_all x1, waiting for transfers between devices: 18.3 us -> 0.01 us  [per_device(): lax.all_to_all(gated.reshape(owners, local // chunks, tokens), token_axes...]
    ppermute x1 -> x2, waiting for transfers between devices: 5.96 us -> 21.9 us  [passed_along(): return lax.ppermute(block, axis, route)]
    ppermute x1 -> x2, starting transfers between devices: 1.92 us -> 4.16 us  [passed_along(): return lax.ppermute(block, axis, route)]
    unnamed x12, local copies, waits for them, and re-layouts: 0.97 us -> 0.03 us
  transfers between devices with their start and end apart: 3 -> 4, of which waited for: 3 -> 3; matrix products, arithmetic and copies ran while one was open for 0% -> 0% of each run, Pallas kernels for 16% -> 17%
where the time goes in v3:
time: 87.3 us; the launch traced here: 86.7 us
  waiting for transfers between devices  39.2 us (45%)
  Pallas kernels  32.9 us (38%)
  starting transfers between devices  13.7 us (16%)
  between operations  0.91 us (1%)
    ppermute x2, waiting for transfers between devices, passed_along(): return lax.ppermute(block, axis, route)  21.9 us
    all_to_all x1, waiting for transfers between devices, per_device(): returned.append(lax.all_to_all(carried, token_axes, 0, 0, tiled=True))  17.2 us
    pallas_call x1, Pallas kernels, long_convolution(): pl.pallas_call(long_kernel, in_specs=[whole, outside, outside], out_specs...  8.26 us
    pallas_call x1, Pallas kernels, query_side(): pl.pallas_call(query_kernel, grid=(channels // rows,), in_specs=[block, p...  7.91 us
    pallas_call x1, Pallas kernels, filter_spectrum(): pl.pallas_call(filter_kernel, in_specs=[whole, whole, whole, outside], ou...  6.94 us
    all_to_all x1, starting transfers between devices, per_device(): lax.all_to_all(gated.reshape(owners, local // chunks, tokens), token_axes...  5.3 us
    pallas_call x1, Pallas kernels, gated_features(): pl.pallas_call(functools.partial(gated_kernel, chunk), in_specs=[whole, w...  4.3 us
    all_to_all x1, starting transfers between devices, per_device(): returned.append(lax.all_to_all(carried, token_axes, 0, 0, tiled=True))  4.23 us
  transfers between devices with their start and end apart: 4, of which 3 were waited for; matrix products, arithmetic and copies ran while one was open for 0% of the time, Pallas kernels for 17%

profile of v3, /device:TPU:16, one launch (start us, length us, event | category | flops | bytes accessed | tf_op | source)
XLA Modules:
  0.0 86.7 jit_solution(16689830302607590361)
XLA Ops:
  0.6 0.0 copy-start.5
  0.6 0.0 copy-start.3
  0.7 0.0 copy-start.4
  0.7 2.2 %rims.1 = (bf16[16,4096]{1,0:T(8,128)(2,1)S(1)}, bf16[4096,128]{1,0:T(8,128)(2,1)S(1)}, bf16[4096,128]{1,0:T(8,128)(2,1)S(1)}) custom-call(bf16[4096,128]{1,0:T(8,128)(2,1)} %k_ref.1, bf16[4096,128]{1,0:T(8,128)(2,1)} %v_ref.1), custom_call_target="tpu_custom_call" | custom-call | flops 16777216 | bytes 2097152 | tf_op jit(solution)/shard_map/rims/pallas_call | solution.py:194
  2.8 1.9 %collective-permute-start = (bf16[16,4096]{1,0:T(8,128)(2,1)S(1)}, bf16[16,4096]{1,0:T(8,128)(2,1)S(1)}, u32[]{:S(2)}, u32[]{:S(2)}) collective-permute-start(bf16[16,4096]{1,0:T(8,128)(2,1)S(1)} %get-tuple-element.16), channel_id=1, source_target_pairs={{0,1},{1,2},{2,3},{3,4},{4,5},{5,6},{6,7},{7,8},{8,9},{9,10},{10,1... | collective-permute-start | bytes 393224 | tf_op jit(solution)/shard_map/ppermute | solution.py:45
  4.8 5.3 %collective-permute-done.before_ref = bf16[16,4096]{1,0:T(8,128)(2,1)S(1)} collective-permute-done((bf16[16,4096]{1,0:T(8,128)(2,1)S(1)}, bf16[16,4096]{1,0:T(8,128)(2,1)S(1)}, u32[]{:S(2)}, u32[]{:S(2)}) %collective-permute-start) | collective-permute-done | bytes 131104 | tf_op jit(solution)/shard_map/ppermute | solution.py:45
  10.0 4.3 %gated.1 = bf16[32,128,128]{2,1,0:T(8,128)(2,1)} custom-call(bf16[32,128,128]{2,1,0:T(8,128)(2,1)S(1)} %bitcast.9, bf16[32,128,128]{2,1,0:T(8,128)(2,1)S(1)} %bitcast.10, bf16[16,4096]{1,0:T(8,128)(2,1)S(1)} %collective-permute-done.before_ref, f32[3,7,4096]{2,1,0:T(8,128)} %taps_ref.3), custom_call_target="tpu_custom_call" | custom-call | flops 14680064 | bytes 3145728 | tf_op jit(solution)/shard_map/gated/pallas_call | solution.py:271
  14.3 5.3 %all-to-all-start = ((bf16[16,256,128]{2,1,0:T(8,128)(2,1)}), bf16[16,256,128]{2,1,0:T(8,128)(2,1)S(1)}, u32[]{:S(2)}, u32[]{:S(2)}) async-start(bf16[16,256,128]{2,1,0:T(8,128)(2,1)} %bitcast.2), calls=%async_computation | async-start | bytes 2097152 | tf_op jit(solution)/shard_map/all_to_all | solution.py:699
  19.6 0.0 copy-done.5
  19.6 0.0 copy-done.3
  19.6 0.0 copy-done.4
  19.7 6.9 %filter_spectrum.1 = (f32[17,256,256]{2,1,0:T(8,128)}, bf16[8,4096]{1,0:T(8,128)(2,1)}) custom-call(f32[256,2048]{1,0:T(8,128)S(1)} %copy-done.3, f32[1,256]{1,0:T(1,128)S(1)} %bitcast.12, bf16[2,256,256]{2,1,0:T(8,128)(2,1)S(1)} %copy-done.5, bf16[4096,128]{1,0:T(8,128)(2,1)} %q_ref.3), custom_call_target="tpu_custom_call" | custom-call | flops 1711276032 | bytes 6684672 | tf_op jit(solution)/shard_map/filter_spectrum/pallas_call | solution.py:385
  26.6 2.2 %collective-permute-start.1 = (bf16[8,4096]{1,0:T(8,128)(2,1)}, bf16[8,4096]{1,0:T(8,128)(2,1)S(1)}, u32[]{:S(2)}, u32[]{:S(2)}) collective-permute-start(bf16[8,4096]{1,0:T(8,128)(2,1)} %get-tuple-element.17), channel_id=1, source_target_pairs={{0,1},{1,2},{2,3},{3,4},{4,5},{5,6},{6,7},{7,8},{8,9},{9,10},{10,1... | collective-permute-start | bytes 196616 | tf_op jit(solution)/shard_map/ppermute | solution.py:45
  28.9 16.7 %collective-permute-done.1.before_ref = bf16[8,4096]{1,0:T(8,128)(2,1)S(1)} collective-permute-done((bf16[8,4096]{1,0:T(8,128)(2,1)}, bf16[8,4096]{1,0:T(8,128)(2,1)S(1)}, u32[]{:S(2)}, u32[]{:S(2)}) %collective-permute-start.1) | collective-permute-done | bytes 65568 | tf_op jit(solution)/shard_map/ppermute | solution.py:45
  45.5 0.0 all-to-all-done.x_ref
  45.5 0.0 copy-start
  45.5 0.0 copy-start.1
  45.5 0.0 copy-start.2
  45.5 8.3 %long_convolution.1 = bf16[16,256,128]{2,1,0:T(8,128)(2,1)} custom-call(bf16[16,256,128]{2,1,0:T(8,128)(2,1)S(1)} %all-to-all-done.x_ref, f32[17,256,256]{2,1,0:T(8,128)} %get-tuple-element.19.spec_out, bf16[2,256,256]{2,1,0:T(8,128)(2,1)} %constant.6.clone.table_ref.table_out), custom_call_target="tpu_custom_call" | custom-call | flops 3422552064 | bytes 6684672 | tf_op jit(solution)/shard_map/long_convolution/pallas_call | solution.py:504
  53.8 4.2 %all-to-all-start.1 = ((bf16[16,256,128]{2,1,0:T(8,128)(2,1)}), bf16[16,256,128]{2,1,0:T(8,128)(2,1)S(1)}, u32[]{:S(2)}, u32[]{:S(2)}) async-start(bf16[16,256,128]{2,1,0:T(8,128)(2,1)} %long_convolution.1), calls=%async_computation.1 | async-start | bytes 2097152 | tf_op jit(solution)/shard_map/all_to_all | solution.py:709
  58.0 0.0 copy-done
  58.0 0.0 copy-done.1
  58.0 0.0 copy-done.2
  58.0 7.9 %query_side.1 = (f32[4096,128]{1,0:T(8,128)}, bf16[4096,128]{1,0:T(8,128)(2,1)}, f32[128,128]{1,0:T(8,128)}) custom-call(bf16[4096,128]{1,0:T(8,128)(2,1)} %q_ref.3, bf16[8,4096]{1,0:T(8,128)(2,1)S(1)} %collective-permute-done.1.before_ref, f32[3,7,4096]{2,1,0:T(8,128)S(1)} %copy-done, bf16[4096,512]{1,0:T(8,128)(2,1)} %unembed_ref.1, ...), custom_call_target="tpu_custom_call" | custom-call | flops 544210944 | bytes 8388608 | tf_op jit(solution)/shard_map/query_side/pallas_call | solution.py:563
  66.0 17.2 %all-to-all-done.1.carried_ref = bf16[16,256,128]{2,1,0:T(8,128)(2,1)S(1)} async-done(((bf16[16,256,128]{2,1,0:T(8,128)(2,1)}), bf16[16,256,128]{2,1,0:T(8,128)(2,1)S(1)}, u32[]{:S(2)}, u32[]{:S(2)}) %all-to-all-start.1) | async-done | bytes 1048608 | tf_op jit(solution)/shard_map/all_to_all | solution.py:709
  83.2 3.3 %result.1 = (bf16[16,256,128]{2,1,0:T(8,128)(2,1)}, f32[8,128]{1,0:T(8,128)}, f32[1,2]{1,0:T(1,128)}) custom-call(bf16[16,256,128]{2,1,0:T(8,128)(2,1)S(1)} %all-to-all-done.1.carried_ref, f32[16,256,128]{2,1,0:T(8,128)} %bitcast.13, bf16[16,256,128]{2,1,0:T(8,128)(2,1)} %bitcast.14, f32[128,128]{1,0:T(8,128)} %get-tuple-element.23.after_out, ...), custom_call_target="tpu_custom_call" | custom-call | flops 2097152 | bytes 5242880 | tf_op jit(solution)/shard_map/result/pallas_call | solution.py:646
  (2 shorter events, 0.0 us)
Async XLA Ops:
  0.6 19.0 %copy-start.5 = (bf16[2,256,256]{2,1,0:T(8,128)(2,1)S(1)}, bf16[2,256,256]{2,1,0:T(8,128)(2,1)}, u32[]{:S(2)}) copy-start(bf16[2,256,256]{2,1,0:T(8,128)(2,1)} %constant.6.clone.table_ref.table_out) | copy-start | bytes 786436
  0.6 19.0 %copy-start.3 = (f32[256,2048]{1,0:T(8,128)S(1)}, f32[256,2048]{1,0:T(8,128)}, u32[]{:S(2)}) copy-start(f32[256,2048]{1,0:T(8,128)} %taps_ref.2) | copy-start | bytes 6291460
  0.7 19.0 %copy-start.4 = (f32[256]{0:T(256)S(1)}, f32[256]{0:T(256)}, u32[]{:S(2)}) copy-start(f32[256]{0:T(256)} %param.15) | copy-start | bytes 3076
  2.8 7.2 %collective-permute-start = (bf16[16,4096]{1,0:T(8,128)(2,1)S(1)}, bf16[16,4096]{1,0:T(8,128)(2,1)S(1)}, u32[]{:S(2)}, u32[]{:S(2)}) collective-permute-start(bf16[16,4096]{1,0:T(8,128)(2,1)S(1)} %get-tuple-element.16), channel_id=1, source_target_pairs={{0,1},{1,2},{2,3},{3,4},{4,5},{5,6},{6,7},{7,8},{8,9},{9,10},{10,1... | collective-permute-start | bytes 393224 | tf_op jit(solution)/shard_map/ppermute | solution.py:45
  14.3 31.2 %all-to-all-start = ((bf16[16,256,128]{2,1,0:T(8,128)(2,1)}), bf16[16,256,128]{2,1,0:T(8,128)(2,1)S(1)}, u32[]{:S(2)}, u32[]{:S(2)}) async-start(bf16[16,256,128]{2,1,0:T(8,128)(2,1)} %bitcast.2), calls=%async_computation | async-start | bytes 2097152 | tf_op jit(solution)/shard_map/all_to_all | solution.py:699
  26.6 18.9 %collective-permute-start.1 = (bf16[8,4096]{1,0:T(8,128)(2,1)}, bf16[8,4096]{1,0:T(8,128)(2,1)S(1)}, u32[]{:S(2)}, u32[]{:S(2)}) collective-permute-start(bf16[8,4096]{1,0:T(8,128)(2,1)} %get-tuple-element.17), channel_id=1, source_target_pairs={{0,1},{1,2},{2,3},{3,4},{4,5},{5,6},{6,7},{7,8},{8,9},{9,10},{10,1... | collective-permute-start | bytes 196616 | tf_op jit(solution)/shard_map/ppermute | solution.py:45
  45.5 12.5 %copy-start = (f32[3,7,4096]{2,1,0:T(8,128)S(1)}, f32[3,7,4096]{2,1,0:T(8,128)}, u32[]{:S(2)}) copy-start(f32[3,7,4096]{2,1,0:T(8,128)} %taps_ref.3) | copy-start | bytes 1032196
  45.5 12.5 %copy-start.1 = (s32[2,64]{1,0:T(2,128)S(1)}, s32[2,64]{1,0:T(2,128)}, u32[]{:S(2)}) copy-start(s32[2,64]{1,0:T(2,128)} %ranks_ref.1) | copy-start | bytes 1540
  45.5 12.5 %copy-start.2 = (s32[128]{0:T(128)S(1)}, s32[128]{0:T(128)}, u32[]{:S(2)}) copy-start(s32[128]{0:T(128)} %param.17) | copy-start | bytes 1540
  53.8 29.4 %all-to-all-start.1 = ((bf16[16,256,128]{2,1,0:T(8,128)(2,1)}), bf16[16,256,128]{2,1,0:T(8,128)(2,1)S(1)}, u32[]{:S(2)}, u32[]{:S(2)}) async-start(bf16[16,256,128]{2,1,0:T(8,128)(2,1)} %long_convolution.1), calls=%async_computation.1 | async-start | bytes 2097152 | tf_op jit(solution)/shard_map/all_to_all | solution.py:709

commit v4 on v3

--- a/solution.py
+++ b/solution.py
@@ -226,70 +226,109 @@
     return pl.ds(pl.multiple_of(start, size), size)
 
 
-def gated_kernel(chunk, k_ref, v_ref, before_ref, taps_out, out_ref, made, key_space, value_space, taps_ref, sems, taps_sem):
-    owners, per, tokens = made.shape
-    local = k_ref.shape[1]
-    (groups,) = sems.shape
-    size = owners // groups
-    first = chunk * per
-    taps_load = pltpu.make_async_copy(taps_out, taps_ref, taps_sem)
-    taps_load.start()
-    parts = [slice(g * size, (g + 1) * size) for g in range(groups)]
-    stores = [pltpu.make_async_copy(made.at[part], out_ref.at[part], sems.at[g]) for g, part in enumerate(parts)]
-    taps_load.wait()
-    tiles = per // tile
-    for g in range(groups):
-
-        @pl.loop(0, size * tiles, unroll=gated_unroll)
-        def _(at):
-            owner = g * size + at // tiles
-            row = at % tiles * tile
-            rows = aligned(first + row, tile)
-            lanes = aligned(owner * local + first + row, tile)
-            before = before_ref[:, lanes].astype(f32)
-            key_short = short_conv(k_ref[owner, rows], before[:rim], taps_ref, 1, lanes, key_space)
-            value_short = short_conv(v_ref[owner, rows], before[rim:], taps_ref, 2, lanes, value_space)
-            made[owner, aligned(row, tile)] = (
-                jnp.concatenate([k * v for k, v in zip(key_short, value_short)], 0).T.astype(bf16)
-            )
-
-        stores[g].start()
-    for copy in stores:
-        copy.wait()
-
-
-gated_unroll = 4
-
-
-def gated_features(chunk, chunks, key_input, value_input, before, short_taps, owners):
+def filtered(space, taps, begin):
+    total = taps[0] * space[rim + begin : rim + begin + 8]
+    for offset in range(1, len(taps)):
+        first = rim + begin - offset
+        total = total + taps[offset] * space[first : first + 8]
+    return total
+
+
+def tap_rows(taps_ref, which, lanes):
+    return [
+        jnp.broadcast_to(taps_ref[which, offset : offset + 1, lanes], (8, tile))
+        for offset in range(taps_ref.shape[1])
+    ]
+
+
+def inner_kernel(k_ref, v_ref, taps_out, part_ref, first_ref, taps_ref, key_space, value_space, sem):
+    tiles, tokens, _ = part_ref.shape
+    load = pltpu.make_async_copy(taps_out, taps_ref, sem)
+    load.start()
+    load.wait()
+    unroll = math.gcd(tiles, 4)
+    for group in range(tiles // unroll):
+
+        @pl.loop(0, unroll, unroll=unroll)
+        def _(step):
+            at = group * unroll + step
+            lanes = aligned(at * tile, tile)
+            for a, (ref, space) in enumerate(((k_ref, key_space), (v_ref, value_space))):
+                turned = ref[lanes].astype(f32).T
+                space[rim:] = turned
+                first_ref[a, at] = turned[:rim]
+            key_taps, value_taps = tap_rows(taps_ref, 1, lanes), tap_rows(taps_ref, 2, lanes)
+            for begin in range(rim, tokens, 8):
+                k = filtered(key_space, key_taps, begin)
+                part_ref[at, begin : begin + 8] = k * filtered(value_space, value_taps, begin)
+
+
+def inner_features(key_input, value_input, short_taps):
     channels, tokens = key_input.shape
-    if chunks == 1:
-        owners = channels // tile
-    local = channels // owners
-    per = local // chunks
-    groups = math.gcd(owners, 8)
+    tiles = channels // tile
     return pl.pallas_call(
-        functools.partial(gated_kernel, chunk),
-        in_specs=[whole, whole, whole, outside],
-        out_specs=outside,
-        out_shape=jax.ShapeDtypeStruct((owners, per, tokens), bf16),
+        inner_kernel,
+        in_specs=[whole, whole, outside],
+        out_specs=[whole] * 3,
+        out_shape=[
+            pltpu.VMEM((tiles, tokens, tile), f32),
+            pltpu.VMEM((2, tiles, rim, tile), f32),
+            pltpu.VMEM(short_taps.shape, f32),
+        ],
         scratch_shapes=[
-            pltpu.VMEM((owners, per, tokens), bf16),
             pltpu.VMEM((rim + tokens, tile), f32),
             pltpu.VMEM((rim + tokens, tile), f32),
-            pltpu.VMEM(short_taps.shape, f32),
+            pltpu.SemaphoreType.DMA,
+        ],
+        compiler_params=params(8),
+        cost_estimate=cost(28 * channels * tokens, 8 * channels * tokens),
+        name="inner",
+    )(key_input, value_input, in_hbm(short_taps))
+
+
+def gated_kernel(part_ref, first_ref, taps_ref, before_ref, out_ref, made, key_space, value_space, sems):
+    tiles, tokens, _ = part_ref.shape
+    (groups,) = sems.shape
+    size = tiles // groups
+    for g in range(groups):
+
+        @pl.loop(0, size, unroll=size)
+        def _(step):
+            at = g * size + step
+            lanes = aligned(at * tile, tile)
+            before = before_ref[:, lanes].astype(f32)
+            for a, space in enumerate((key_space, value_space)):
+                space[:rim] = before[a * rim : (a + 1) * rim]
+                space[rim:] = first_ref[a, at]
+            k = filtered(key_space, tap_rows(taps_ref, 1, lanes), 0)
+            v = filtered(value_space, tap_rows(taps_ref, 2, lanes), 0)
+            made[at] = jnp.concatenate([k * v, part_ref[at, rim:]], 0).T.astype(bf16)
+
+        here = slice(g * size, (g + 1) * size)
+        pltpu.make_async_copy(made.at[here], out_ref.at[here], sems.at[g]).start()
+    for g in range(groups):
+        here = slice(g * size, (g + 1) * size)
+        pltpu.make_async_copy(made.at[here], out_ref.at[here], sems.at[g]).wait()
+
+
+def gated_features(part, first, taps, before):
+    tiles, tokens, _ = part.shape
+    groups = math.gcd(tiles, 8)
+    return pl.pallas_call(
+        gated_kernel,
+        in_specs=[whole] * 4,
+        out_specs=outside,
+        out_shape=jax.ShapeDtypeStruct((tiles, tile, tokens), bf16),
+        scratch_shapes=[
+            pltpu.VMEM((tiles, tile, tokens), bf16),
+            pltpu.VMEM((2 * rim, tile), f32),
+            pltpu.VMEM((2 * rim, tile), f32),
             pltpu.SemaphoreType.DMA((groups,)),
-            pltpu.SemaphoreType.DMA,
-        ],
-        compiler_params=params(8),
-        cost_estimate=cost(28 * channels * tokens // chunks, 6 * channels * tokens // chunks),
+        ],
+        compiler_params=params(6),
+        cost_estimate=cost(4 * tiles * tile * tokens, 6 * tiles * tile * tokens),
         name="gated",
-    )(
-        key_input.reshape(owners, local, tokens),
-        value_input.reshape(owners, local, tokens),
-        before,
-        in_hbm(short_taps),
-    )
+    )(part, first, taps, before)
 
 
 step_rows = 16
@@ -692,12 +731,11 @@
     chunks = most_chunks if local % (most_chunks * tile) == 0 else 1
     last, held_key, held_value = rims(key_input, value_input)
     before = passed_along(last, token_axes, 1)
-    arrived = []
-    for chunk in range(chunks):
-        gated = gated_features(chunk, chunks, held_key, held_value, before, short_taps, owners)
-        arrived.append(
-            lax.all_to_all(gated.reshape(owners, local // chunks, tokens), token_axes, 0, 0, tiled=True)
-        )
+    inner = inner_features(held_key, held_value, short_taps)
+    gated = gated_features(*inner, before).reshape(owners, chunks, local // chunks, tokens)
+    arrived = [
+        lax.all_to_all(gated[:, chunk], token_axes, 0, 0, tiled=True) for chunk in range(chunks)
+    ]
     transform = table(tokens)
     *specs, last_query = filter_spectrum(long_filter, skip_gain, transform, query_input, chunks)
     before_query = passed_along(last_query, token_axes, 1)

time: 87.3 us -> 84.3 us (0.966)
  waiting for transfers between devices: 39.2 us -> 35.4 us
    ppermute x2, waiting for transfers between devices: 21.9 us -> 18.2 us  [passed_along(): return lax.ppermute(block, axis, route)]
    pallas_call x1 -> x2, Pallas kernels: 4.3 us -> 4.94 us  [the longest x1 3.73 us: inner_features(): pl.pallas_call(inner_kernel, in_specs=[whole, whole, outside], out_specs=...]
  transfers between devices with their start and end apart: 4 -> 4, of which waited for: 3 -> 3; matrix products, arithmetic and copies ran while one was open for 0% -> 0% of each run, Pallas kernels for 17% -> 22%
where the time goes in v4:
time: 84.3 us; the launch traced here: 83.6 us
  waiting for transfers between devices  35.4 us (42%)
  Pallas kernels  33.4 us (40%)
  starting transfers between devices  13.8 us (16%)
  between operations  0.92 us (1%)
    ppermute x2, waiting for transfers between devices, passed_along(): return lax.ppermute(block, axis, route)  18.2 us
    all_to_all x1, waiting for transfers between devices, per_device(): returned.append(lax.all_to_all(carried, token_axes, 0, 0, tiled=True))  17.2 us
    pallas_call x1, Pallas kernels, long_convolution(): pl.pallas_call(long_kernel, in_specs=[whole, outside, outside], out_specs...  8.25 us
    pallas_call x1, Pallas kernels, query_side(): pl.pallas_call(query_kernel, grid=(channels // rows,), in_specs=[block, p...  7.92 us
    pallas_call x1, Pallas kernels, filter_spectrum(): pl.pallas_call(filter_kernel, in_specs=[whole, whole, whole, outside], ou...  6.94 us
    all_to_all x1, starting transfers between devices, per_device(): lax.all_to_all(gated[:, chunk], token_axes, 0, 0, tiled=True)  5.3 us
    all_to_all x1, starting transfers between devices, per_device(): returned.append(lax.all_to_all(carried, token_axes, 0, 0, tiled=True))  4.36 us
    ppermute x2, starting transfers between devices, passed_along(): return lax.ppermute(block, axis, route)  4.16 us
  transfers between devices with their start and end apart: 4, of which 3 were waited for; matrix products, arithmetic and copies ran while one was open for 0% of the time, Pallas kernels for 22%

profile of v4, /device:TPU:16, one launch (start us, length us, event | category | flops | bytes accessed | tf_op | source)
XLA Modules:
  0.0 83.6 jit_solution(10438726504327221522)
XLA Ops:
  0.6 2.0 %rims.1 = (bf16[16,4096]{1,0:T(8,128)(2,1)S(1)}, bf16[4096,128]{1,0:T(8,128)(2,1)S(1)}, bf16[4096,128]{1,0:T(8,128)(2,1)S(1)}) custom-call(bf16[4096,128]{1,0:T(8,128)(2,1)} %k_ref.1, bf16[4096,128]{1,0:T(8,128)(2,1)} %v_ref.1), custom_call_target="tpu_custom_call" | custom-call | flops 16777216 | bytes 2097152 | tf_op jit(solution)/shard_map/rims/pallas_call | solution.py:194
  2.7 1.9 %collective-permute-start = (bf16[16,4096]{1,0:T(8,128)(2,1)S(1)}, bf16[16,4096]{1,0:T(8,128)(2,1)S(1)}, u32[]{:S(2)}, u32[]{:S(2)}) collective-permute-start(bf16[16,4096]{1,0:T(8,128)(2,1)S(1)} %get-tuple-element.22), channel_id=1, source_target_pairs={{0,1},{1,2},{2,3},{3,4},{4,5},{5,6},{6,7},{7,8},{8,9},{9,10},{10,1... | collective-permute-start | bytes 393224 | tf_op jit(solution)/shard_map/ppermute | solution.py:45
  4.6 3.7 %inner.1 = (f32[32,128,128]{2,1,0:T(8,128)S(1)}, f32[2,32,8,128]{3,2,1,0:T(8,128)S(1)}, f32[3,7,4096]{2,1,0:T(8,128)S(1)}) custom-call(bf16[4096,128]{1,0:T(8,128)(2,1)S(1)} %get-tuple-element.17.k_ref, bf16[4096,128]{1,0:T(8,128)(2,1)S(1)} %get-tuple-element.18.v_ref, f32[3,7,4096]{2,1,0:T(8,128)} %taps_ref.3), custom_call_target="tpu_custom_call" | custom-call | flops 14680064 | bytes 4194304 | tf_op jit(solution)/shard_map/inner/pallas_call | solution.py:269
  8.3 1.5 %collective-permute-done.before_ref = bf16[16,4096]{1,0:T(8,128)(2,1)S(1)} collective-permute-done((bf16[16,4096]{1,0:T(8,128)(2,1)S(1)}, bf16[16,4096]{1,0:T(8,128)(2,1)S(1)}, u32[]{:S(2)}, u32[]{:S(2)}) %collective-permute-start) | collective-permute-done | bytes 131104 | tf_op jit(solution)/shard_map/ppermute | solution.py:45
  9.8 0.0 copy-start.3
  9.8 0.0 copy-start.4
  9.8 0.0 copy-start.5
  9.8 1.2 %gated.1 = bf16[32,128,128]{2,1,0:T(8,128)(2,1)} custom-call(f32[32,128,128]{2,1,0:T(8,128)S(1)} %get-tuple-element.19.part_ref, f32[2,32,8,128]{3,2,1,0:T(8,128)S(1)} %get-tuple-element.20.first_ref, f32[3,7,4096]{2,1,0:T(8,128)S(1)} %get-tuple-element.21.taps_ref, bf16[16,4096]{1,0:T(8,128)(2,1)S(1)} %collective-permute-done.before_ref), custom_call_target="tpu_custom_call" | custom-call | flops 2097152 | bytes 3145728 | tf_op jit(solution)/shard_map/gated/pallas_call | solution.py:317
  11.1 5.3 %all-to-all-start = ((bf16[16,256,128]{2,1,0:T(8,128)(2,1)}), bf16[16,256,128]{2,1,0:T(8,128)(2,1)S(1)}, u32[]{:S(2)}, u32[]{:S(2)}) async-start(bf16[16,256,128]{2,1,0:T(8,128)(2,1)} %bitcast), calls=%async_computation | async-start | bytes 2097152 | tf_op jit(solution)/shard_map/all_to_all | solution.py:737
  16.4 0.0 copy-done.3
  16.4 0.0 copy-done.4
  16.4 0.0 copy-done.5
  16.4 6.9 %filter_spectrum.1 = (f32[17,256,256]{2,1,0:T(8,128)}, bf16[8,4096]{1,0:T(8,128)(2,1)}) custom-call(f32[256,2048]{1,0:T(8,128)S(1)} %copy-done.3, f32[1,256]{1,0:T(1,128)S(1)} %bitcast.8, bf16[2,256,256]{2,1,0:T(8,128)(2,1)S(1)} %copy-done.5, bf16[4096,128]{1,0:T(8,128)(2,1)} %q_ref.3), custom_call_target="tpu_custom_call" | custom-call | flops 1711276032 | bytes 6684672 | tf_op jit(solution)/shard_map/filter_spectrum/pallas_call | solution.py:424
  23.3 2.2 %collective-permute-start.1 = (bf16[8,4096]{1,0:T(8,128)(2,1)}, bf16[8,4096]{1,0:T(8,128)(2,1)S(1)}, u32[]{:S(2)}, u32[]{:S(2)}) collective-permute-start(bf16[8,4096]{1,0:T(8,128)(2,1)} %get-tuple-element.23), channel_id=1, source_target_pairs={{0,1},{1,2},{2,3},{3,4},{4,5},{5,6},{6,7},{7,8},{8,9},{9,10},{10,1... | collective-permute-start | bytes 196616 | tf_op jit(solution)/shard_map/ppermute | solution.py:45
  25.6 16.7 %collective-permute-done.1.before_ref = bf16[8,4096]{1,0:T(8,128)(2,1)S(1)} collective-permute-done((bf16[8,4096]{1,0:T(8,128)(2,1)}, bf16[8,4096]{1,0:T(8,128)(2,1)S(1)}, u32[]{:S(2)}, u32[]{:S(2)}) %collective-permute-start.1) | collective-permute-done | bytes 65568 | tf_op jit(solution)/shard_map/ppermute | solution.py:45
  42.2 0.0 all-to-all-done.x_ref
  42.2 8.3 %long_convolution.1 = bf16[16,256,128]{2,1,0:T(8,128)(2,1)} custom-call(bf16[16,256,128]{2,1,0:T(8,128)(2,1)S(1)} %all-to-all-done.x_ref, f32[17,256,256]{2,1,0:T(8,128)} %get-tuple-element.25.spec_out, bf16[2,256,256]{2,1,0:T(8,128)(2,1)} %constant.6.clone.table_ref.table_out), custom_call_target="tpu_custom_call" | custom-call | flops 3422552064 | bytes 6684672 | tf_op jit(solution)/shard_map/long_convolution/pallas_call | solution.py:543
  50.5 0.0 copy-start
  50.5 0.0 copy-start.1
  50.5 0.0 copy-start.2
  50.5 4.4 %all-to-all-start.1 = ((bf16[16,256,128]{2,1,0:T(8,128)(2,1)}), bf16[16,256,128]{2,1,0:T(8,128)(2,1)S(1)}, u32[]{:S(2)}, u32[]{:S(2)}) async-start(bf16[16,256,128]{2,1,0:T(8,128)(2,1)} %long_convolution.1), calls=%async_computation.1 | async-start | bytes 2097152 | tf_op jit(solution)/shard_map/all_to_all | solution.py:747
  54.9 0.0 copy-done
  54.9 0.0 copy-done.1
  54.9 0.0 copy-done.2
  54.9 7.9 %query_side.1 = (f32[4096,128]{1,0:T(8,128)}, bf16[4096,128]{1,0:T(8,128)(2,1)}, f32[128,128]{1,0:T(8,128)}) custom-call(bf16[4096,128]{1,0:T(8,128)(2,1)} %q_ref.3, bf16[8,4096]{1,0:T(8,128)(2,1)S(1)} %collective-permute-done.1.before_ref, f32[3,7,4096]{2,1,0:T(8,128)S(1)} %copy-done, bf16[4096,512]{1,0:T(8,128)(2,1)} %unembed_ref.1, s32[1,128]{1,0:T(1,128)S(1)} %bitcast.7, ...), custom_call_target="tpu_custom_call" | custom-call | flops 544210944 | bytes 8388608 | tf_op jit(solution)/shard_map/query_side/pallas_call | solution.py:602
  62.9 17.2 %all-to-all-done.1.carried_ref = bf16[16,256,128]{2,1,0:T(8,128)(2,1)S(1)} async-done(((bf16[16,256,128]{2,1,0:T(8,128)(2,1)}), bf16[16,256,128]{2,1,0:T(8,128)(2,1)S(1)}, u32[]{:S(2)}, u32[]{:S(2)}) %all-to-all-start.1) | async-done | bytes 1048608 | tf_op jit(solution)/shard_map/all_to_all | solution.py:747
  80.1 3.4 %result.1 = (bf16[16,256,128]{2,1,0:T(8,128)(2,1)}, f32[8,128]{1,0:T(8,128)}, f32[1,2]{1,0:T(1,128)}) custom-call(bf16[16,256,128]{2,1,0:T(8,128)(2,1)S(1)} %all-to-all-done.1.carried_ref, f32[16,256,128]{2,1,0:T(8,128)} %bitcast.9, bf16[16,256,128]{2,1,0:T(8,128)(2,1)} %bitcast.10, f32[128,128]{1,0:T(8,128)} %get-tuple-element.29.after_out, ...), custom_call_target="tpu_custom_call" | custom-call | flops 2097152 | bytes 5242880 | tf_op jit(solution)/shard_map/result/pallas_call | solution.py:685
  (2 shorter events, 0.0 us)
Async XLA Ops:
  2.7 7.2 %collective-permute-start = (bf16[16,4096]{1,0:T(8,128)(2,1)S(1)}, bf16[16,4096]{1,0:T(8,128)(2,1)S(1)}, u32[]{:S(2)}, u32[]{:S(2)}) collective-permute-start(bf16[16,4096]{1,0:T(8,128)(2,1)S(1)} %get-tuple-element.22), channel_id=1, source_target_pairs={{0,1},{1,2},{2,3},{3,4},{4,5},{5,6},{6,7},{7,8},{8,9},{9,10},{10,1... | collective-permute-start | bytes 393224 | tf_op jit(solution)/shard_map/ppermute | solution.py:45
  9.8 6.5 %copy-start.3 = (f32[256,2048]{1,0:T(8,128)S(1)}, f32[256,2048]{1,0:T(8,128)}, u32[]{:S(2)}) copy-start(f32[256,2048]{1,0:T(8,128)} %taps_ref.2) | copy-start | bytes 6291460
  9.8 6.5 %copy-start.4 = (f32[256]{0:T(256)S(1)}, f32[256]{0:T(256)}, u32[]{:S(2)}) copy-start(f32[256]{0:T(256)} %param.15) | copy-start | bytes 3076
  9.8 6.5 %copy-start.5 = (bf16[2,256,256]{2,1,0:T(8,128)(2,1)S(1)}, bf16[2,256,256]{2,1,0:T(8,128)(2,1)}, u32[]{:S(2)}) copy-start(bf16[2,256,256]{2,1,0:T(8,128)(2,1)} %constant.6.clone.table_ref.table_out) | copy-start | bytes 786436
  11.1 31.2 %all-to-all-start = ((bf16[16,256,128]{2,1,0:T(8,128)(2,1)}), bf16[16,256,128]{2,1,0:T(8,128)(2,1)S(1)}, u32[]{:S(2)}, u32[]{:S(2)}) async-start(bf16[16,256,128]{2,1,0:T(8,128)(2,1)} %bitcast), calls=%async_computation | async-start | bytes 2097152 | tf_op jit(solution)/shard_map/all_to_all | solution.py:737
  23.3 18.9 %collective-permute-start.1 = (bf16[8,4096]{1,0:T(8,128)(2,1)}, bf16[8,4096]{1,0:T(8,128)(2,1)S(1)}, u32[]{:S(2)}, u32[]{:S(2)}) collective-permute-start(bf16[8,4096]{1,0:T(8,128)(2,1)} %get-tuple-element.23), channel_id=1, source_target_pairs={{0,1},{1,2},{2,3},{3,4},{4,5},{5,6},{6,7},{7,8},{8,9},{9,10},{10,1... | collective-permute-start | bytes 196616 | tf_op jit(solution)/shard_map/ppermute | solution.py:45
  50.5 4.4 %copy-start = (f32[3,7,4096]{2,1,0:T(8,128)S(1)}, f32[3,7,4096]{2,1,0:T(8,128)}, u32[]{:S(2)}) copy-start(f32[3,7,4096]{2,1,0:T(8,128)} %taps_ref.3) | copy-start | bytes 1032196
  50.5 4.4 %copy-start.1 = (s32[2,64]{1,0:T(2,128)S(1)}, s32[2,64]{1,0:T(2,128)}, u32[]{:S(2)}) copy-start(s32[2,64]{1,0:T(2,128)} %ranks_ref.1) | copy-start | bytes 1540
  50.5 4.4 %copy-start.2 = (s32[128]{0:T(128)S(1)}, s32[128]{0:T(128)}, u32[]{:S(2)}) copy-start(s32[128]{0:T(128)} %param.17) | copy-start | bytes 1540
  50.5 29.5 %all-to-all-start.1 = ((bf16[16,256,128]{2,1,0:T(8,128)(2,1)}), bf16[16,256,128]{2,1,0:T(8,128)(2,1)S(1)}, u32[]{:S(2)}, u32[]{:S(2)}) async-start(bf16[16,256,128]{2,1,0:T(8,128)(2,1)} %long_convolution.1), calls=%async_computation.1 | async-start | bytes 2097152 | tf_op jit(solution)/shard_map/all_to_all | solution.py:747

commit v5 on v4

--- a/solution.py
+++ b/solution.py
@@ -353,11 +353,16 @@
         for value, part in ((re, slice(0, lanes)), (im, slice(lanes, 2 * lanes))):
             high, low = halves(value)
             high_ref[at, rows, part] = high
-            low_ref[at, rows, part] = low
+            if low_ref is not None:
+                low_ref[at, rows, part] = low
 
 
 def three_pass(ah, al, wh, wl, over):
     return dot(ah, wh, over) + (dot(al, wh, over) + dot(ah, wl, over))
+
+
+def two_pass(a, wh, wl, over):
+    return dot(a, wh, over) + dot(a, wl, over)
 
 
 def over_frequencies(count, body):
@@ -439,7 +444,7 @@
     )(long_filter, skip_gain.reshape(1, channels), table, in_hbm(query_input))
 
 
-def long_kernel(x_ref, spec_out, table_out, out_hbm, ah, al, back, spec_ref, table_ref, turn_ref, out_ref, sems):
+def long_kernel(x_ref, spec_out, table_out, out_hbm, ah, back, spec_ref, table_ref, turn_ref, out_ref, sems):
     blocks, channels, lanes = x_ref.shape
     count = blocks + 1
     table_load = pltpu.make_async_copy(table_out, table_ref, sems.at[0])
@@ -457,20 +462,19 @@
 
     def forward(rows):
         x = [x_ref[j, rows].astype(f32) for j in range(blocks)]
-        put_spectrum(padded_real_dft(x), turn_ref, ah, al, rows, lanes)
+        put_spectrum(padded_real_dft(x), turn_ref, ah, None, rows, lanes)
 
     def multiply(first, size, rows):
         def take(ref):
             part = ref[pl.ds(first, size), rows]
             return part.reshape(size * part.shape[1], 2 * lanes)
 
-        x = three_pass(take(ah), take(al), table_ref[0], table_ref[1], ((1,), (0,)))
+        x = two_pass(take(ah), table_ref[0], table_ref[1], ((1,), (0,)))
         spec = take(spec_ref)
         xr, xi = x[:, :lanes], x[:, lanes:]
         fr, fi = spec[:, :lanes], spec[:, lanes:]
         product = jnp.concatenate([xr * fr - xi * fi, xr * fi + xi * fr], axis=1)
-        high, low = halves(product)
-        y = three_pass(high, low, table_ref[0], table_ref[1], ((1,), (1,)))
+        y = two_pass(product.astype(bf16), table_ref[0], table_ref[1], ((1,), (1,)))
         back[pl.ds(first, size), rows] = y.reshape(size, -1, 2 * lanes)
 
     def backward(rows):
@@ -546,7 +550,6 @@
         out_specs=outside,
         out_shape=jax.ShapeDtypeStruct(arrived.shape, bf16),
         scratch_shapes=[
-            pltpu.VMEM((count, channels, 2 * lanes), bf16),
             pltpu.VMEM((count, channels, 2 * lanes), bf16),
             pltpu.VMEM((count, channels, 2 * lanes), f32),
             pltpu.VMEM((count, channels, 2 * lanes), f32),

time: 84.3 us -> 82.6 us (0.980)
  Pallas kernels: 33.4 us -> 31.8 us
    pallas_call x1, Pallas kernels: 8.25 us -> 6.65 us  [long_convolution(): pl.pallas_call(long_kernel, in_specs=[whole, outside, outside], out_specs...]
  transfers between devices with their start and end apart: 4 -> 4, of which waited for: 3 -> 3; matrix products, arithmetic and copies ran while one was open for 0% -> 0% of each run, Pallas kernels for 22% -> 23%
where the time goes in v5:
time: 82.6 us; the launch traced here: 82 us
  waiting for transfers between devices  35.4 us (43%)
  Pallas kernels  31.8 us (38%)
  starting transfers between devices  13.8 us (17%)
  between operations  0.92 us (1%)
    ppermute x2, waiting for transfers between devices, passed_along(): return lax.ppermute(block, axis, route)  18.2 us
    all_to_all x1, waiting for transfers between devices, per_device(): returned.append(lax.all_to_all(carried, token_axes, 0, 0, tiled=True))  17.2 us
    pallas_call x1, Pallas kernels, query_side(): pl.pallas_call(query_kernel, grid=(channels // rows,), in_specs=[block, p...  7.92 us
    pallas_call x1, Pallas kernels, filter_spectrum(): pl.pallas_call(filter_kernel, in_specs=[whole, whole, whole, outside], ou...  6.94 us
    pallas_call x1, Pallas kernels, long_convolution(): pl.pallas_call(long_kernel, in_specs=[whole, outside, outside], out_specs...  6.65 us
    all_to_all x1, starting transfers between devices, per_device(): lax.all_to_all(gated[:, chunk], token_axes, 0, 0, tiled=True)  5.3 us
    all_to_all x1, starting transfers between devices, per_device(): returned.append(lax.all_to_all(carried, token_axes, 0, 0, tiled=True))  4.36 us
    ppermute x2, starting transfers between devices, passed_along(): return lax.ppermute(block, axis, route)  4.16 us
  transfers between devices with their start and end apart: 4, of which 3 were waited for; matrix products, arithmetic and copies ran while one was open for 0% of the time, Pallas kernels for 23%

profile of v5, /device:TPU:16, one launch (start us, length us, event | category | flops | bytes accessed | tf_op | source)
XLA Modules:
  0.0 82.0 jit_solution(7420614694227818836)
XLA Ops:
  0.6 2.0 %rims.1 = (bf16[16,4096]{1,0:T(8,128)(2,1)S(1)}, bf16[4096,128]{1,0:T(8,128)(2,1)S(1)}, bf16[4096,128]{1,0:T(8,128)(2,1)S(1)}) custom-call(bf16[4096,128]{1,0:T(8,128)(2,1)} %k_ref.1, bf16[4096,128]{1,0:T(8,128)(2,1)} %v_ref.1), custom_call_target="tpu_custom_call" | custom-call | flops 16777216 | bytes 2097152 | tf_op jit(solution)/shard_map/rims/pallas_call | solution.py:194
  2.7 1.9 %collective-permute-start = (bf16[16,4096]{1,0:T(8,128)(2,1)S(1)}, bf16[16,4096]{1,0:T(8,128)(2,1)S(1)}, u32[]{:S(2)}, u32[]{:S(2)}) collective-permute-start(bf16[16,4096]{1,0:T(8,128)(2,1)S(1)} %get-tuple-element.22), channel_id=1, source_target_pairs={{0,1},{1,2},{2,3},{3,4},{4,5},{5,6},{6,7},{7,8},{8,9},{9,10},{10,1... | collective-permute-start | bytes 393224 | tf_op jit(solution)/shard_map/ppermute | solution.py:45
  4.6 3.7 %inner.1 = (f32[32,128,128]{2,1,0:T(8,128)S(1)}, f32[2,32,8,128]{3,2,1,0:T(8,128)S(1)}, f32[3,7,4096]{2,1,0:T(8,128)S(1)}) custom-call(bf16[4096,128]{1,0:T(8,128)(2,1)S(1)} %get-tuple-element.17.k_ref, bf16[4096,128]{1,0:T(8,128)(2,1)S(1)} %get-tuple-element.18.v_ref, f32[3,7,4096]{2,1,0:T(8,128)} %taps_ref.3), custom_call_target="tpu_custom_call" | custom-call | flops 14680064 | bytes 4194304 | tf_op jit(solution)/shard_map/inner/pallas_call | solution.py:269
  8.3 1.5 %collective-permute-done.before_ref = bf16[16,4096]{1,0:T(8,128)(2,1)S(1)} collective-permute-done((bf16[16,4096]{1,0:T(8,128)(2,1)S(1)}, bf16[16,4096]{1,0:T(8,128)(2,1)S(1)}, u32[]{:S(2)}, u32[]{:S(2)}) %collective-permute-start) | collective-permute-done | bytes 131104 | tf_op jit(solution)/shard_map/ppermute | solution.py:45
  9.8 0.0 copy-start.3
  9.8 0.0 copy-start.4
  9.8 0.0 copy-start.5
  9.8 1.2 %gated.1 = bf16[32,128,128]{2,1,0:T(8,128)(2,1)} custom-call(f32[32,128,128]{2,1,0:T(8,128)S(1)} %get-tuple-element.19.part_ref, f32[2,32,8,128]{3,2,1,0:T(8,128)S(1)} %get-tuple-element.20.first_ref, f32[3,7,4096]{2,1,0:T(8,128)S(1)} %get-tuple-element.21.taps_ref, bf16[16,4096]{1,0:T(8,128)(2,1)S(1)} %collective-permute-done.before_ref), custom_call_target="tpu_custom_call" | custom-call | flops 2097152 | bytes 3145728 | tf_op jit(solution)/shard_map/gated/pallas_call | solution.py:317
  11.1 5.3 %all-to-all-start = ((bf16[16,256,128]{2,1,0:T(8,128)(2,1)}), bf16[16,256,128]{2,1,0:T(8,128)(2,1)S(1)}, u32[]{:S(2)}, u32[]{:S(2)}) async-start(bf16[16,256,128]{2,1,0:T(8,128)(2,1)} %bitcast), calls=%async_computation | async-start | bytes 2097152 | tf_op jit(solution)/shard_map/all_to_all | solution.py:740
  16.4 0.0 copy-done.3
  16.4 0.0 copy-done.4
  16.4 0.0 copy-done.5
  16.4 6.9 %filter_spectrum.1 = (f32[17,256,256]{2,1,0:T(8,128)}, bf16[8,4096]{1,0:T(8,128)(2,1)}) custom-call(f32[256,2048]{1,0:T(8,128)S(1)} %copy-done.3, f32[1,256]{1,0:T(1,128)S(1)} %bitcast.8, bf16[2,256,256]{2,1,0:T(8,128)(2,1)S(1)} %copy-done.5, bf16[4096,128]{1,0:T(8,128)(2,1)} %q_ref.3), custom_call_target="tpu_custom_call" | custom-call | flops 1711276032 | bytes 6684672 | tf_op jit(solution)/shard_map/filter_spectrum/pallas_call | solution.py:429
  23.3 2.2 %collective-permute-start.1 = (bf16[8,4096]{1,0:T(8,128)(2,1)}, bf16[8,4096]{1,0:T(8,128)(2,1)S(1)}, u32[]{:S(2)}, u32[]{:S(2)}) collective-permute-start(bf16[8,4096]{1,0:T(8,128)(2,1)} %get-tuple-element.23), channel_id=1, source_target_pairs={{0,1},{1,2},{2,3},{3,4},{4,5},{5,6},{6,7},{7,8},{8,9},{9,10},{10,1... | collective-permute-start | bytes 196616 | tf_op jit(solution)/shard_map/ppermute | solution.py:45
  25.6 16.7 %collective-permute-done.1.before_ref = bf16[8,4096]{1,0:T(8,128)(2,1)S(1)} collective-permute-done((bf16[8,4096]{1,0:T(8,128)(2,1)}, bf16[8,4096]{1,0:T(8,128)(2,1)S(1)}, u32[]{:S(2)}, u32[]{:S(2)}) %collective-permute-start.1) | collective-permute-done | bytes 65568 | tf_op jit(solution)/shard_map/ppermute | solution.py:45
  42.2 0.0 all-to-all-done.x_ref
  42.2 6.6 %long_convolution.1 = bf16[16,256,128]{2,1,0:T(8,128)(2,1)} custom-call(bf16[16,256,128]{2,1,0:T(8,128)(2,1)S(1)} %all-to-all-done.x_ref, f32[17,256,256]{2,1,0:T(8,128)} %get-tuple-element.25.spec_out, bf16[2,256,256]{2,1,0:T(8,128)(2,1)} %constant.6.clone.table_ref.table_out), custom_call_target="tpu_custom_call" | custom-call | flops 3422552064 | bytes 6684672 | tf_op jit(solution)/shard_map/long_convolution/pallas_call | solution.py:547
  48.9 0.0 copy-start
  48.9 0.0 copy-start.1
  48.9 0.0 copy-start.2
  48.9 4.4 %all-to-all-start.1 = ((bf16[16,256,128]{2,1,0:T(8,128)(2,1)}), bf16[16,256,128]{2,1,0:T(8,128)(2,1)S(1)}, u32[]{:S(2)}, u32[]{:S(2)}) async-start(bf16[16,256,128]{2,1,0:T(8,128)(2,1)} %long_convolution.1), calls=%async_computation.1 | async-start | bytes 2097152 | tf_op jit(solution)/shard_map/all_to_all | solution.py:750
  53.3 0.0 copy-done
  53.3 0.0 copy-done.1
  53.3 0.0 copy-done.2
  53.3 7.9 %query_side.1 = (f32[4096,128]{1,0:T(8,128)}, bf16[4096,128]{1,0:T(8,128)(2,1)}, f32[128,128]{1,0:T(8,128)}) custom-call(bf16[4096,128]{1,0:T(8,128)(2,1)} %q_ref.3, bf16[8,4096]{1,0:T(8,128)(2,1)S(1)} %collective-permute-done.1.before_ref, f32[3,7,4096]{2,1,0:T(8,128)S(1)} %copy-done, bf16[4096,512]{1,0:T(8,128)(2,1)} %unembed_ref.1, s32[1,128]{1,0:T(1,128)S(1)} %bitcast.7, ...), custom_call_target="tpu_custom_call" | custom-call | flops 544210944 | bytes 8388608 | tf_op jit(solution)/shard_map/query_side/pallas_call | solution.py:605
  61.2 17.2 %all-to-all-done.1.carried_ref = bf16[16,256,128]{2,1,0:T(8,128)(2,1)S(1)} async-done(((bf16[16,256,128]{2,1,0:T(8,128)(2,1)}), bf16[16,256,128]{2,1,0:T(8,128)(2,1)S(1)}, u32[]{:S(2)}, u32[]{:S(2)}) %all-to-all-start.1) | async-done | bytes 1048608 | tf_op jit(solution)/shard_map/all_to_all | solution.py:750
  78.5 3.4 %result.1 = (bf16[16,256,128]{2,1,0:T(8,128)(2,1)}, f32[8,128]{1,0:T(8,128)}, f32[1,2]{1,0:T(1,128)}) custom-call(bf16[16,256,128]{2,1,0:T(8,128)(2,1)S(1)} %all-to-all-done.1.carried_ref, f32[16,256,128]{2,1,0:T(8,128)} %bitcast.9, bf16[16,256,128]{2,1,0:T(8,128)(2,1)} %bitcast.10, f32[128,128]{1,0:T(8,128)} %get-tuple-element.29.after_out, ...), custom_call_target="tpu_custom_call" | custom-call | flops 2097152 | bytes 5242880 | tf_op jit(solution)/shard_map/result/pallas_call | solution.py:688
  (2 shorter events, 0.0 us)
Async XLA Ops:
  2.7 7.2 %collective-permute-start = (bf16[16,4096]{1,0:T(8,128)(2,1)S(1)}, bf16[16,4096]{1,0:T(8,128)(2,1)S(1)}, u32[]{:S(2)}, u32[]{:S(2)}) collective-permute-start(bf16[16,4096]{1,0:T(8,128)(2,1)S(1)} %get-tuple-element.22), channel_id=1, source_target_pairs={{0,1},{1,2},{2,3},{3,4},{4,5},{5,6},{6,7},{7,8},{8,9},{9,10},{10,1... | collective-permute-start | bytes 393224 | tf_op jit(solution)/shard_map/ppermute | solution.py:45
  9.8 6.5 %copy-start.3 = (f32[256,2048]{1,0:T(8,128)S(1)}, f32[256,2048]{1,0:T(8,128)}, u32[]{:S(2)}) copy-start(f32[256,2048]{1,0:T(8,128)} %taps_ref.2) | copy-start | bytes 6291460
  9.8 6.5 %copy-start.4 = (f32[256]{0:T(256)S(1)}, f32[256]{0:T(256)}, u32[]{:S(2)}) copy-start(f32[256]{0:T(256)} %param.15) | copy-start | bytes 3076
  9.8 6.5 %copy-start.5 = (bf16[2,256,256]{2,1,0:T(8,128)(2,1)S(1)}, bf16[2,256,256]{2,1,0:T(8,128)(2,1)}, u32[]{:S(2)}) copy-start(bf16[2,256,256]{2,1,0:T(8,128)(2,1)} %constant.6.clone.table_ref.table_out) | copy-start | bytes 786436
  11.1 31.2 %all-to-all-start = ((bf16[16,256,128]{2,1,0:T(8,128)(2,1)}), bf16[16,256,128]{2,1,0:T(8,128)(2,1)S(1)}, u32[]{:S(2)}, u32[]{:S(2)}) async-start(bf16[16,256,128]{2,1,0:T(8,128)(2,1)} %bitcast), calls=%async_computation | async-start | bytes 2097152 | tf_op jit(solution)/shard_map/all_to_all | solution.py:740
  23.3 18.9 %collective-permute-start.1 = (bf16[8,4096]{1,0:T(8,128)(2,1)}, bf16[8,4096]{1,0:T(8,128)(2,1)S(1)}, u32[]{:S(2)}, u32[]{:S(2)}) collective-permute-start(bf16[8,4096]{1,0:T(8,128)(2,1)} %get-tuple-element.23), channel_id=1, source_target_pairs={{0,1},{1,2},{2,3},{3,4},{4,5},{5,6},{6,7},{7,8},{8,9},{9,10},{10,1... | collective-permute-start | bytes 196616 | tf_op jit(solution)/shard_map/ppermute | solution.py:45
  48.9 4.4 %copy-start = (f32[3,7,4096]{2,1,0:T(8,128)S(1)}, f32[3,7,4096]{2,1,0:T(8,128)}, u32[]{:S(2)}) copy-start(f32[3,7,4096]{2,1,0:T(8,128)} %taps_ref.3) | copy-start | bytes 1032196
  48.9 4.4 %copy-start.1 = (s32[2,64]{1,0:T(2,128)S(1)}, s32[2,64]{1,0:T(2,128)}, u32[]{:S(2)}) copy-start(s32[2,64]{1,0:T(2,128)} %ranks_ref.1) | copy-start | bytes 1540
  48.9 4.4 %copy-start.2 = (s32[128]{0:T(128)S(1)}, s32[128]{0:T(128)}, u32[]{:S(2)}) copy-start(s32[128]{0:T(128)} %param.17) | copy-start | bytes 1540
  48.9 29.5 %all-to-all-start.1 = ((bf16[16,256,128]{2,1,0:T(8,128)(2,1)}), bf16[16,256,128]{2,1,0:T(8,128)(2,1)S(1)}, u32[]{:S(2)}, u32[]{:S(2)}) async-start(bf16[16,256,128]{2,1,0:T(8,128)(2,1)} %long_convolution.1), calls=%async_computation.1 | async-start | bytes 2097152 | tf_op jit(solution)/shard_map/all_to_all | solution.py:750

commit v6 on v5

--- a/solution.py
+++ b/solution.py
@@ -361,10 +361,6 @@
     return dot(ah, wh, over) + (dot(al, wh, over) + dot(ah, wl, over))
 
 
-def two_pass(a, wh, wl, over):
-    return dot(a, wh, over) + dot(a, wl, over)
-
-
 def over_frequencies(count, body):
     if count <= 33:
         for k in range(count):
@@ -395,7 +391,7 @@
         scale = jnp.where(ends, 1.0, 2.0) / (2 * blocks * lanes)
         spec = three_pass(ah[k], al[k], table_ref[0], table_ref[1], ((1,), (0,))) * scale
         for at, ref in enumerate(spec_refs):
-            ref[k] = spec[at * per : (at + 1) * per]
+            ref[k] = spec[at * per : (at + 1) * per].astype(bf16)
 
     over_frequencies(blocks + 1, one)
     load.wait()
@@ -430,7 +426,7 @@
         filter_kernel,
         in_specs=[whole, whole, whole, outside],
         out_specs=[whole] * (chunks + 1),
-        out_shape=[pltpu.HBM((count, channels // chunks, 2 * lanes), f32)] * chunks
+        out_shape=[pltpu.HBM((count, channels // chunks, 2 * lanes), bf16)] * chunks
         + [pltpu.HBM((rim, query_input.shape[0]), bf16)],
         scratch_shapes=[pltpu.VMEM((count, channels, 2 * lanes), bf16)] * 2
         + [
@@ -447,7 +443,7 @@
 def long_kernel(x_ref, spec_out, table_out, out_hbm, ah, back, spec_ref, table_ref, turn_ref, out_ref, sems):
     blocks, channels, lanes = x_ref.shape
     count = blocks + 1
-    table_load = pltpu.make_async_copy(table_out, table_ref, sems.at[0])
+    table_load = pltpu.make_async_copy(table_out.at[0], table_ref, sems.at[0])
     split = channels % (long_parts * step_rows) == 0 and count <= 33
     share = channels // long_parts if split else channels
     parts = [slice(first, first + share) for first in range(0, channels, share)]
@@ -469,12 +465,12 @@
             part = ref[pl.ds(first, size), rows]
             return part.reshape(size * part.shape[1], 2 * lanes)
 
-        x = two_pass(take(ah), table_ref[0], table_ref[1], ((1,), (0,)))
-        spec = take(spec_ref)
+        x = dot(take(ah), table_ref[...], ((1,), (0,)))
+        spec = take(spec_ref).astype(f32)
         xr, xi = x[:, :lanes], x[:, lanes:]
         fr, fi = spec[:, :lanes], spec[:, lanes:]
         product = jnp.concatenate([xr * fr - xi * fi, xr * fi + xi * fr], axis=1)
-        y = two_pass(product.astype(bf16), table_ref[0], table_ref[1], ((1,), (1,)))
+        y = dot(product.astype(bf16), table_ref[...], ((1,), (1,)))
         back[pl.ds(first, size), rows] = y.reshape(size, -1, 2 * lanes)
 
     def backward(rows):
@@ -552,8 +548,8 @@
         scratch_shapes=[
             pltpu.VMEM((count, channels, 2 * lanes), bf16),
             pltpu.VMEM((count, channels, 2 * lanes), f32),
-            pltpu.VMEM((count, channels, 2 * lanes), f32),
-            pltpu.VMEM(table.shape, bf16),
+            pltpu.VMEM((count, channels, 2 * lanes), bf16),
+            pltpu.VMEM(table.shape[1:], bf16),
             pltpu.VMEM((2, count, lanes), f32),
             pltpu.VMEM(arrived.shape, bf16),
             pltpu.SemaphoreType.DMA((1 + 2 * long_parts,)),

time: 82.6 us -> 81.3 us (0.984)
  Pallas kernels: 31.8 us -> 29.8 us
    pallas_call x1, Pallas kernels: 6.65 us -> 5.26 us  [long_convolution(): pl.pallas_call(long_kernel, in_specs=[whole, outside, outside], out_specs...]
  transfers between devices with their start and end apart: 4 -> 4, of which waited for: 3 -> 3; matrix products, arithmetic and copies ran while one was open for 0% -> 0% of each run, Pallas kernels for 23% -> 22%
where the time goes in v6:
time: 81.3 us; the launch traced here: 80.6 us
  waiting for transfers between devices  36.1 us (44%)
  Pallas kernels  29.8 us (37%)
  starting transfers between devices  13.8 us (17%)
  between operations  0.92 us (1%)
    ppermute x2, waiting for transfers between devices, passed_along(): return lax.ppermute(block, axis, route)  18.8 us
    all_to_all x1, waiting for transfers between devices, per_device(): returned.append(lax.all_to_all(carried, token_axes, 0, 0, tiled=True))  17.2 us
    pallas_call x1, Pallas kernels, query_side(): pl.pallas_call(query_kernel, grid=(channels // rows,), in_specs=[block, p...  7.92 us
    pallas_call x1, Pallas kernels, filter_spectrum(): pl.pallas_call(filter_kernel, in_specs=[whole, whole, whole, outside], ou...  6.27 us
    all_to_all x1, starting transfers between devices, per_device(): lax.all_to_all(gated[:, chunk], token_axes, 0, 0, tiled=True)  5.3 us
    pallas_call x1, Pallas kernels, long_convolution(): pl.pallas_call(long_kernel, in_specs=[whole, outside, outside], out_specs...  5.26 us
    all_to_all x1, starting transfers between devices, per_device(): returned.append(lax.all_to_all(carried, token_axes, 0, 0, tiled=True))  4.36 us
    ppermute x2, starting transfers between devices, passed_along(): return lax.ppermute(block, axis, route)  4.16 us
  transfers between devices with their start and end apart: 4, of which 3 were waited for; matrix products, arithmetic and copies ran while one was open for 0% of the time, Pallas kernels for 22%

profile of v6, /device:TPU:16, one launch (start us, length us, event | category | flops | bytes accessed | tf_op | source)
XLA Modules:
  0.0 80.6 jit_solution(967528568127675658)
XLA Ops:
  0.6 2.0 %rims.1 = (bf16[16,4096]{1,0:T(8,128)(2,1)S(1)}, bf16[4096,128]{1,0:T(8,128)(2,1)S(1)}, bf16[4096,128]{1,0:T(8,128)(2,1)S(1)}) custom-call(bf16[4096,128]{1,0:T(8,128)(2,1)} %k_ref.1, bf16[4096,128]{1,0:T(8,128)(2,1)} %v_ref.1), custom_call_target="tpu_custom_call" | custom-call | flops 16777216 | bytes 2097152 | tf_op jit(solution)/shard_map/rims/pallas_call | solution.py:194
  2.7 1.9 %collective-permute-start = (bf16[16,4096]{1,0:T(8,128)(2,1)S(1)}, bf16[16,4096]{1,0:T(8,128)(2,1)S(1)}, u32[]{:S(2)}, u32[]{:S(2)}) collective-permute-start(bf16[16,4096]{1,0:T(8,128)(2,1)S(1)} %get-tuple-element.22), channel_id=1, source_target_pairs={{0,1},{1,2},{2,3},{3,4},{4,5},{5,6},{6,7},{7,8},{8,9},{9,10},{10,1... | collective-permute-start | bytes 393224 | tf_op jit(solution)/shard_map/ppermute | solution.py:45
  4.6 3.7 %inner.1 = (f32[32,128,128]{2,1,0:T(8,128)S(1)}, f32[2,32,8,128]{3,2,1,0:T(8,128)S(1)}, f32[3,7,4096]{2,1,0:T(8,128)S(1)}) custom-call(bf16[4096,128]{1,0:T(8,128)(2,1)S(1)} %get-tuple-element.17.k_ref, bf16[4096,128]{1,0:T(8,128)(2,1)S(1)} %get-tuple-element.18.v_ref, f32[3,7,4096]{2,1,0:T(8,128)} %taps_ref.3), custom_call_target="tpu_custom_call" | custom-call | flops 14680064 | bytes 4194304 | tf_op jit(solution)/shard_map/inner/pallas_call | solution.py:269
  8.3 1.5 %collective-permute-done.before_ref = bf16[16,4096]{1,0:T(8,128)(2,1)S(1)} collective-permute-done((bf16[16,4096]{1,0:T(8,128)(2,1)S(1)}, bf16[16,4096]{1,0:T(8,128)(2,1)S(1)}, u32[]{:S(2)}, u32[]{:S(2)}) %collective-permute-start) | collective-permute-done | bytes 131104 | tf_op jit(solution)/shard_map/ppermute | solution.py:45
  9.8 0.0 copy-start.3
  9.8 0.0 copy-start.4
  9.8 0.0 copy-start.5
  9.8 1.2 %gated.1 = bf16[32,128,128]{2,1,0:T(8,128)(2,1)} custom-call(f32[32,128,128]{2,1,0:T(8,128)S(1)} %get-tuple-element.19.part_ref, f32[2,32,8,128]{3,2,1,0:T(8,128)S(1)} %get-tuple-element.20.first_ref, f32[3,7,4096]{2,1,0:T(8,128)S(1)} %get-tuple-element.21.taps_ref, bf16[16,4096]{1,0:T(8,128)(2,1)S(1)} %collective-permute-done.before_ref), custom_call_target="tpu_custom_call" | custom-call | flops 2097152 | bytes 3145728 | tf_op jit(solution)/shard_map/gated/pallas_call | solution.py:317
  11.1 5.3 %all-to-all-start = ((bf16[16,256,128]{2,1,0:T(8,128)(2,1)}), bf16[16,256,128]{2,1,0:T(8,128)(2,1)S(1)}, u32[]{:S(2)}, u32[]{:S(2)}) async-start(bf16[16,256,128]{2,1,0:T(8,128)(2,1)} %bitcast), calls=%async_computation | async-start | bytes 2097152 | tf_op jit(solution)/shard_map/all_to_all | solution.py:736
  16.4 0.0 copy-done.3
  16.4 0.0 copy-done.4
  16.4 0.0 copy-done.5
  16.4 6.3 %filter_spectrum.1 = (bf16[17,256,256]{2,1,0:T(8,128)(2,1)}, bf16[8,4096]{1,0:T(8,128)(2,1)}) custom-call(f32[256,2048]{1,0:T(8,128)S(1)} %copy-done.3, f32[1,256]{1,0:T(1,128)S(1)} %bitcast.8, bf16[2,256,256]{2,1,0:T(8,128)(2,1)S(1)} %copy-done.5, bf16[4096,128]{1,0:T(8,128)(2,1)} %q_ref.3), custom_call_target="tpu_custom_call" | custom-call | flops 1711276032 | bytes 6684672 | tf_op jit(solution)/shard_map/filter_spectrum/pallas_call | solution.py:425
  22.7 2.2 %collective-permute-start.1 = (bf16[8,4096]{1,0:T(8,128)(2,1)}, bf16[8,4096]{1,0:T(8,128)(2,1)S(1)}, u32[]{:S(2)}, u32[]{:S(2)}) collective-permute-start(bf16[8,4096]{1,0:T(8,128)(2,1)} %get-tuple-element.23), channel_id=1, source_target_pairs={{0,1},{1,2},{2,3},{3,4},{4,5},{5,6},{6,7},{7,8},{8,9},{9,10},{10,1... | collective-permute-start | bytes 196616 | tf_op jit(solution)/shard_map/ppermute | solution.py:45
  24.9 17.3 %collective-permute-done.1.before_ref = bf16[8,4096]{1,0:T(8,128)(2,1)S(1)} collective-permute-done((bf16[8,4096]{1,0:T(8,128)(2,1)}, bf16[8,4096]{1,0:T(8,128)(2,1)S(1)}, u32[]{:S(2)}, u32[]{:S(2)}) %collective-permute-start.1) | collective-permute-done | bytes 65568 | tf_op jit(solution)/shard_map/ppermute | solution.py:45
  42.2 0.0 all-to-all-done.x_ref
  42.2 5.3 %long_convolution.1 = bf16[16,256,128]{2,1,0:T(8,128)(2,1)} custom-call(bf16[16,256,128]{2,1,0:T(8,128)(2,1)S(1)} %all-to-all-done.x_ref, bf16[17,256,256]{2,1,0:T(8,128)(2,1)} %get-tuple-element.25.spec_out, bf16[2,256,256]{2,1,0:T(8,128)(2,1)} %constant.6.clone.table_ref.table_out), custom_call_target="tpu_custom_call" | custom-call | flops 3422552064 | bytes 6684672 | tf_op jit(solution)/shard_map/long_convolution/pallas_call | solution.py:543
  47.5 0.0 copy-start
  47.5 0.0 copy-start.1
  47.5 0.0 copy-start.2
  47.5 4.4 %all-to-all-start.1 = ((bf16[16,256,128]{2,1,0:T(8,128)(2,1)}), bf16[16,256,128]{2,1,0:T(8,128)(2,1)S(1)}, u32[]{:S(2)}, u32[]{:S(2)}) async-start(bf16[16,256,128]{2,1,0:T(8,128)(2,1)} %long_convolution.1), calls=%async_computation.1 | async-start | bytes 2097152 | tf_op jit(solution)/shard_map/all_to_all | solution.py:746
  51.9 0.0 copy-done
  51.9 0.0 copy-done.1
  51.9 0.0 copy-done.2
  51.9 7.9 %query_side.1 = (f32[4096,128]{1,0:T(8,128)}, bf16[4096,128]{1,0:T(8,128)(2,1)}, f32[128,128]{1,0:T(8,128)}) custom-call(bf16[4096,128]{1,0:T(8,128)(2,1)} %q_ref.3, bf16[8,4096]{1,0:T(8,128)(2,1)S(1)} %collective-permute-done.1.before_ref, f32[3,7,4096]{2,1,0:T(8,128)S(1)} %copy-done, bf16[4096,512]{1,0:T(8,128)(2,1)} %unembed_ref.1, s32[1,128]{1,0:T(1,128)S(1)} %bitcast.7, ...), custom_call_target="tpu_custom_call" | custom-call | flops 544210944 | bytes 8388608 | tf_op jit(solution)/shard_map/query_side/pallas_call | solution.py:601
  59.9 17.2 %all-to-all-done.1.carried_ref = bf16[16,256,128]{2,1,0:T(8,128)(2,1)S(1)} async-done(((bf16[16,256,128]{2,1,0:T(8,128)(2,1)}), bf16[16,256,128]{2,1,0:T(8,128)(2,1)S(1)}, u32[]{:S(2)}, u32[]{:S(2)}) %all-to-all-start.1) | async-done | bytes 1048608 | tf_op jit(solution)/shard_map/all_to_all | solution.py:746
  77.1 3.4 %result.1 = (bf16[16,256,128]{2,1,0:T(8,128)(2,1)}, f32[8,128]{1,0:T(8,128)}, f32[1,2]{1,0:T(1,128)}) custom-call(bf16[16,256,128]{2,1,0:T(8,128)(2,1)S(1)} %all-to-all-done.1.carried_ref, f32[16,256,128]{2,1,0:T(8,128)} %bitcast.9, bf16[16,256,128]{2,1,0:T(8,128)(2,1)} %bitcast.10, f32[128,128]{1,0:T(8,128)} %get-tuple-element.29.after_out, ...), custom_call_target="tpu_custom_call" | custom-call | flops 2097152 | bytes 5242880 | tf_op jit(solution)/shard_map/result/pallas_call | solution.py:684
  (2 shorter events, 0.0 us)
Async XLA Ops:
  2.7 7.2 %collective-permute-start = (bf16[16,4096]{1,0:T(8,128)(2,1)S(1)}, bf16[16,4096]{1,0:T(8,128)(2,1)S(1)}, u32[]{:S(2)}, u32[]{:S(2)}) collective-permute-start(bf16[16,4096]{1,0:T(8,128)(2,1)S(1)} %get-tuple-element.22), channel_id=1, source_target_pairs={{0,1},{1,2},{2,3},{3,4},{4,5},{5,6},{6,7},{7,8},{8,9},{9,10},{10,1... | collective-permute-start | bytes 393224 | tf_op jit(solution)/shard_map/ppermute | solution.py:45
  9.8 6.5 %copy-start.3 = (f32[256,2048]{1,0:T(8,128)S(1)}, f32[256,2048]{1,0:T(8,128)}, u32[]{:S(2)}) copy-start(f32[256,2048]{1,0:T(8,128)} %taps_ref.2) | copy-start | bytes 6291460
  9.8 6.5 %copy-start.4 = (f32[256]{0:T(256)S(1)}, f32[256]{0:T(256)}, u32[]{:S(2)}) copy-start(f32[256]{0:T(256)} %param.15) | copy-start | bytes 3076
  9.8 6.5 %copy-start.5 = (bf16[2,256,256]{2,1,0:T(8,128)(2,1)S(1)}, bf16[2,256,256]{2,1,0:T(8,128)(2,1)}, u32[]{:S(2)}) copy-start(bf16[2,256,256]{2,1,0:T(8,128)(2,1)} %constant.6.clone.table_ref.table_out) | copy-start | bytes 786436
  11.1 31.2 %all-to-all-start = ((bf16[16,256,128]{2,1,0:T(8,128)(2,1)}), bf16[16,256,128]{2,1,0:T(8,128)(2,1)S(1)}, u32[]{:S(2)}, u32[]{:S(2)}) async-start(bf16[16,256,128]{2,1,0:T(8,128)(2,1)} %bitcast), calls=%async_computation | async-start | bytes 2097152 | tf_op jit(solution)/shard_map/all_to_all | solution.py:736
  22.7 19.6 %collective-permute-start.1 = (bf16[8,4096]{1,0:T(8,128)(2,1)}, bf16[8,4096]{1,0:T(8,128)(2,1)S(1)}, u32[]{:S(2)}, u32[]{:S(2)}) collective-permute-start(bf16[8,4096]{1,0:T(8,128)(2,1)} %get-tuple-element.23), channel_id=1, source_target_pairs={{0,1},{1,2},{2,3},{3,4},{4,5},{5,6},{6,7},{7,8},{8,9},{9,10},{10,1... | collective-permute-start | bytes 196616 | tf_op jit(solution)/shard_map/ppermute | solution.py:45
  47.5 4.4 %copy-start = (f32[3,7,4096]{2,1,0:T(8,128)S(1)}, f32[3,7,4096]{2,1,0:T(8,128)}, u32[]{:S(2)}) copy-start(f32[3,7,4096]{2,1,0:T(8,128)} %taps_ref.3) | copy-start | bytes 1032196
  47.5 4.4 %copy-start.1 = (s32[2,64]{1,0:T(2,128)S(1)}, s32[2,64]{1,0:T(2,128)}, u32[]{:S(2)}) copy-start(s32[2,64]{1,0:T(2,128)} %ranks_ref.1) | copy-start | bytes 1540
  47.5 4.4 %copy-start.2 = (s32[128]{0:T(128)S(1)}, s32[128]{0:T(128)}, u32[]{:S(2)}) copy-start(s32[128]{0:T(128)} %param.17) | copy-start | bytes 1540
  47.5 29.5 %all-to-all-start.1 = ((bf16[16,256,128]{2,1,0:T(8,128)(2,1)}), bf16[16,256,128]{2,1,0:T(8,128)(2,1)S(1)}, u32[]{:S(2)}, u32[]{:S(2)}) async-start(bf16[16,256,128]{2,1,0:T(8,128)(2,1)} %long_convolution.1), calls=%async_computation.1 | async-start | bytes 2097152 | tf_op jit(solution)/shard_map/all_to_all | solution.py:746

commit v7 on v6

--- a/solution.py
+++ b/solution.py
@@ -167,7 +167,7 @@
     return (lane == row + (lanes - rim)).astype(bf16)
 
 
-def rim_kernel(k_ref, v_ref, out_ref, held_k, held_v, sems):
+def rim_kernel(k_ref, v_ref, taps_out, out_ref, held_k, held_v, taps_ref, sems, taps_sem):
     pieces = sems.shape[1]
     channels, lanes = k_ref.shape
     rows = channels // pieces
@@ -180,28 +180,32 @@
     for group in copies:
         for copy in group:
             copy.start()
+    taps_load = pltpu.make_async_copy(taps_out, taps_ref, taps_sem)
+    taps_load.start()
     picker = rim_picker(lanes)
     for part, group in zip(parts, copies):
         for copy in group:
             copy.wait()
         last = [dot(picker, held[part], ((1,), (1,))) for _, held in pairs]
         out_ref[:, part] = jnp.concatenate(last, axis=0).astype(bf16)
-
-
-def rims(key_input, value_input):
+    taps_load.wait()
+
+
+def rims(key_input, value_input, short_taps):
     channels, tokens = key_input.shape
     pieces = 2
     return pl.pallas_call(
         rim_kernel,
-        in_specs=[outside] * 2,
-        out_specs=[whole] * 3,
+        in_specs=[outside] * 3,
+        out_specs=[whole] * 4,
         out_shape=[jax.ShapeDtypeStruct((2 * rim, channels), bf16)]
-        + [pltpu.VMEM((channels, tokens), bf16)] * 2,
-        scratch_shapes=[pltpu.SemaphoreType.DMA((2, pieces))],
+        + [pltpu.VMEM((channels, tokens), bf16)] * 2
+        + [pltpu.VMEM(short_taps.shape, f32)],
+        scratch_shapes=[pltpu.SemaphoreType.DMA((2, pieces)), pltpu.SemaphoreType.DMA],
         compiler_params=params(6),
         cost_estimate=cost(4 * channels * tokens * rim, 4 * channels * tokens),
         name="rims",
-    )(in_hbm(key_input), in_hbm(value_input))
+    )(in_hbm(key_input), in_hbm(value_input), in_hbm(short_taps))
 
 
 def short_conv(x, before, taps_ref, which, lanes, space):
@@ -241,11 +245,8 @@
     ]
 
 
-def inner_kernel(k_ref, v_ref, taps_out, part_ref, first_ref, taps_ref, key_space, value_space, sem):
+def inner_kernel(k_ref, v_ref, taps_ref, part_ref, first_ref, key_space, value_space):
     tiles, tokens, _ = part_ref.shape
-    load = pltpu.make_async_copy(taps_out, taps_ref, sem)
-    load.start()
-    load.wait()
     unroll = math.gcd(tiles, 4)
     for group in range(tiles // unroll):
 
@@ -268,22 +269,20 @@
     tiles = channels // tile
     return pl.pallas_call(
         inner_kernel,
-        in_specs=[whole, whole, outside],
-        out_specs=[whole] * 3,
+        in_specs=[whole] * 3,
+        out_specs=[whole] * 2,
         out_shape=[
             pltpu.VMEM((tiles, tokens, tile), f32),
             pltpu.VMEM((2, tiles, rim, tile), f32),
-            pltpu.VMEM(short_taps.shape, f32),
         ],
         scratch_shapes=[
             pltpu.VMEM((rim + tokens, tile), f32),
             pltpu.VMEM((rim + tokens, tile), f32),
-            pltpu.SemaphoreType.DMA,
         ],
         compiler_params=params(8),
         cost_estimate=cost(28 * channels * tokens, 8 * channels * tokens),
         name="inner",
-    )(key_input, value_input, in_hbm(short_taps))
+    )(key_input, value_input, short_taps)
 
 
 def gated_kernel(part_ref, first_ref, taps_ref, before_ref, out_ref, made, key_space, value_space, sems):
@@ -677,7 +676,7 @@
 def result(chunk, chunks, carried, query_short, picked, after, lists, total, out):
     owners, per, tokens = carried.shape
     local = per * chunks
-    groups = math.gcd(owners, 8)
+    groups = math.gcd(owners, 4)
     start = out is None
     if start:
         total, out = jnp.zeros((8, tokens), f32), jnp.zeros((8, tokens), bf16)
@@ -728,10 +727,10 @@
     local = channels // owners
     lists = rankings.shape[0]
     chunks = most_chunks if local % (most_chunks * tile) == 0 else 1
-    last, held_key, held_value = rims(key_input, value_input)
+    last, held_key, held_value, held_taps = rims(key_input, value_input, short_taps)
     before = passed_along(last, token_axes, 1)
-    inner = inner_features(held_key, held_value, short_taps)
-    gated = gated_features(*inner, before).reshape(owners, chunks, local // chunks, tokens)
+    inner = inner_features(held_key, held_value, held_taps)
+    gated = gated_features(*inner, held_taps, before).reshape(owners, chunks, local // chunks, tokens)
     arrived = [
         lax.all_to_all(gated[:, chunk], token_axes, 0, 0, tiled=True) for chunk in range(chunks)
     ]

time: 81.3 us -> 81.2 us (level)
  Pallas kernels: 29.8 us -> 28.7 us
  waiting for transfers between devices: 36.1 us -> 37.1 us
    ppermute x2, waiting for transfers between devices: 18.8 us -> 19.9 us  [passed_along(): return lax.ppermute(block, axis, route)]
    pallas_call x2, Pallas kernels: 5.75 us -> 4.75 us  [the longest x1 2.72 us: inner_features(): pl.pallas_call(inner_kernel, in_specs=[whole] * 3, out_specs=[whole] * 2,...]
  transfers between devices with their start and end apart: 4 -> 4, of which waited for: 3 -> 3; matrix products, arithmetic and copies ran while one was open for 0% -> 0% of each run, Pallas kernels for 22% -> 21%
where the time goes in v7:
time: 81.2 us; the launch traced here: 80.6 us
  waiting for transfers between devices  37.1 us (46%)
  Pallas kernels  28.7 us (35%)
  starting transfers between devices  13.8 us (17%)
  between operations  0.91 us (1%)
    ppermute x2, waiting for transfers between devices, passed_along(): return lax.ppermute(block, axis, route)  19.9 us
    all_to_all x1, waiting for transfers between devices, per_device(): returned.append(lax.all_to_all(carried, token_axes, 0, 0, tiled=True))  17.2 us
    pallas_call x1, Pallas kernels, query_side(): pl.pallas_call(query_kernel, grid=(channels // rows,), in_specs=[block, p...  7.92 us
    pallas_call x1, Pallas kernels, filter_spectrum(): pl.pallas_call(filter_kernel, in_specs=[whole, whole, whole, outside], ou...  6.27 us
    all_to_all x1, starting transfers between devices, per_device(): lax.all_to_all(gated[:, chunk], token_axes, 0, 0, tiled=True)  5.3 us
    pallas_call x1, Pallas kernels, long_convolution(): pl.pallas_call(long_kernel, in_specs=[whole, outside, outside], out_specs...  5.26 us
    all_to_all x1, starting transfers between devices, per_device(): returned.append(lax.all_to_all(carried, token_axes, 0, 0, tiled=True))  4.36 us
    ppermute x2, starting transfers between devices, passed_along(): return lax.ppermute(block, axis, route)  4.16 us
  transfers between devices with their start and end apart: 4, of which 3 were waited for; matrix products, arithmetic and copies ran while one was open for 0% of the time, Pallas kernels for 21%

profile of v7, /device:TPU:16, one launch (start us, length us, event | category | flops | bytes accessed | tf_op | source)
XLA Modules:
  0.0 80.6 jit_solution(3665625302618761944)
XLA Ops:
  0.6 2.0 %rims.1 = (bf16[16,4096]{1,0:T(8,128)(2,1)S(1)}, bf16[4096,128]{1,0:T(8,128)(2,1)S(1)}, bf16[4096,128]{1,0:T(8,128)(2,1)S(1)}, f32[3,7,4096]{2,1,0:T(8,128)S(1)}) custom-call(bf16[4096,128]{1,0:T(8,128)(2,1)} %k_ref.1, bf16[4096,128]{1,0:T(8,128)(2,1)} %v_ref.1, f32[3,7,4096]{2,1,0:T(8,128)} %taps_ref.3), custom_call_target="tpu_custom_call" | custom-call | flops 16777216 | bytes 2097152 | tf_op jit(solution)/shard_map/rims/pallas_call | solution.py:197
  2.7 1.9 %collective-permute-start = (bf16[16,4096]{1,0:T(8,128)(2,1)S(1)}, bf16[16,4096]{1,0:T(8,128)(2,1)S(1)}, u32[]{:S(2)}, u32[]{:S(2)}) collective-permute-start(bf16[16,4096]{1,0:T(8,128)(2,1)S(1)} %get-tuple-element.22), channel_id=1, source_target_pairs={{0,1},{1,2},{2,3},{3,4},{4,5},{5,6},{6,7},{7,8},{8,9},{9,10},{10,1... | collective-permute-start | bytes 393224 | tf_op jit(solution)/shard_map/ppermute | solution.py:45
  4.6 2.7 %inner.1 = (f32[32,128,128]{2,1,0:T(8,128)S(1)}, f32[2,32,8,128]{3,2,1,0:T(8,128)S(1)}) custom-call(bf16[4096,128]{1,0:T(8,128)(2,1)S(1)} %get-tuple-element.17.k_ref, bf16[4096,128]{1,0:T(8,128)(2,1)S(1)} %get-tuple-element.18.v_ref, f32[3,7,4096]{2,1,0:T(8,128)S(1)} %get-tuple-element.19.taps_ref), custom_call_target="tpu_custom_call" | custom-call | flops 14680064 | bytes 4194304 | tf_op jit(solution)/shard_map/inner/pallas_call | solution.py:270
  7.3 2.5 %collective-permute-done.before_ref = bf16[16,4096]{1,0:T(8,128)(2,1)S(1)} collective-permute-done((bf16[16,4096]{1,0:T(8,128)(2,1)S(1)}, bf16[16,4096]{1,0:T(8,128)(2,1)S(1)}, u32[]{:S(2)}, u32[]{:S(2)}) %collective-permute-start) | collective-permute-done | bytes 131104 | tf_op jit(solution)/shard_map/ppermute | solution.py:45
  9.8 0.0 copy-start.3
  9.9 0.0 copy-start.4
  9.9 0.0 copy-start.5
  9.9 1.2 %gated.1 = bf16[32,128,128]{2,1,0:T(8,128)(2,1)} custom-call(f32[32,128,128]{2,1,0:T(8,128)S(1)} %get-tuple-element.20.part_ref, f32[2,32,8,128]{3,2,1,0:T(8,128)S(1)} %get-tuple-element.21.first_ref, f32[3,7,4096]{2,1,0:T(8,128)S(1)} %get-tuple-element.19.taps_ref, bf16[16,4096]{1,0:T(8,128)(2,1)S(1)} %collective-permute-done.before_ref), custom_call_target="tpu_custom_call" | custom-call | flops 2097152 | bytes 3145728 | tf_op jit(solution)/shard_map/gated/pallas_call | solution.py:316
  11.1 5.3 %all-to-all-start = ((bf16[16,256,128]{2,1,0:T(8,128)(2,1)}), bf16[16,256,128]{2,1,0:T(8,128)(2,1)S(1)}, u32[]{:S(2)}, u32[]{:S(2)}) async-start(bf16[16,256,128]{2,1,0:T(8,128)(2,1)} %bitcast), calls=%async_computation | async-start | bytes 2097152 | tf_op jit(solution)/shard_map/all_to_all | solution.py:735
  16.4 0.0 copy-done.3
  16.4 0.0 copy-done.4
  16.4 0.0 copy-done.5
  16.4 6.3 %filter_spectrum.1 = (bf16[17,256,256]{2,1,0:T(8,128)(2,1)}, bf16[8,4096]{1,0:T(8,128)(2,1)}) custom-call(f32[256,2048]{1,0:T(8,128)S(1)} %copy-done.3, f32[1,256]{1,0:T(1,128)S(1)} %bitcast.8, bf16[2,256,256]{2,1,0:T(8,128)(2,1)S(1)} %copy-done.5, bf16[4096,128]{1,0:T(8,128)(2,1)} %q_ref.3), custom_call_target="tpu_custom_call" | custom-call | flops 1711276032 | bytes 6684672 | tf_op jit(solution)/shard_map/filter_spectrum/pallas_call | solution.py:424
  22.7 2.2 %collective-permute-start.1 = (bf16[8,4096]{1,0:T(8,128)(2,1)}, bf16[8,4096]{1,0:T(8,128)(2,1)S(1)}, u32[]{:S(2)}, u32[]{:S(2)}) collective-permute-start(bf16[8,4096]{1,0:T(8,128)(2,1)} %get-tuple-element.23), channel_id=1, source_target_pairs={{0,1},{1,2},{2,3},{3,4},{4,5},{5,6},{6,7},{7,8},{8,9},{9,10},{10,1... | collective-permute-start | bytes 196616 | tf_op jit(solution)/shard_map/ppermute | solution.py:45
  24.9 17.3 %collective-permute-done.1.before_ref = bf16[8,4096]{1,0:T(8,128)(2,1)S(1)} collective-permute-done((bf16[8,4096]{1,0:T(8,128)(2,1)}, bf16[8,4096]{1,0:T(8,128)(2,1)S(1)}, u32[]{:S(2)}, u32[]{:S(2)}) %collective-permute-start.1) | collective-permute-done | bytes 65568 | tf_op jit(solution)/shard_map/ppermute | solution.py:45
  42.3 0.0 all-to-all-done.x_ref
  42.3 5.3 %long_convolution.1 = bf16[16,256,128]{2,1,0:T(8,128)(2,1)} custom-call(bf16[16,256,128]{2,1,0:T(8,128)(2,1)S(1)} %all-to-all-done.x_ref, bf16[17,256,256]{2,1,0:T(8,128)(2,1)} %get-tuple-element.25.spec_out, bf16[2,256,256]{2,1,0:T(8,128)(2,1)} %constant.6.clone.table_ref.table_out), custom_call_target="tpu_custom_call" | custom-call | flops 3422552064 | bytes 6684672 | tf_op jit(solution)/shard_map/long_convolution/pallas_call | solution.py:542
  47.5 0.0 copy-start
  47.5 0.0 copy-start.1
  47.5 0.0 copy-start.2
  47.6 4.4 %all-to-all-start.1 = ((bf16[16,256,128]{2,1,0:T(8,128)(2,1)}), bf16[16,256,128]{2,1,0:T(8,128)(2,1)S(1)}, u32[]{:S(2)}, u32[]{:S(2)}) async-start(bf16[16,256,128]{2,1,0:T(8,128)(2,1)} %long_convolution.1), calls=%async_computation.1 | async-start | bytes 2097152 | tf_op jit(solution)/shard_map/all_to_all | solution.py:745
  51.9 0.0 copy-done
  51.9 0.0 copy-done.1
  51.9 0.0 copy-done.2
  51.9 7.9 %query_side.1 = (f32[4096,128]{1,0:T(8,128)}, bf16[4096,128]{1,0:T(8,128)(2,1)}, f32[128,128]{1,0:T(8,128)}) custom-call(bf16[4096,128]{1,0:T(8,128)(2,1)} %q_ref.3, bf16[8,4096]{1,0:T(8,128)(2,1)S(1)} %collective-permute-done.1.before_ref, f32[3,7,4096]{2,1,0:T(8,128)S(1)} %copy-done, bf16[4096,512]{1,0:T(8,128)(2,1)} %unembed_ref.1, s32[1,128]{1,0:T(1,128)S(1)} %bitcast.7, ...), custom_call_target="tpu_custom_call" | custom-call | flops 544210944 | bytes 8388608 | tf_op jit(solution)/shard_map/query_side/pallas_call | solution.py:600
  59.9 17.2 %all-to-all-done.1.carried_ref = bf16[16,256,128]{2,1,0:T(8,128)(2,1)S(1)} async-done(((bf16[16,256,128]{2,1,0:T(8,128)(2,1)}), bf16[16,256,128]{2,1,0:T(8,128)(2,1)S(1)}, u32[]{:S(2)}, u32[]{:S(2)}) %all-to-all-start.1) | async-done | bytes 1048608 | tf_op jit(solution)/shard_map/all_to_all | solution.py:745
  77.1 3.3 %result.1 = (bf16[16,256,128]{2,1,0:T(8,128)(2,1)}, f32[8,128]{1,0:T(8,128)}, f32[1,2]{1,0:T(1,128)}) custom-call(bf16[16,256,128]{2,1,0:T(8,128)(2,1)S(1)} %all-to-all-done.1.carried_ref, f32[16,256,128]{2,1,0:T(8,128)} %bitcast.9, bf16[16,256,128]{2,1,0:T(8,128)(2,1)} %bitcast.10, f32[128,128]{1,0:T(8,128)} %get-tuple-element.29.after_out, ...), custom_call_target="tpu_custom_call" | custom-call | flops 2097152 | bytes 5242880 | tf_op jit(solution)/shard_map/result/pallas_call | solution.py:683
  (2 shorter events, 0.0 us)
Async XLA Ops:
  2.7 7.2 %collective-permute-start = (bf16[16,4096]{1,0:T(8,128)(2,1)S(1)}, bf16[16,4096]{1,0:T(8,128)(2,1)S(1)}, u32[]{:S(2)}, u32[]{:S(2)}) collective-permute-start(bf16[16,4096]{1,0:T(8,128)(2,1)S(1)} %get-tuple-element.22), channel_id=1, source_target_pairs={{0,1},{1,2},{2,3},{3,4},{4,5},{5,6},{6,7},{7,8},{8,9},{9,10},{10,1... | collective-permute-start | bytes 393224 | tf_op jit(solution)/shard_map/ppermute | solution.py:45
  9.8 6.5 %copy-start.3 = (f32[256,2048]{1,0:T(8,128)S(1)}, f32[256,2048]{1,0:T(8,128)}, u32[]{:S(2)}) copy-start(f32[256,2048]{1,0:T(8,128)} %taps_ref.2) | copy-start | bytes 6291460
  9.9 6.5 %copy-start.4 = (f32[256]{0:T(256)S(1)}, f32[256]{0:T(256)}, u32[]{:S(2)}) copy-start(f32[256]{0:T(256)} %param.15) | copy-start | bytes 3076
  9.9 6.5 %copy-start.5 = (bf16[2,256,256]{2,1,0:T(8,128)(2,1)S(1)}, bf16[2,256,256]{2,1,0:T(8,128)(2,1)}, u32[]{:S(2)}) copy-start(bf16[2,256,256]{2,1,0:T(8,128)(2,1)} %constant.6.clone.table_ref.table_out) | copy-start | bytes 786436
  11.1 31.2 %all-to-all-start = ((bf16[16,256,128]{2,1,0:T(8,128)(2,1)}), bf16[16,256,128]{2,1,0:T(8,128)(2,1)S(1)}, u32[]{:S(2)}, u32[]{:S(2)}) async-start(bf16[16,256,128]{2,1,0:T(8,128)(2,1)} %bitcast), calls=%async_computation | async-start | bytes 2097152 | tf_op jit(solution)/shard_map/all_to_all | solution.py:735
  22.7 19.6 %collective-permute-start.1 = (bf16[8,4096]{1,0:T(8,128)(2,1)}, bf16[8,4096]{1,0:T(8,128)(2,1)S(1)}, u32[]{:S(2)}, u32[]{:S(2)}) collective-permute-start(bf16[8,4096]{1,0:T(8,128)(2,1)} %get-tuple-element.23), channel_id=1, source_target_pairs={{0,1},{1,2},{2,3},{3,4},{4,5},{5,6},{6,7},{7,8},{8,9},{9,10},{10,1... | collective-permute-start | bytes 196616 | tf_op jit(solution)/shard_map/ppermute | solution.py:45
  47.5 4.4 %copy-start = (f32[3,7,4096]{2,1,0:T(8,128)S(1)}, f32[3,7,4096]{2,1,0:T(8,128)}, u32[]{:S(2)}) copy-start(f32[3,7,4096]{2,1,0:T(8,128)} %taps_ref.3) | copy-start | bytes 1032196
  47.5 4.4 %copy-start.1 = (s32[2,64]{1,0:T(2,128)S(1)}, s32[2,64]{1,0:T(2,128)}, u32[]{:S(2)}) copy-start(s32[2,64]{1,0:T(2,128)} %ranks_ref.1) | copy-start | bytes 1540
  47.5 4.4 %copy-start.2 = (s32[128]{0:T(128)S(1)}, s32[128]{0:T(128)}, u32[]{:S(2)}) copy-start(s32[128]{0:T(128)} %param.17) | copy-start | bytes 1540
  47.6 29.5 %all-to-all-start.1 = ((bf16[16,256,128]{2,1,0:T(8,128)(2,1)}), bf16[16,256,128]{2,1,0:T(8,128)(2,1)S(1)}, u32[]{:S(2)}, u32[]{:S(2)}) async-start(bf16[16,256,128]{2,1,0:T(8,128)(2,1)} %long_convolution.1), calls=%async_computation.1 | async-start | bytes 2097152 | tf_op jit(solution)/shard_map/all_to_all | solution.py:745
